TPU v7x, 32 devices: a whole 2x2x4 slice. The times are simulated.
32 devices in a mesh: dp: 16 (over z, x, core), tensor: 2 (over y).
Axes of the slice: x: 2, y: 2, z: 4, core: 2. Of those that a mesh axis runs over, the one named last changes fastest.
Arguments:
- images: bfloat16 [96, 729, 1152], P('dp', None, 'tensor'), may hold values from -6 to 6
- valid_flags: int32 [96], P('dp'), may hold values 0 or 1
- cotangent: bfloat16 [96, 729, 1152], P('dp', None, 'tensor'), may hold values from -6 to 6
- ln1_gain: bfloat16 [1152], P('tensor'), may hold values from 0.099609375 to 1.8984375
- ln1_bias: bfloat16 [1152], P('tensor'), may hold values from -3 to 3
- q_weight: bfloat16 [1152, 1152], P(None, 'tensor'), may hold values from -0.1875 to 0.1875
- q_bias: bfloat16 [1152], P('tensor'), may hold values from -3 to 3
- k_weight: bfloat16 [1152, 1152], P(None, 'tensor'), may hold values from -0.1875 to 0.1875
- v_weight: bfloat16 [1152, 1152], P(None, 'tensor'), may hold values from -0.1875 to 0.1875
- v_bias: bfloat16 [1152], P('tensor'), may hold values from -3 to 3
- o_weight: bfloat16 [1152, 1152], P('tensor'), may hold values from -2.5 to 2.5
- o_bias: bfloat16 [1152], P('tensor'), may hold values from -3 to 3
- ln2_gain: bfloat16 [1152], P('tensor'), may hold values from 0.099609375 to 1.8984375
- ln2_bias: bfloat16 [1152], P('tensor'), may hold values from -3 to 3
- fc1_weight: bfloat16 [1152, 4304], P(None, 'tensor'), may hold values from -0.1875 to 0.1875
- fc1_bias: bfloat16 [4304], P('tensor'), may hold values from -3 to 3
- fc2_weight: bfloat16 [4304, 1152], P('tensor'), may hold values from -0.09375 to 0.09375
- fc2_bias: bfloat16 [1152], P('tensor'), may hold values from -3 to 3
Outputs:
- layer_out: bfloat16 [96, 729, 1152], P('dp', None, 'tensor')
- input_grad: bfloat16 [96, 729, 1152], P('dp', None, 'tensor')
- ln1_gain_grad: float32 [1152], P('tensor')
- ln1_bias_grad: float32 [1152], P('tensor')
- q_weight_grad: float32 [1152, 1152], P(None, 'tensor')
- q_bias_grad: float32 [1152], P('tensor')
- k_weight_grad: float32 [1152, 1152], P(None, 'tensor')
- v_weight_grad: float32 [1152, 1152], P(None, 'tensor')
- v_bias_grad: float32 [1152], P('tensor')
- o_weight_grad: float32 [1152, 1152], P('tensor')
- o_bias_grad: float32 [1152], P('tensor')
- ln2_gain_grad: float32 [1152], P('tensor')
- ln2_bias_grad: float32 [1152], P('tensor')
- fc1_weight_grad: float32 [1152, 4304], P(None, 'tensor')
- fc1_bias_grad: float32 [4304], P('tensor')
- fc2_weight_grad: float32 [4304, 1152], P('tensor')
- fc2_bias_grad: float32 [1152], P('tensor')
Inputs may be any that keep to these rules, and one draw needn't show every extreme that they name: `valid_flags`: 1 marks an image, 0 a padding slot.
All inputs are finite; a program needn't handle non-finite values. No bound on the sum of `valid_flags` on one device may be relied on, other than what follows from the above.
Results may differ from a plain program's by a relative error of at most 0.02.
Values may be sent and summed in bfloat16 or wider, within the bound.
No kernel may reach another device: no remote copies, remote signals or barrier semaphores. Data moves between devices by JAX's collectives and lax.ppermute only.
A program may use at most 576 MiB of HBM per device.

v0:
```python
import math

import jax
import jax.numpy as jnp
from jax import lax
from jax.sharding import PartitionSpec as P

HDIM = 72
MICRO = 2


EPS = 1e-06
GELU_C = math.sqrt(2.0 / math.pi)
GELU_A = 0.044715


def matmul(left, right):
    return jnp.dot(left, right, preferred_element_type=jnp.float32)


def left_transposed(left, right):
    return lax.dot_general(
        left, right, (((0,), (0,)), ((), ())), preferred_element_type=jnp.float32
    )


def right_transposed(left, right):
    return lax.dot_general(
        left, right, (((1,), (1,)), ((), ())), preferred_element_type=jnp.float32
    )


def rounded(values):
    return values.astype(jnp.bfloat16).astype(jnp.float32)


def norm_rows(values):
    feat_total = values.shape[1] * lax.axis_size("tensor")
    row_sum, row_square = lax.psum(
        (jnp.sum(values, axis=1), jnp.sum(values * values, axis=1)), "tensor"
    )
    row_mean = row_sum / feat_total
    row_var = row_square / feat_total - row_mean * row_mean
    inverse = lax.rsqrt(row_var + EPS)
    normed = (values - row_mean[:, None]) * inverse[:, None]
    return (normed, inverse)


def norm_back(grad_normed, normed, inverse, gain_vec):
    feat_total = normed.shape[1] * lax.axis_size("tensor")
    scaled = grad_normed * gain_vec.astype(jnp.float32)
    sum_plain, sum_cross = lax.psum(
        (jnp.sum(scaled, axis=1), jnp.sum(scaled * normed, axis=1)), "tensor"
    )
    return inverse[:, None] * (
        scaled - sum_plain[:, None] / feat_total - normed * (sum_cross[:, None] / feat_total)
    )


def gather_rows(shard):
    return lax.all_gather(shard, "tensor", axis=1, tiled=True)


def gather_grads(shard):
    return lax.all_gather(shard, "tensor", axis=1, tiled=True)


def gelu_parts(pre):
    tanh_val = jnp.tanh(GELU_C * (pre + GELU_A * pre * pre * pre))
    value = 0.5 * pre * (1.0 + tanh_val)
    slope = 0.5 * (1.0 + tanh_val) + 0.5 * pre * (1.0 - tanh_val * tanh_val) * GELU_C * (
        1.0 + 3.0 * GELU_A * pre * pre
    )
    return (value, slope)


def per_device(
    images,
    valid_flags,
    cotangent,
    ln1_gain,
    ln1_bias,
    q_weight,
    q_bias,
    k_weight,
    v_weight,
    v_bias,
    o_weight,
    o_bias,
    ln2_gain,
    ln2_bias,
    fc1_weight,
    fc1_bias,
    fc2_weight,
    fc2_bias,
):
    img_local, seq_len, feat_local = images.shape
    per_micro = img_local // MICRO
    rows = per_micro * seq_len
    head_local = q_weight.shape[1] // HDIM
    scale = 1.0 / math.sqrt(HDIM)
    shaped = (per_micro, seq_len, head_local, HDIM)
    split_images = images.reshape(per_micro, MICRO, seq_len, feat_local)
    split_cot = cotangent.reshape(per_micro, MICRO, seq_len, feat_local)
    split_flags = valid_flags.reshape(per_micro, MICRO).astype(jnp.float32)
    param_list = (
        ln1_gain,
        ln1_bias,
        q_weight,
        q_bias,
        k_weight,
        v_weight,
        v_bias,
        o_weight,
        o_bias,
        ln2_gain,
        ln2_bias,
        fc1_weight,
        fc1_bias,
        fc2_weight,
        fc2_bias,
    )
    totals = tuple((jnp.zeros(weight_arr.shape, jnp.float32) for weight_arr in param_list))
    out_list = []
    grad_list = []
    for micro_index in range(MICRO):
        flag_rows = jnp.repeat(split_flags[:, micro_index], seq_len)[:, None]
        inputs = split_images[:, micro_index].reshape(rows, feat_local).astype(jnp.float32)
        normed1, inverse1 = norm_rows(inputs)
        low_first = (normed1 * ln1_gain + ln1_bias).astype(jnp.bfloat16)
        full_first = gather_rows(low_first)
        query = (matmul(full_first, q_weight) + q_bias).astype(jnp.bfloat16)
        keys = matmul(full_first, k_weight).astype(jnp.bfloat16)
        values = (matmul(full_first, v_weight) + v_bias).astype(jnp.bfloat16)
        query4 = query.reshape(shaped)
        keys4 = keys.reshape(shaped)
        values4 = values.reshape(shaped)
        scores = (
            jnp.einsum("nqhd,nkhd->nhqk", query4, keys4, preferred_element_type=jnp.float32) * scale
        )
        log_total = jax.nn.logsumexp(scores, axis=-1)
        probs_low = jnp.exp(scores - log_total[..., None]).astype(jnp.bfloat16)
        mixed = jnp.einsum(
            "nhqk,nkhd->nqhd", probs_low, values4, preferred_element_type=jnp.float32
        )
        context = mixed.reshape(rows, head_local * HDIM).astype(jnp.bfloat16)
        attended = lax.psum_scatter(
            rounded(matmul(context, o_weight)).astype(jnp.bfloat16),
            "tensor",
            scatter_dimension=1,
            tiled=True,
        ).astype(jnp.float32)
        resid = inputs + attended + o_bias
        normed2, inverse2 = norm_rows(resid)
        low_second = (normed2 * ln2_gain + ln2_bias).astype(jnp.bfloat16)
        full_second = gather_rows(low_second)
        hidden_pre = matmul(full_second, fc1_weight) + fc1_bias
        act_value, act_slope = gelu_parts(hidden_pre)
        act_low = act_value.astype(jnp.bfloat16)
        branch = lax.psum_scatter(
            rounded(matmul(act_low, fc2_weight)).astype(jnp.bfloat16),
            "tensor",
            scatter_dimension=1,
            tiled=True,
        ).astype(jnp.float32)
        layer_rows = (resid + branch + fc2_bias) * flag_rows
        out_list.append(layer_rows.astype(jnp.bfloat16).reshape(per_micro, seq_len, feat_local))
        grad_out = (
            split_cot[:, micro_index].reshape(rows, feat_local).astype(jnp.float32) * flag_rows
        )
        grad_full = gather_grads(grad_out.astype(jnp.bfloat16))
        g_fc2w = left_transposed(act_low, grad_full)
        g_fc2b = jnp.sum(grad_out, axis=0)
        hidden_grad = (right_transposed(grad_full, fc2_weight) * act_slope).astype(jnp.bfloat16)
        g_fc1w = left_transposed(full_second, hidden_grad)
        g_fc1b = jnp.sum(hidden_grad.astype(jnp.float32), axis=0)
        grad_second = lax.psum_scatter(
            rounded(right_transposed(hidden_grad, fc1_weight)).astype(jnp.bfloat16),
            "tensor",
            scatter_dimension=1,
            tiled=True,
        ).astype(jnp.float32)
        g_ln2g = jnp.sum(grad_second * normed2, axis=0)
        g_ln2b = jnp.sum(grad_second, axis=0)
        grad_resid = grad_out + norm_back(grad_second, normed2, inverse2, ln2_gain)
        g_ob = jnp.sum(grad_resid, axis=0)
        resid_full = gather_grads(grad_resid.astype(jnp.bfloat16))
        g_ow = left_transposed(context, resid_full)
        grad_context = right_transposed(resid_full, o_weight).astype(jnp.bfloat16)
        context4 = grad_context.reshape(shaped)
        probs = jnp.exp(
            jnp.einsum("nqhd,nkhd->nhqk", query4, keys4, preferred_element_type=jnp.float32) * scale
            - log_total[..., None]
        )
        probs_again = probs.astype(jnp.bfloat16)
        grad_probs = jnp.einsum(
            "nqhd,nkhd->nhqk", context4, values4, preferred_element_type=jnp.float32
        )
        row_delta = jnp.sum(probs * grad_probs, axis=-1)
        grad_scores = (probs * (grad_probs - row_delta[..., None])).astype(jnp.bfloat16)
        grad_query = (
            (
                jnp.einsum(
                    "nhqk,nkhd->nqhd", grad_scores, keys4, preferred_element_type=jnp.float32
                )
                * scale
            )
            .reshape(rows, head_local * HDIM)
            .astype(jnp.bfloat16)
        )
        grad_keys = (
            (
                jnp.einsum(
                    "nhqk,nqhd->nkhd", grad_scores, query4, preferred_element_type=jnp.float32
                )
                * scale
            )
            .reshape(rows, head_local * HDIM)
            .astype(jnp.bfloat16)
        )
        grad_values = (
            jnp.einsum("nhqk,nqhd->nkhd", probs_again, context4, preferred_element_type=jnp.float32)
            .reshape(rows, head_local * HDIM)
            .astype(jnp.bfloat16)
        )
        g_qw = left_transposed(full_first, grad_query)
        g_qb = jnp.sum(grad_query.astype(jnp.float32), axis=0)
        g_kw = left_transposed(full_first, grad_keys)
        g_vw = left_transposed(full_first, grad_values)
        g_vb = jnp.sum(grad_values.astype(jnp.float32), axis=0)
        partial_first = (
            right_transposed(grad_query, q_weight)
            + right_transposed(grad_keys, k_weight)
            + right_transposed(grad_values, v_weight)
        )
        grad_first = lax.psum_scatter(
            rounded(partial_first).astype(jnp.bfloat16), "tensor", scatter_dimension=1, tiled=True
        ).astype(jnp.float32)
        g_ln1g = jnp.sum(grad_first * normed1, axis=0)
        g_ln1b = jnp.sum(grad_first, axis=0)
        grad_input = grad_resid + norm_back(grad_first, normed1, inverse1, ln1_gain)
        grad_list.append(grad_input.astype(jnp.bfloat16).reshape(per_micro, seq_len, feat_local))
        micro_grads = (
            g_ln1g,
            g_ln1b,
            g_qw,
            g_qb,
            g_kw,
            g_vw,
            g_vb,
            g_ow,
            g_ob,
            g_ln2g,
            g_ln2b,
            g_fc1w,
            g_fc1b,
            g_fc2w,
            g_fc2b,
        )
        totals = jax.tree.map(jnp.add, totals, micro_grads)
    totals = (
        lax.psum(totals[0].astype(jnp.bfloat16), "dp").astype(jnp.float32),
        lax.psum(totals[1].astype(jnp.bfloat16), "dp").astype(jnp.float32),
        lax.psum(totals[2].astype(jnp.bfloat16), "dp").astype(jnp.float32),
        lax.psum(totals[3].astype(jnp.bfloat16), "dp").astype(jnp.float32),
        lax.psum(totals[4].astype(jnp.bfloat16), "dp").astype(jnp.float32),
        lax.psum(totals[5].astype(jnp.bfloat16), "dp").astype(jnp.float32),
        lax.psum(totals[6].astype(jnp.bfloat16), "dp").astype(jnp.float32),
        lax.psum(totals[7].astype(jnp.bfloat16), "dp").astype(jnp.float32),
        lax.psum(totals[8].astype(jnp.bfloat16), "dp").astype(jnp.float32),
        lax.psum(totals[9].astype(jnp.bfloat16), "dp").astype(jnp.float32),
        lax.psum(totals[10].astype(jnp.bfloat16), "dp").astype(jnp.float32),
        lax.psum(totals[11].astype(jnp.bfloat16), "dp").astype(jnp.float32),
        lax.psum(totals[12].astype(jnp.bfloat16), "dp").astype(jnp.float32),
        lax.psum(totals[13].astype(jnp.bfloat16), "dp").astype(jnp.float32),
        lax.psum(totals[14].astype(jnp.bfloat16), "dp").astype(jnp.float32),
    )
    layer_out = jnp.stack(out_list, axis=1).reshape(img_local, seq_len, feat_local)
    input_grad = jnp.stack(grad_list, axis=1).reshape(img_local, seq_len, feat_local)
    return (
        layer_out,
        input_grad,
        totals[0],
        totals[1],
        totals[2],
        totals[3],
        totals[4],
        totals[5],
        totals[6],
        totals[7],
        totals[8],
        totals[9],
        totals[10],
        totals[11],
        totals[12],
        totals[13],
        totals[14],
    )


def solution(mesh):
    in_specs = (
        P("dp", None, "tensor"),
        P("dp"),
        P("dp", None, "tensor"),
        P("tensor"),
        P("tensor"),
        P(None, "tensor"),
        P("tensor"),
        P(None, "tensor"),
        P(None, "tensor"),
        P("tensor"),
        P("tensor", None),
        P("tensor"),
        P("tensor"),
        P("tensor"),
        P(None, "tensor"),
        P("tensor"),
        P("tensor", None),
        P("tensor"),
    )
    out_specs = (
        P("dp", None, "tensor"),
        P("dp", None, "tensor"),
        P("tensor"),
        P("tensor"),
        P(None, "tensor"),
        P("tensor"),
        P(None, "tensor"),
        P(None, "tensor"),
        P("tensor"),
        P("tensor", None),
        P("tensor"),
        P("tensor"),
        P("tensor"),
        P(None, "tensor"),
        P("tensor"),
        P("tensor", None),
        P("tensor"),
    )
    return jax.shard_map(
        per_device, mesh=mesh, in_specs=in_specs, out_specs=out_specs, check_vma=False
    )
```

profile of v0, /device:TPU:0, one launch (start us, length us, event | category | flops | bytes accessed | tf_op | source)
XLA Modules:
  0.0 2153.9 jit_solution(511137464178588783)
XLA Ops:
  52.4 10.2 all-reduce.3
  70.5 68.6 %all-gather.13.cloned.1.call-done = bf16[2187,1152]{0,1:T(8,128)(2,1)} async-done(((bf16[2187,576]{0,1:T(8,128)(2,1)}), bf16[2187,1152]{0,1:T(8,128)(2,1)}) %all-gather.13.cloned.1.call-update) | async-done | bytes 5038864 | tf_op jit(solution)/shard_map/all_gather | solution.py:61
  146.4 8.4 reshape.191
  154.8 55.7 %all-gather.9.cloned.1.call-done = bf16[2187,1152]{0,1:T(8,128)(2,1)} async-done(((bf16[2187,576]{0,1:T(8,128)(2,1)}), bf16[2187,1152]{0,1:T(8,128)(2,1)}) %all-gather.9.cloned.1.call-update) | async-done | bytes 5038864 | tf_op jit(solution)/shard_map/all_gather | solution.py:61
  217.9 8.2 reshape.187
  226.1 8.0 add_convert_fusion.6
  234.1 8.4 reshape.186
  242.4 8.0 convolution_convert_fusion.9
  250.4 8.1 reshape.188
  258.6 22.3 %multiply_reduce_fusion.3 = (f32[3,8,729]{2,1,0:T(8,128)S(1)}, f32[3,8,729,729]{2,3,1,0:T(8,128)}) fusion(bf16[3,729,8,72]{1,0,3,2:T(4,128)(2,1)} %reshape.188, bf16[3,729,8,72]{1,0,3,2:T(4,128)(2,1)} %reshape.187), kind=kOutput, calls=%fused_computation.9 | convolution fusion | flops 1862151680 | bytes 56127168 | tf_op jit(solution)/shard_map/nqhd,nkhd->nhqk/dot_general | solution.py:139
  280.9 21.1 exponential_reduce_fusion.1
  302.0 22.6 %convert_bitcast_fusion.1 = bf16[3,729,8,72]{1,3,2,0:T(8,128)(2,1)} fusion(f32[3,8,729,729]{2,3,1,0:T(8,128)} %get-tuple-element.112, f32[3,8,729]{2,1,0:T(8,128)S(1)} %log_add_fusion.1, bf16[3,729,8,72]{1,0,3,2:T(4,128)(2,1)} %reshape.186), kind=kOutput, calls=%fused_computation.153 | convolution fusion | flops 1876183552 | bytes 56127168 | tf_op jit(solution)/shard_map/nhqk,nkhd->nqhd/dot_general | solution.py:143
  353.8 8.3 reshape.190
  369.7 8.2 reshape.189
  377.9 22.7 %multiply_reduce_fusion.2 = (f32[3,8,729]{2,1,0:T(8,128)S(1)}, f32[3,8,729,729]{2,3,1,0:T(8,128)}) fusion(bf16[3,729,8,72]{1,0,3,2:T(4,128)(2,1)} %reshape.191, bf16[3,729,8,72]{1,0,3,2:T(4,128)(2,1)} %reshape.190), kind=kOutput, calls=%fused_computation.8 | convolution fusion | flops 1862151680 | bytes 56127168 | tf_op jit(solution)/shard_map/nqhd,nkhd->nhqk/dot_general | solution.py:139
  400.6 21.2 exponential_reduce_fusion
  421.8 22.8 %convert_bitcast_fusion = bf16[3,729,8,72]{1,3,2,0:T(8,128)(2,1)} fusion(f32[3,8,729,729]{2,3,1,0:T(8,128)} %get-tuple-element.114, f32[3,8,729]{2,1,0:T(8,128)S(1)} %log_add_fusion, bf16[3,729,8,72]{1,0,3,2:T(4,128)(2,1)} %reshape.189), kind=kOutput, calls=%fused_computation.152 | convolution fusion | flops 1876183552 | bytes 56127168 | tf_op jit(solution)/shard_map/nhqk,nkhd->nqhd/dot_general | solution.py:143
  466.6 65.9 %reduce-scatter.13.cloned.1.call-done = bf16[2187,576]{0,1:T(8,128)(2,1)} async-done(((bf16[2187,1152]{0,1:T(8,128)(2,1)}), bf16[2187,576]{0,1:T(8,128)(2,1)}) %reduce-scatter.13.cloned.1.call-update) | async-done | bytes 2519440 | tf_op jit(solution)/shard_map/reduce_scatter | solution.py:147
  532.4 9.6 fusion.101
  606.8 20.0 all-gather.15.cloned.1.call-done
  626.8 19.7 convolution_add_fusion
  646.5 51.0 %all-gather.21.cloned.1.call-done = bf16[2187,1152]{0,1:T(8,128)(2,1)} async-done(((bf16[2187,576]{0,1:T(8,128)(2,1)}), bf16[2187,1152]{0,1:T(8,128)(2,1)}) %all-gather.21.cloned.1.call-update) | async-done | bytes 5038864 | tf_op jit(solution)/shard_map/all_gather | solution.py:65
  697.6 30.4 %convert_reduce_fusion = (f32[2152]{0:T(1024)}, bf16[2187,2152]{1,0:T(8,128)(2,1)S(1)}) fusion(f32[2187,2152]{1,0:T(8,128)} %convolution_add_fusion, bf16[2187,1152]{0,1:T(8,128)(2,1)} %all-gather.21.cloned.1.call-done, bf16[2152,1152]{1,0:T(8,128)(2,1)} %param.34), kind=kOutput, calls=%fused_computation.30 | convolution fusion | flops 10942431232 | bytes 38244208 | tf_op jit(solution)/shard_map/dot_general | solution.py:28
  731.6 17.0 convolution_convert_fusion
  748.7 20.4 all-gather.11.cloned.1.call-done
  769.0 19.5 convolution_add_fusion.1
  788.6 51.9 %all-gather.17.cloned.1.call-done = bf16[2187,1152]{0,1:T(8,128)(2,1)} async-done(((bf16[2187,576]{0,1:T(8,128)(2,1)}), bf16[2187,1152]{0,1:T(8,128)(2,1)}) %all-gather.17.cloned.1.call-update) | async-done | bytes 5038864 | tf_op jit(solution)/shard_map/all_gather | solution.py:65
  840.5 30.6 %convert_reduce_fusion.1 = (f32[2152]{0:T(1024)}, bf16[2187,2152]{1,0:T(8,128)(2,1)S(1)}) fusion(f32[2187,2152]{1,0:T(8,128)} %convolution_add_fusion.1, bf16[2187,1152]{0,1:T(8,128)(2,1)} %all-gather.17.cloned.1.call-done, bf16[2152,1152]{1,0:T(8,128)(2,1)} %param.34), kind=kOutput, calls=%fused_computation.31 | convolution fusion | flops 10942431232 | bytes 38244208 | tf_op jit(solution)/shard_map/dot_general | solution.py:28
  874.9 16.8 convolution_convert_fusion.1
  891.8 20.0 convolution_convert_fusion.4
  911.8 19.9 convolution_convert_fusion.2
  932.4 20.4 fusion.115
  952.8 24.5 %fusion.100 = f32[2152,1152]{1,0:T(8,128)} fusion(bf16[2187,1152]{0,1:T(8,128)(2,1)} %all-gather.17.cloned.1.call-done, f32[2187,2152]{1,0:T(8,128)} %convolution_add_fusion.1), kind=kOutput, calls=%fused_computation.211 | convolution fusion | flops 10885958656 | bytes 33780960 | tf_op jit(solution)/shard_map/dot_general | solution.py:22
  977.8 8.4 fusion.48
  986.3 8.4 all-reduce.1
  994.7 52.9 %reduce-scatter.11.cloned.1.call-done = bf16[2187,576]{0,1:T(8,128)(2,1)} async-done(((bf16[2187,1152]{0,1:T(8,128)(2,1)}), bf16[2187,576]{0,1:T(8,128)(2,1)}) %reduce-scatter.11.cloned.1.call-update) | async-done | bytes 2519440 | tf_op jit(solution)/shard_map/reduce_scatter | solution.py:160
  1047.6 9.0 fusion.105
  1060.7 21.3 fusion.16
  1082.0 24.5 %fusion.17 = bf16[2152,1152]{1,0:T(8,128)(2,1)} fusion(f32[2152,1152]{1,0:T(8,128)} %fusion.100, bf16[2187,1152]{0,1:T(8,128)(2,1)} %all-gather.21.cloned.1.call-done, f32[2187,2152]{1,0:T(8,128)} %convolution_add_fusion), kind=kOutput, calls=%fused_computation.45 | convolution fusion | flops 10890916864 | bytes 38739168 | tf_op jit(solution)/shard_map/dot_general | solution.py:22
  1106.5 9.7 reduce-scatter.15.cloned.1.call-done
  1116.2 9.0 fusion.103
  1129.7 57.9 %all-gather.19.cloned.1.call-done = bf16[2187,1152]{0,1:T(8,128)(2,1)} async-done(((bf16[2187,576]{0,1:T(8,128)(2,1)}), bf16[2187,1152]{0,1:T(8,128)(2,1)}) %all-gather.19.cloned.1.call-update) | async-done | bytes 5038864 | tf_op jit(solution)/shard_map/all_gather | solution.py:65
  1195.4 8.3 reshape.194
  1203.7 36.5 %multiply_reduce_fusion.1 = (f32[3,8,729]{2,1,0:T(8,128)S(1)}, f32[3,8,729,729]{2,3,1,0:T(8,128)}) fusion(f32[3,8,729,729]{2,3,1,0:T(8,128)} %get-tuple-element.112, f32[3,8,729]{2,1,0:T(8,128)S(1)} %copy-done.6, bf16[3,729,8,72]{1,0,3,2:T(4,128)(2,1)} %reshape.186, bf16[3,729,8,72]{1,0,3,2:T(4,128)(2,1)} %reshape.194), kind=kOutput, calls=%fused_computation.3 | convolution fusion | flops 1887660800 | bytes 107215488 | tf_op jit(solution)/shard_map/nqhd,nkhd->nhqk/dot_general | solution.py:196
  1240.2 43.3 %multiply_convert_fusion.1 = bf16[3,8,729,729]{2,3,1,0:T(8,128)(2,1)} fusion(f32[3,8,729,729]{2,3,1,0:T(8,128)} %get-tuple-element.116, f32[3,8,729,729]{2,3,1,0:T(8,128)} %get-tuple-element.112, f32[3,8,729]{2,1,0:T(8,128)S(1)} %get-tuple-element.115, f32[3,8,729]{2,1,0:T(8,128)S(1)} %copy-done.6), kind=kLoop, calls=%fused_computation.2 | loop fusion | flops 63772920 | bytes 127685808 | tf_op jit(solution)/shard_map/convert_element_type | solution.py:200
  1283.5 15.5 fusion.64
  1299.0 16.6 convert_reduce_fusion.9
  1315.6 21.5 %convert_reduce_fusion.7 = (f32[8,72]{1,0:T(8,128)}, bf16[3,8,72,729]{3,2,1,0:T(8,128)(2,1)}) fusion(f32[3,8,729,729]{2,3,1,0:T(8,128)} %get-tuple-element.112, f32[3,8,729]{2,1,0:T(8,128)S(1)} %copy-done.6, bf16[3,729,8,72]{1,0,3,2:T(4,128)(2,1)S(1)} %copy-done.3), kind=kOutput, calls=%fused_computation.105 | convolution fusion | flops 1878702464 | bytes 56129472 | tf_op jit(solution)/shard_map/nhqk,nqhd->nkhd/dot_general | solution.py:222
  1344.5 8.2 reshape.195
  1352.7 22.6 %convert_reduce_fusion.6 = (f32[8,72]{1,0:T(8,128)}, bf16[3,8,72,729]{3,2,1,0:T(8,128)(2,1)}) fusion(f32[3,8,729,729]{2,3,1,0:T(8,128)} %get-tuple-element.114, f32[3,8,729]{2,1,0:T(8,128)S(1)} %copy-done.8, bf16[3,729,8,72]{1,0,3,2:T(4,128)(2,1)} %reshape.195), kind=kOutput, calls=%fused_computation.104 | convolution fusion | flops 1878702464 | bytes 56129472 | tf_op jit(solution)/shard_map/nhqk,nqhd->nkhd/dot_general | solution.py:222
  1375.3 36.6 %multiply_reduce_fusion = (f32[3,8,729]{2,1,0:T(8,128)S(1)}, f32[3,8,729,729]{2,3,1,0:T(8,128)}) fusion(f32[3,8,729,729]{2,3,1,0:T(8,128)} %get-tuple-element.114, f32[3,8,729]{2,1,0:T(8,128)S(1)} %copy-done.8, bf16[3,729,8,72]{1,0,3,2:T(4,128)(2,1)} %reshape.189, bf16[3,729,8,72]{1,0,3,2:T(4,128)(2,1)} %reshape.195), kind=kOutput, calls=%fused_computation.1 | convolution fusion | flops 1887660800 | bytes 107215488 | tf_op jit(solution)/shard_map/nqhd,nkhd->nhqk/dot_general | solution.py:196
  1411.9 43.3 %multiply_convert_fusion = bf16[3,8,729,729]{2,3,1,0:T(8,128)(2,1)} fusion(f32[3,8,729,729]{2,3,1,0:T(8,128)} %get-tuple-element.118, f32[3,8,729,729]{2,3,1,0:T(8,128)} %get-tuple-element.114, f32[3,8,729]{2,1,0:T(8,128)S(1)} %get-tuple-element.117, f32[3,8,729]{2,1,0:T(8,128)S(1)} %copy-done.8), kind=kLoop, calls=%fused_computation | loop fusion | flops 63772920 | bytes 127685808 | tf_op jit(solution)/shard_map/convert_element_type | solution.py:200
  1455.2 15.4 fusion.65
  1470.6 16.6 convert_reduce_fusion.8
  1605.2 9.0 fusion.109
  1614.3 8.0 convolution_add_fusion.7
  1629.2 8.9 fusion.110
  1682.8 8.7 copy.129
  1691.8 190.5 %all-reduce.8.cloned.1.call-done = (bf16[1152,576]{0,1:T(8,128)(2,1)}, bf16[1152,576]{0,1:T(8,128)(2,1)}, bf16[1152,576]{0,1:T(8,128)(2,1)}, bf16[576,1152]{1,0:...) async-done(((bf16[1152,576]{0,1:T(8,128)(2,1)}, bf16[1152,576]{0,1:T(8,128)(2,1)}, bf16[1152,576]{0,1:T(8,128)(2,1)}, bf16[576,1152]{1,0:T(8,128)(2,1)}, ...) | async-done | bytes 15224848 | tf_op jit(solution)/shard_map/psum | solution.py:264
  1901.1 49.4 %reduce-scatter.19.cloned.1.call-done = bf16[2187,576]{0,1:T(8,128)(2,1)} async-done(((bf16[2187,1152]{0,1:T(8,128)(2,1)}), bf16[2187,576]{0,1:T(8,128)(2,1)}) %reduce-scatter.19.cloned.1.call-update) | async-done | bytes 2519440 | tf_op jit(solution)/shard_map/reduce_scatter | solution.py:236
  1950.6 68.6 %reduce-scatter.23.cloned.1.call-done = bf16[2187,576]{0,1:T(8,128)(2,1)} async-done(((bf16[2187,1152]{0,1:T(8,128)(2,1)}), bf16[2187,576]{0,1:T(8,128)(2,1)}) %reduce-scatter.23.cloned.1.call-update) | async-done | bytes 2519440 | tf_op jit(solution)/shard_map/reduce_scatter | solution.py:236
  2026.8 61.2 %all-reduce.4 = (bf16[576]{0:T(1024)(128)(2,1)S(1)}, bf16[576]{0:T(1024)(128)(2,1)S(1)}, bf16[576]{0:T(1024)(128)(2,1)S(1)}, bf16[576]{0:T(1024)(128)(2,1)S(1)},...) all-reduce(bf16[576]{0:T(1024)(128)(2,1)S(1)} %add_convert_fusion.1, ...), channel_id=1, replica_groups=mesh['dp'=16,'tensor'=2] {'dp'}, use_global_device_ids=true, to_apply=%region_48.0 | all-reduce | flops 6760 | bytes 27040 | tf_op jit(solution)/shard_map/psum | solution.py:262
  2101.1 13.1 fusion.42
  2138.4 8.7 copy.158
  (359 shorter events, 456.7 us)
Async XLA Ops:
  7.2 330.9 %copy-start = (bf16[576,1152]{1,0:T(8,128)(2,1)S(1)}, bf16[576,1152]{1,0:T(8,128)(2,1)}, u32[]{:S(2)}) copy-start(bf16[576,1152]{1,0:T(8,128)(2,1)} %param.28) | copy-start | bytes 3981316
  7.2 131.9 %all-gather.13.cloned.1.call-start = ((), (), s32[]{:S(2)}) async-start(), calls=%async_computation.12 | async-start | bytes 7962624 | tf_op jit(solution)/shard_map/all_gather | solution.py:61
  31.3 8.1 copy-start.63
  31.3 8.1 copy-start.64
  39.4 23.3 %copy-start.44 = (f32[576]{0:T(1024)}, f32[576]{0:T(1024)S(1)}, u32[]{:S(2)}) copy-start(f32[576]{0:T(1024)S(1)} %convert_element_type.439) | copy-start | bytes 6916
  69.4 69.6 %copy-start.73 = (bf16[1152,576]{0,1:T(8,128)(2,1)S(1)}, bf16[1152,576]{0,1:T(8,128)(2,1)}, u32[]{:S(2)}) copy-start(bf16[1152,576]{0,1:T(8,128)(2,1)} %param.25) | copy-start | bytes 3981316
  69.5 141.1 %all-gather.9.cloned.1.call-start = ((), (), s32[]{:S(2)}) async-start(), calls=%async_computation.8 | async-start | bytes 7962624 | tf_op jit(solution)/shard_map/all_gather | solution.py:61
  70.2 396.3 %reduce-scatter.9.cloned.1.call-start = ((), (), s32[]{:S(2)}) async-start(), calls=%async_computation.9 | async-start | bytes 7962624 | tf_op jit(solution)/shard_map/reduce_scatter | solution.py:147
  146.4 64.1 %copy-start.71 = (bf16[1152,576]{0,1:T(8,128)(2,1)S(1)}, bf16[1152,576]{0,1:T(8,128)(2,1)}, u32[]{:S(2)}) copy-start(bf16[1152,576]{0,1:T(8,128)(2,1)} %param.23) | copy-start | bytes 3981316
  302.0 22.7 %copy-start.5 = (f32[3,8,729]{2,1,0:T(8,128)}, f32[3,8,729]{2,1,0:T(8,128)S(1)}, u32[]{:S(2)}) copy-start(f32[3,8,729]{2,1,0:T(8,128)S(1)} %log_add_fusion.1) | copy-start | bytes 209956
  345.9 186.6 %reduce-scatter.13.cloned.1.call-start = ((), (), s32[]{:S(2)}) async-start(), calls=%async_computation.13 | async-start | bytes 7962624 | tf_op jit(solution)/shard_map/reduce_scatter | solution.py:147
  353.8 8.3 copy-start.76
  421.8 22.8 %copy-start.7 = (f32[3,8,729]{2,1,0:T(8,128)}, f32[3,8,729]{2,1,0:T(8,128)S(1)}, u32[]{:S(2)}) copy-start(f32[3,8,729]{2,1,0:T(8,128)S(1)} %log_add_fusion) | copy-start | bytes 209956
  465.8 161.0 %all-gather.15.cloned.1.call-start = ((), (), s32[]{:S(2)}) async-start(), calls=%async_computation.14 | async-start | bytes 7962624 | tf_op jit(solution)/shard_map/all_gather | solution.py:61
  466.5 83.0 %copy-start.42 = (f32[576]{0:T(1024)}, f32[576]{0:T(1024)S(1)}, u32[]{:S(2)}) copy-start(f32[576]{0:T(1024)S(1)} %convert_element_type.454) | copy-start | bytes 6916
  556.2 141.3 %all-gather.21.cloned.1.call-start = ((), (), s32[]{:S(2)}) async-start(), calls=%async_computation.20 | async-start | bytes 7962624 | tf_op jit(solution)/shard_map/all_gather | solution.py:65
  556.6 28.5 %copy-start.59 = (f32[3]{0:T(128)}, f32[3]{0:T(128)S(1)}, u32[]{:S(2)}) copy-start(f32[3]{0:T(128)S(1)} %get-tuple-element.41) | copy-start | bytes 40
  557.3 22.7 %copy-start.38 = (f32[2187]{0:T(1024)}, f32[2187]{0:T(1024)S(1)}, u32[]{:S(2)}) copy-start(f32[2187]{0:T(1024)S(1)} %mul.393) | copy-start | bytes 26248
  584.3 184.7 %all-gather.11.cloned.1.call-start = ((), (), s32[]{:S(2)}) async-start(), calls=%async_computation.10 | async-start | bytes 7962624 | tf_op jit(solution)/shard_map/all_gather | solution.py:61
  585.1 255.4 %all-gather.17.cloned.1.call-start = ((), (), s32[]{:S(2)}) async-start(), calls=%async_computation.16 | async-start | bytes 7962624 | tf_op jit(solution)/shard_map/all_gather | solution.py:65
  585.3 17.1 copy-start.40
  606.7 370.5 %reduce-scatter.21.cloned.1.call-start = ((), (), s32[]{:S(2)}) async-start(), calls=%async_computation.21 | async-start | bytes 7962624 | tf_op jit(solution)/shard_map/reduce_scatter | solution.py:177
  748.6 229.2 %reduce-scatter.17.cloned.1.call-start = ((), (), s32[]{:S(2)}) async-start(), calls=%async_computation.17 | async-start | bytes 7962624 | tf_op jit(solution)/shard_map/reduce_scatter | solution.py:177
  891.7 155.9 %reduce-scatter.11.cloned.1.call-start = ((), (), s32[]{:S(2)}) async-start(), calls=%async_computation.11 | async-start | bytes 7962624 | tf_op jit(solution)/shard_map/reduce_scatter | solution.py:160
  911.8 204.4 %reduce-scatter.15.cloned.1.call-start = ((), (), s32[]{:S(2)}) async-start(), calls=%async_computation.15 | async-start | bytes 7962624 | tf_op jit(solution)/shard_map/reduce_scatter | solution.py:160
  931.7 255.9 %all-gather.19.cloned.1.call-start = ((), (), s32[]{:S(2)}) async-start(), calls=%async_computation.18 | async-start | bytes 7962624 | tf_op jit(solution)/shard_map/all_gather | solution.py:65
  952.7 25.1 %copy-start.31 = (f32[2187]{0:T(1024)S(1)}, f32[2187]{0:T(1024)}, u32[]{:S(2)}) copy-start(f32[2187]{0:T(1024)} %copy-done.30) | copy-start | bytes 26248
  952.7 25.1 %copy-start.33 = (f32[2187]{0:T(1024)S(1)}, f32[2187]{0:T(1024)}, u32[]{:S(2)}) copy-start(f32[2187]{0:T(1024)} %copy-done.32) | copy-start | bytes 26248
  952.7 25.1 %copy-start.35 = (f32[2187]{0:T(1024)S(1)}, f32[2187]{0:T(1024)}, u32[]{:S(2)}) copy-start(f32[2187]{0:T(1024)} %copy-done.34) | copy-start | bytes 26248
  952.7 25.1 %copy-start.37 = (f32[2187]{0:T(1024)S(1)}, f32[2187]{0:T(1024)}, u32[]{:S(2)}) copy-start(f32[2187]{0:T(1024)} %copy-done.36) | copy-start | bytes 26248
  952.7 25.1 %copy-start.43 = (f32[576]{0:T(1024)S(1)}, f32[576]{0:T(1024)}, u32[]{:S(2)}) copy-start(f32[576]{0:T(1024)} %copy-done.42) | copy-start | bytes 6916
  977.2 70.4 %copy-start.41 = (f32[2187]{0:T(1024)S(1)}, f32[2187]{0:T(1024)}, u32[]{:S(2)}) copy-start(f32[2187]{0:T(1024)} %copy-done.40) | copy-start | bytes 26248
  1060.7 276.5 %all-gather.23.cloned.1.call-start = ((), (), s32[]{:S(2)}) async-start(), calls=%async_computation.22 | async-start | bytes 7962624 | tf_op jit(solution)/shard_map/all_gather | solution.py:65
  1082.0 34.2 %copy-start.39 = (f32[2187]{0:T(1024)S(1)}, f32[2187]{0:T(1024)}, u32[]{:S(2)}) copy-start(f32[2187]{0:T(1024)} %copy-done.38) | copy-start | bytes 26248
  1129.7 752.6 %all-reduce.8.cloned.1.call-start = ((), (), s32[]{:S(2)}) async-start(), calls=%async_computation.24 | async-start | bytes 30449664 | tf_op jit(solution)/shard_map/psum | solution.py:264
  1195.4 8.3 copy-start.6
  1299.0 16.6 copy-start.3
  1344.5 8.2 copy-start.8
  1470.6 16.6 copy-start.4
  1558.6 14.8 slice-start.8
  1566.4 12.1 slice-start.6
  1603.9 346.6 %reduce-scatter.19.cloned.1.call-start = ((), (), s32[]{:S(2)}) async-start(), calls=%async_computation.19 | async-start | bytes 7962624 | tf_op jit(solution)/shard_map/reduce_scatter | solution.py:236
  1605.2 9.1 copy-start.19
  1605.2 9.1 copy-start.74
  1614.3 8.1 copy-start.14
  1614.3 8.1 copy-start.77
  1629.1 390.0 %reduce-scatter.23.cloned.1.call-start = ((), (), s32[]{:S(2)}) async-start(), calls=%async_computation.23 | async-start | bytes 7962624 | tf_op jit(solution)/shard_map/reduce_scatter | solution.py:236
  1629.2 9.0 copy-start.16
  1629.2 9.0 copy-start.75
  1682.7 8.8 copy-start.52
  1682.7 8.8 copy-start.53
  1682.7 8.8 copy-start.50
  1682.7 8.8 copy-start.51
  1682.7 8.8 copy-start.54
  1682.7 8.8 copy-start.55
  1682.8 8.8 copy-start.47
  1682.8 8.8 copy-start.48
  1682.8 8.9 copy-start.46
  1682.8 8.9 copy-start.49
  1896.6 122.6 %copy-start.23 = (f32[2187]{0:T(1024)S(1)}, f32[2187]{0:T(1024)}, u32[]{:S(2)}) copy-start(f32[2187]{0:T(1024)} %copy-done.22) | copy-start | bytes 26248
  1896.6 122.6 %copy-start.25 = (f32[2187]{0:T(1024)S(1)}, f32[2187]{0:T(1024)}, u32[]{:S(2)}) copy-start(f32[2187]{0:T(1024)} %copy-done.24) | copy-start | bytes 26248
  1896.6 122.6 %copy-start.27 = (f32[2187]{0:T(1024)S(1)}, f32[2187]{0:T(1024)}, u32[]{:S(2)}) copy-start(f32[2187]{0:T(1024)} %copy-done.26) | copy-start | bytes 26248
  1896.6 122.6 %copy-start.29 = (f32[2187]{0:T(1024)S(1)}, f32[2187]{0:T(1024)}, u32[]{:S(2)}) copy-start(f32[2187]{0:T(1024)} %copy-done.28) | copy-start | bytes 26248
  1896.6 122.6 %copy-start.45 = (f32[576]{0:T(1024)S(1)}, f32[576]{0:T(1024)}, u32[]{:S(2)}) copy-start(f32[576]{0:T(1024)} %copy-done.44) | copy-start | bytes 6916
  (45 other events, 201.8 us)
Sparse Core Ops, SparseCore 0:
  69.6 69.4 all-gather.12
  141.2 69.2 all-gather.8
  346.0 66.3 reduce-scatter.8
  466.0 66.4 reduce-scatter.12
  556.4 70.4 all-gather.14
  628.2 69.2 all-gather.20
  699.7 69.3 all-gather.10
  771.2 69.2 all-gather.16
  842.8 66.3 reduce-scatter.20
  911.4 66.3 reduce-scatter.16
  980.1 67.4 reduce-scatter.10
  1049.8 66.3 reduce-scatter.14
  1118.3 69.2 all-gather.18
  1189.0 69.2 all-gather.22
  1604.0 278.1 all-reduce.7
  1884.4 66.0 reduce-scatter.18
  1952.7 66.3 reduce-scatter.22
where the time goes:
time: 2170 us; the launch traced here: 2150 us
  waiting for transfers between devices  765 us (35%)
  matrix products  698 us (32%)
  local copies, waits for them, and re-layouts  323 us (15%)
  other arithmetic  257 us (12%)
  blocking collectives  95 us (4%)
    psum x1, waiting for transfers between devices, per_device(): lax.psum(totals[2].astype(jnp.bfloat16), 'dp').astype(jnp.float32)  190 us
    all_gather x4, waiting for transfers between devices, gather_rows(): return lax.all_gather(shard, 'tensor', axis=1, tiled=True)  165 us
    all_gather x4, waiting for transfers between devices, gather_grads(): return lax.all_gather(shard, 'tensor', axis=1, tiled=True)  161 us
    dot_general x12, matrix products, right_transposed(): lax.dot_general(left, right, (((1,), (1,)), ((), ())), preferred_element_...  158 us
    dot_general x12, matrix products, matmul(): return jnp.dot(left, right, preferred_element_type=jnp.float32)  141 us
    dot_general x12, matrix products, left_transposed(): lax.dot_general(left, right, (((0,), (0,)), ((), ())), preferred_element_...  128 us
    reduce_scatter x2, waiting for transfers between devices, per_device(): lax.psum_scatter(rounded(partial_first).astype(jnp.bfloat16), 'tensor', s...  118 us
    convert_element_type x2, other arithmetic, per_device(): (probs * (grad_probs - row_delta[..., None])).astype(jnp.bfloat16)  86.6 us
  transfers between devices with their start and end apart: 17, of which 14 were waited for; matrix products, arithmetic and copies ran while one was open for 34% of the time, Pallas kernels for 0%

commit v1 on v0

--- a/solution.py
+++ b/solution.py
@@ -1,8 +1,11 @@
+import functools
 import math
 
 import jax
 import jax.numpy as jnp
 from jax import lax
+from jax.experimental import pallas as pl
+from jax.experimental.pallas import tpu as pltpu
 from jax.sharding import PartitionSpec as P
 
 HDIM = 72
@@ -74,7 +77,7 @@
     return (value, slope)
 
 
-def per_device(
+def split_device(
     images,
     valid_flags,
     cotangent,
@@ -298,6 +301,1041 @@
     )
 
 
+F32 = jnp.float32
+BF16 = jnp.bfloat16
+LOG2E = math.log2(math.e)
+VMEM_BYTES = 58 * 1024 * 1024
+COST_SHARE = 0.02
+
+
+def dot_nn(left, right):
+    return jnp.dot(left, right, preferred_element_type=F32)
+
+
+def dot_nt(left, right):
+    return lax.dot_general(left, right, (((1,), (1,)), ((), ())), preferred_element_type=F32)
+
+
+def dot_tn(left, right):
+    return lax.dot_general(left, right, (((0,), (0,)), ((), ())), preferred_element_type=F32)
+
+
+def cost(flops, moved, trans=0):
+    return pl.CostEstimate(
+        flops=int(flops * COST_SHARE),
+        bytes_accessed=int(moved * COST_SHARE),
+        transcendentals=int(trans * COST_SHARE),
+    )
+
+
+def params(grid_dims):
+    return pltpu.CompilerParams(
+        dimension_semantics=("arbitrary",) * grid_dims, vmem_limit_bytes=VMEM_BYTES
+    )
+
+
+def once(shape, spot=None):
+    spot = spot or (0,) * len(shape)
+    return pl.BlockSpec(shape, lambda *_: spot, pipeline_mode=pl.Buffered(1))
+
+
+def image_block(shape, offset=0):
+    return pl.BlockSpec((1,) + shape, lambda i, *_: (offset + i, 0, 0))
+
+
+ANYWHERE = pl.BlockSpec(memory_space=pl.ANY)
+
+
+def column_stats(values):
+    mean = jnp.mean(values, axis=0, keepdims=True)
+    centred = values - mean
+    inverse = lax.rsqrt(jnp.mean(centred * centred, axis=0, keepdims=True) + EPS)
+    return centred * inverse, inverse
+
+
+def join_halves(first, own, other):
+    return jnp.concatenate(
+        [jnp.where(first, own, other), jnp.where(first, other, own)], axis=0
+    )
+
+
+def split_halves(first, full):
+    half = full.shape[0] // 2
+    low, high = full[:half], full[half:]
+    return jnp.where(first, low, high), jnp.where(first, high, low)
+
+
+def token_sum(values):
+    return jnp.sum(values, axis=1, keepdims=True)
+
+
+LN1_GAIN, LN1_BIAS, O_BIAS, LN2_GAIN, LN2_BIAS, FC2_BIAS = range(6)
+
+
+def as_row(column_sum):
+    rows = column_sum.shape[0]
+    return jnp.broadcast_to(column_sum, (rows, 128)).T[0:1]
+
+
+def column(ref, index):
+    return ref[:, index : index + 1]
+
+
+def write_rows(row_refs, sum_refs):
+    @pl.when(pl.program_id(0) == pl.num_programs(0) - 1)
+    def _():
+        for row_ref, sum_ref in zip(row_refs, sum_refs):
+            row_ref[...] = as_row(sum_ref[...])
+
+
+def store_heads(out_ref, first, product):
+    head_dim = out_ref.shape[2]
+    for head in range(product.shape[0] // head_dim):
+        out_ref[0, first + head] = product[head * head_dim : (head + 1) * head_dim].astype(BF16)
+
+
+def first_norm_kernel(
+    place_ref, own_ref, other_ref, feature_ref, q_ref, k_ref, v_ref, head_ref, *rest
+):
+    rows_ref, normed_ref, qkv_ref = rest[-3:]
+    full = join_halves(place_ref[0] == 0, own_ref[0].astype(F32), other_ref[0].astype(F32))
+    rows_ref[0] = full.astype(BF16)
+    normed, _ = column_stats(full)
+    low = (normed * column(feature_ref, LN1_GAIN) + column(feature_ref, LN1_BIAS)).astype(BF16)
+    normed_ref[0] = low
+    heads = qkv_ref.shape[1] // 3
+    store_heads(qkv_ref, 0, dot_nn(q_ref[...], low) + column(head_ref, 0))
+    store_heads(qkv_ref, heads, dot_nn(k_ref[...], low))
+    store_heads(qkv_ref, 2 * heads, dot_nn(v_ref[...], low) + column(head_ref, 1))
+
+
+def first_norm(index, count, place, images, other, features, weights, head_vectors, earlier):
+    _, half, seq = images.shape
+    width, feat = weights[0].shape
+    groups = 3 * width // HDIM
+    held = list(earlier) if earlier else []
+    return pl.pallas_call(
+        first_norm_kernel,
+        out_shape=[
+            jax.ShapeDtypeStruct((count, feat, seq), BF16),
+            jax.ShapeDtypeStruct((count, feat, seq), BF16),
+            jax.ShapeDtypeStruct((count, groups, HDIM, seq), BF16),
+        ],
+        grid_spec=pltpu.PrefetchScalarGridSpec(
+            num_scalar_prefetch=1,
+            grid=(1,),
+            in_specs=[
+                pl.BlockSpec((1, half, seq), lambda i, p: (p[0] * count + index, 0, 0)),
+                once((1, half, seq)),
+                once((feat, 8)),
+                once((width, feat)),
+                once((width, feat)),
+                once((width, feat)),
+                once((width, 8)),
+            ]
+            + [ANYWHERE] * len(held),
+            out_specs=[
+                once((1, feat, seq), (index, 0, 0)),
+                once((1, feat, seq), (index, 0, 0)),
+                once((1, groups, HDIM, seq), (index, 0, 0, 0)),
+            ],
+        ),
+        input_output_aliases={8 + k: k for k in range(len(held))},
+        compiler_params=params(1),
+        cost_estimate=cost(6 * seq * feat * width, 12 << 20),
+        name="first_norm",
+    )(place, images, other, features, *weights, head_vectors, *held)
+
+
+def project_kernel(normed_ref, q_ref, k_ref, v_ref, head_ref, qkv_ref):
+    low = normed_ref[0]
+    heads = qkv_ref.shape[1] // 3
+    store_heads(qkv_ref, 0, dot_nn(q_ref[...], low) + column(head_ref, 2))
+    store_heads(qkv_ref, heads, dot_nn(k_ref[...], low))
+    store_heads(qkv_ref, 2 * heads, dot_nn(v_ref[...], low) + column(head_ref, 3))
+
+
+def project(normed, weight, head_vectors, width):
+    count, feat, seq = normed.shape
+    groups = 3 * width // HDIM
+    return pl.pallas_call(
+        project_kernel,
+        grid=(count,),
+        out_shape=jax.ShapeDtypeStruct((count, groups, HDIM, seq), BF16),
+        in_specs=[
+            image_block((feat, seq)),
+            once((width, feat), (0, 0)),
+            once((width, feat), (1, 0)),
+            once((width, feat), (2, 0)),
+            once((width, 8)),
+        ],
+        out_specs=pl.BlockSpec((1, groups, HDIM, seq), lambda i: (i, 0, 0, 0)),
+        compiler_params=params(1),
+        cost_estimate=cost(6 * count * seq * feat * width, 20 << 20),
+        name="project",
+    )(normed, weight, weight, weight, head_vectors)
+
+
+def mix_kernel(q_ref, k_ref, v_ref, *rest, scale):
+    out_ref, log_ref = rest[-2:]
+    factor = scale * LOG2E
+    for head in range(q_ref.shape[1]):
+        scores = dot_tn(k_ref[0, head], q_ref[0, head])
+        top = jnp.max(scores, axis=0, keepdims=True)
+        probs = jnp.exp2((scores - top) * factor)
+        total = jnp.sum(probs, axis=0, keepdims=True)
+        mixed = dot_nn(v_ref[0, head], probs.astype(BF16))
+        out_ref[0, head] = (mixed * (1.0 / total)).astype(BF16)
+        log_ref[0, head] = top * factor + jnp.log2(total)
+
+
+def mix(qkv, half, start, steps, earlier, per_step=1):
+    count, groups, head_dim, seq = qkv.shape
+    heads = groups // 3
+    blocks = heads // per_step
+    block = (1, per_step, head_dim, seq)
+    held = list(earlier) if earlier else []
+
+    def at(offset):
+        return pl.BlockSpec(block, lambda i, j: (start + i, offset + j, 0, 0))
+
+    return pl.pallas_call(
+        functools.partial(mix_kernel, scale=1.0 / math.sqrt(head_dim)),
+        grid=(steps, blocks),
+        out_shape=[
+            jax.ShapeDtypeStruct((count, 2 * heads, head_dim, seq), BF16),
+            jax.ShapeDtypeStruct((count, 2 * heads, 1, seq), F32),
+        ],
+        in_specs=[at(0), at(blocks), at(2 * blocks)] + [ANYWHERE] * len(held),
+        out_specs=[
+            at(half * blocks),
+            pl.BlockSpec(
+                (1, per_step, 1, seq), lambda i, j: (start + i, half * blocks + j, 0, 0)
+            ),
+        ],
+        input_output_aliases={3 + k: k for k in range(len(held))},
+        compiler_params=params(2),
+        cost_estimate=cost(
+            4 * steps * heads * seq * seq * 256,
+            steps * heads * head_dim * seq * 8,
+            steps * heads * seq * seq,
+        ),
+        name="mix",
+    )(qkv, qkv, qkv, *held)
+
+
+def mix_back_kernel(q_ref, k_ref, v_ref, out_ref, log_ref, grad_ref, *rest, scale, heads):
+    d_ref = rest[-1]
+    factor = scale * LOG2E
+    per_step = q_ref.shape[1]
+    first = pl.program_id(1) * per_step
+    for head in range(per_step):
+        query, keys, values = q_ref[0, head], k_ref[0, head], v_ref[0, head]
+        grad = grad_ref[0, head]
+        delta = jnp.sum(grad.astype(F32) * out_ref[0, head].astype(F32), axis=0, keepdims=True)
+        probs = jnp.exp2(dot_tn(keys, query) * factor - log_ref[0, head])
+        grad_scores = (probs * (dot_tn(values, grad) - delta)).astype(BF16)
+        d_ref[0, 2 * heads + first + head] = dot_nt(grad, probs.astype(BF16)).astype(BF16)
+        d_ref[0, first + head] = (dot_nn(keys, grad_scores) * scale).astype(BF16)
+        d_ref[0, heads + first + head] = (dot_nt(query, grad_scores) * scale).astype(BF16)
+
+
+def mix_back(qkv, out, log_total, grad, half, start, steps, earlier, per_step=2):
+    count, groups, head_dim, seq = qkv.shape
+    heads = groups // 3
+    blocks = heads // per_step
+    block = (1, per_step, head_dim, seq)
+    held = [] if earlier is None else [earlier]
+
+    def at(offset):
+        return pl.BlockSpec(block, lambda i, j: (start + i, offset + j, 0, 0))
+
+    return pl.pallas_call(
+        functools.partial(mix_back_kernel, scale=1.0 / math.sqrt(head_dim), heads=heads),
+        grid=(steps, blocks),
+        out_shape=jax.ShapeDtypeStruct(qkv.shape, BF16),
+        in_specs=[
+            at(0),
+            at(blocks),
+            at(2 * blocks),
+            at(half * blocks),
+            pl.BlockSpec((1, per_step, 1, seq), lambda i, j: (start + i, half * blocks + j, 0, 0)),
+            at(half * blocks),
+        ]
+        + [ANYWHERE] * len(held),
+        input_output_aliases={6: 0} if held else {},
+        out_specs=pl.BlockSpec((1, groups, head_dim, seq), lambda i, j: (start + i, 0, 0, 0)),
+        compiler_params=params(2),
+        cost_estimate=cost(
+            10 * steps * heads * seq * seq * 256,
+            steps * heads * head_dim * seq * 16,
+            steps * heads * seq * seq,
+        ),
+        name="mix_back",
+    )(qkv, qkv, qkv, out, log_total, grad, *held)
+
+
+def second_norm_kernel(
+    place_ref,
+    ctx_ref,
+    w_own_ref,
+    w_other_ref,
+    rows_ref,
+    feature_ref,
+    cot_own_ref,
+    cot_other_ref,
+    resid_ref,
+    low_ref,
+    grad_ref,
+    row_ref,
+    w_ref,
+    sum_ref,
+):
+    step = pl.program_id(0)
+    half = w_own_ref.shape[0]
+
+    @pl.when(step == 0)
+    def _():
+        w_ref[:half] = w_own_ref[...]
+        w_ref[half:] = w_other_ref[...]
+        sum_ref[...] = jnp.zeros_like(sum_ref)
+
+    resid = rows_ref[0].astype(F32) + dot_tn(w_ref[...], ctx_ref[0])
+    resid += column(feature_ref, O_BIAS)
+    resid_ref[0] = resid
+    normed, _ = column_stats(resid)
+    low_ref[0] = (
+        normed * column(feature_ref, LN2_GAIN) + column(feature_ref, LN2_BIAS)
+    ).astype(BF16)
+    flag = place_ref[2 + place_ref[0] * pl.num_programs(0) + step].astype(F32)
+    grad = flag * join_halves(
+        place_ref[0] == 0, cot_own_ref[0].astype(F32), cot_other_ref[0].astype(F32)
+    )
+    grad_ref[0] = grad.astype(BF16)
+    sum_ref[...] += token_sum(grad)
+    write_rows((row_ref,), (sum_ref,))
+
+
+def second_norm(place, ctx, w_own, w_other, rows, features, cot, cot_other):
+    count, feat, seq = rows.shape
+    half = w_own.shape[0]
+    full = image_block((feat, seq))
+    return pl.pallas_call(
+        second_norm_kernel,
+        out_shape=[
+            jax.ShapeDtypeStruct((count, feat, seq), F32),
+            jax.ShapeDtypeStruct((count, feat, seq), BF16),
+            jax.ShapeDtypeStruct((count, feat, seq), BF16),
+            jax.ShapeDtypeStruct((1, feat), F32),
+        ],
+        grid_spec=pltpu.PrefetchScalarGridSpec(
+            num_scalar_prefetch=1,
+            grid=(count,),
+            in_specs=[
+                full,
+                once((half, feat)),
+                once((half, feat), (3, 0)),
+                full,
+                once((feat, 8)),
+                pl.BlockSpec((1, feat // 2, seq), lambda i, p: (p[0] * count + i, 0, 0)),
+                image_block((feat // 2, seq)),
+            ],
+            out_specs=[full, full, full, once((1, feat))],
+            scratch_shapes=[pltpu.VMEM((feat, feat), BF16), pltpu.VMEM((feat, 1), F32)],
+        ),
+        compiler_params=params(1),
+        cost_estimate=cost(4 * count * seq * half * feat, 40 << 20),
+        name="second_norm",
+    )(place, ctx, w_own, w_other, rows, features, cot, cot_other)
+
+
+def hidden_kernel(place_ref, low_ref, grad_ref, fc1_ref, fc2_ref, bias_ref, *rest, which):
+    act_ref, back_ref, gb_ref, g1_ref, g2_ref = rest[-5:]
+    g1, g2, gb = None, None, None
+    for image in range(low_ref.shape[0]):
+        low, grad = low_ref[image], grad_ref[image]
+        pre = dot_nn(fc1_ref[...], low) + column(bias_ref, which)
+        square = pre * pre
+        tanh_val = jnp.tanh(pre * (GELU_C + (GELU_C * GELU_A) * square))
+        half = 0.5 * tanh_val + 0.5
+        act = pre * half
+        slope = half + act * (1.0 - half) * (2 * GELU_C + (6 * GELU_C * GELU_A) * square)
+        act = act.astype(BF16)
+        act_ref[image] = act
+        back = (dot_nn(fc2_ref[...], grad) * slope).astype(BF16)
+        back_ref[image] = back
+        parts = dot_nt(back, low), dot_nt(act, grad), token_sum(back.astype(F32))
+        g1 = parts[0] if g1 is None else g1 + parts[0]
+        g2 = parts[1] if g2 is None else g2 + parts[1]
+        gb = parts[2] if gb is None else gb + parts[2]
+    gb_ref[...] = gb
+    g1_ref[...] = g1.astype(BF16)
+    g2_ref[...] = g2.astype(BF16)
+
+
+def quarter_rows(hidden):
+    return (-(-hidden // 4) + 7) // 8 * 8
+
+
+def hidden_stage(keep, place, low, grad, fc1, fc2, fc2_offset, bias, which, earlier):
+    count, feat, seq = low.shape
+    hidden = bias.shape[0]
+    block = quarter_rows(hidden)
+    held = list(earlier) if earlier else []
+
+    def chunk(j, p):
+        return j + 2 * (p[1] if keep else 1 - p[1])
+
+    weight = pl.BlockSpec((block, feat), lambda j, p: (chunk(j, p), 0))
+    tokens = pl.BlockSpec((count, block, seq), lambda j, p: (0, chunk(j, p), 0))
+    grads = pl.BlockSpec((block, feat), lambda j, p: (j, 0))
+    part = jax.ShapeDtypeStruct((2 * block, feat), BF16)
+    return pl.pallas_call(
+        functools.partial(hidden_kernel, which=which),
+        out_shape=[
+            jax.ShapeDtypeStruct((count, hidden, seq), BF16),
+            jax.ShapeDtypeStruct((count, hidden, seq), BF16),
+            jax.ShapeDtypeStruct((hidden, 1), F32),
+            part,
+            part,
+        ],
+        grid_spec=pltpu.PrefetchScalarGridSpec(
+            num_scalar_prefetch=1,
+            grid=(2,),
+            in_specs=[
+                once((count, feat, seq)),
+                once((count, feat, seq)),
+                weight,
+                pl.BlockSpec((block, feat), lambda j, p: (fc2_offset + chunk(j, p), 0)),
+                pl.BlockSpec((block, 2), lambda j, p: (chunk(j, p), 0)),
+            ]
+            + [ANYWHERE] * len(held),
+            out_specs=[
+                tokens,
+                tokens,
+                pl.BlockSpec((block, 1), lambda j, p: (chunk(j, p), 0)),
+                grads,
+                grads,
+            ],
+        ),
+        input_output_aliases={6 + k: k for k in range(len(held))},
+        compiler_params=params(1),
+        cost_estimate=cost(4 * count * seq * feat * hidden, 30 << 20, count * seq * hidden // 2),
+        name="hidden_stage",
+    )(place, low, grad, fc1, fc2, bias, *held)
+
+
+def layer_kernel(
+    place_ref, act_own_ref, act_other_ref, w_own_ref, w_other_ref, resid_ref, b_ref, out_ref, send_ref
+):
+    hidden = act_own_ref.shape[1]
+    branch = dot_tn(w_own_ref[:hidden], act_own_ref[0])
+    branch += dot_tn(w_other_ref[:hidden], act_other_ref[0])
+    flag = place_ref[2 + place_ref[0] * pl.num_programs(0) + pl.program_id(0)].astype(F32)
+    result = (resid_ref[0] + branch + column(b_ref, FC2_BIAS)) * flag
+    own, other = split_halves(place_ref[0] == 0, result)
+    out_ref[0] = own.astype(BF16)
+    send_ref[0] = other.astype(BF16)
+
+
+def layer_result(place, act_own, act_other, w_own, w_other, resid, bias):
+    count, feat, seq = resid.shape
+    hidden = act_own.shape[1]
+    full = image_block((hidden, seq))
+    padded = 4 * quarter_rows(hidden)
+    return pl.pallas_call(
+        layer_kernel,
+        out_shape=[
+            jax.ShapeDtypeStruct((2 * count, feat // 2, seq), BF16),
+            jax.ShapeDtypeStruct((count, feat // 2, seq), BF16),
+        ],
+        grid_spec=pltpu.PrefetchScalarGridSpec(
+            num_scalar_prefetch=1,
+            grid=(count,),
+            in_specs=[
+                full,
+                full,
+                once((hidden, feat)),
+                once((padded, feat), (1, 0)),
+                image_block((feat, seq)),
+                once((feat, 8)),
+            ],
+            out_specs=[
+                pl.BlockSpec((1, feat // 2, seq), lambda i, p: (p[0] * count + i, 0, 0)),
+                image_block((feat // 2, seq)),
+            ],
+        ),
+        compiler_params=params(1),
+        cost_estimate=cost(4 * count * seq * feat * hidden, 45 << 20),
+        name="layer_result",
+    )(place, act_own, act_other, w_own, w_other, resid, bias)
+
+
+def resid_back_kernel(
+    back_own_ref,
+    back_other_ref,
+    w_own_ref,
+    w_other_ref,
+    resid_ref,
+    grad_ref,
+    gain_ref,
+    low_ref,
+    row_gain_ref,
+    row_bias_ref,
+    row_ob_ref,
+    sum_gain_ref,
+    sum_bias_ref,
+    sum_ob_ref,
+):
+    hidden = back_own_ref.shape[1]
+    grad_norm = dot_tn(w_own_ref[:hidden], back_own_ref[0])
+    grad_norm += dot_tn(w_other_ref[:hidden], back_other_ref[0])
+    normed, inverse = column_stats(resid_ref[0])
+    scaled = grad_norm * column(gain_ref, LN2_GAIN)
+    plain = jnp.mean(scaled, axis=0, keepdims=True)
+    cross = jnp.mean(scaled * normed, axis=0, keepdims=True)
+    grad = grad_ref[0].astype(F32) + inverse * (scaled - plain - normed * cross)
+    low_ref[0] = grad.astype(BF16)
+
+    @pl.when(pl.program_id(0) == 0)
+    def _():
+        sum_gain_ref[...] = jnp.zeros_like(sum_gain_ref)
+        sum_bias_ref[...] = jnp.zeros_like(sum_bias_ref)
+        sum_ob_ref[...] = jnp.zeros_like(sum_ob_ref)
+
+    sum_gain_ref[...] += token_sum(grad_norm * normed)
+    sum_bias_ref[...] += token_sum(grad_norm)
+    sum_ob_ref[...] += token_sum(grad)
+    write_rows((row_gain_ref, row_bias_ref, row_ob_ref), (sum_gain_ref, sum_bias_ref, sum_ob_ref))
+
+
+def resid_back(back_own, back_other, w_own, w_other, resid, grad, gain):
+    count, feat, seq = resid.shape
+    hidden = back_own.shape[1]
+    padded = 4 * quarter_rows(hidden)
+    wide = image_block((hidden, seq))
+    full = image_block((feat, seq))
+    return pl.pallas_call(
+        resid_back_kernel,
+        grid=(count,),
+        out_shape=[jax.ShapeDtypeStruct((count, feat, seq), BF16)]
+        + [jax.ShapeDtypeStruct((1, feat), F32)] * 3,
+        in_specs=[
+            wide,
+            wide,
+            once((hidden, feat)),
+            once((padded, feat)),
+            full,
+            full,
+            once((feat, 8)),
+        ],
+        out_specs=[full] + [once((1, feat))] * 3,
+        scratch_shapes=[pltpu.VMEM((feat, 1), F32)] * 3,
+        compiler_params=params(1),
+        cost_estimate=cost(4 * count * seq * feat * hidden, 50 << 20),
+        name="resid_back",
+    )(back_own, back_other, w_own, w_other, resid, grad, gain)
+
+
+def context_back_kernel(
+    place_ref,
+    low_ref,
+    ctx_ref,
+    w_own_ref,
+    w_other_ref,
+    d_ref,
+    own_keep_ref,
+    own_send_ref,
+    other_keep_ref,
+    other_send_ref,
+    acc_ref,
+):
+    step = pl.program_id(0)
+    low = low_ref[0]
+    half = w_own_ref.shape[0]
+    d_ref[0, :half] = dot_nn(w_own_ref[...], low).astype(BF16)
+    d_ref[0, half:] = dot_nn(w_other_ref[...], low).astype(BF16)
+    product = dot_nt(ctx_ref[0], low)
+
+    @pl.when(step == 0)
+    def _():
+        acc_ref[...] = product
+
+    @pl.when(step > 0)
+    def _():
+        acc_ref[...] += product
+
+    @pl.when(step == pl.num_programs(0) - 1)
+    def _():
+        part = half // 2
+        keep = place_ref[1] * part
+        send = part - keep
+        own_keep_ref[...] = acc_ref[pl.ds(pl.multiple_of(keep, 8), part)].astype(BF16)
+        own_send_ref[...] = acc_ref[pl.ds(pl.multiple_of(send, 8), part)].astype(BF16)
+        other_keep_ref[...] = acc_ref[pl.ds(pl.multiple_of(half + keep, 8), part)].astype(BF16)
+        other_send_ref[...] = acc_ref[pl.ds(pl.multiple_of(half + send, 8), part)].astype(BF16)
+
+
+def context_back(place, low, ctx, w_own, w_other):
+    count, feat, seq = low.shape
+    half = w_own.shape[0]
+    full = image_block((feat, seq))
+    part = jax.ShapeDtypeStruct((half // 2, feat), BF16)
+    return pl.pallas_call(
+        context_back_kernel,
+        out_shape=[jax.ShapeDtypeStruct((count, 2 * half, seq), BF16)] + [part] * 4,
+        grid_spec=pltpu.PrefetchScalarGridSpec(
+            num_scalar_prefetch=1,
+            grid=(count,),
+            in_specs=[
+                full,
+                image_block((2 * half, seq)),
+                once((half, feat)),
+                once((half, feat), (3, 0)),
+            ],
+            out_specs=[image_block((2 * half, seq))] + [once((half // 2, feat))] * 4,
+            scratch_shapes=[pltpu.VMEM((2 * half, feat), F32)],
+        ),
+        compiler_params=params(1),
+        cost_estimate=cost(8 * count * seq * half * feat, 25 << 20),
+        name="context_back",
+    )(place, low, ctx, w_own, w_other)
+
+
+def project_back_kernel(place_ref, normed_ref, d_ref, keep_ref, send_ref, col_ref, acc_ref):
+    step = pl.program_id(0)
+    product = dot_nt(d_ref[0], normed_ref[0])
+    column = token_sum(d_ref[0].astype(F32))
+
+    @pl.when(step == 0)
+    def _():
+        acc_ref[...] = product
+        col_ref[...] = column
+
+    @pl.when(step > 0)
+    def _():
+        acc_ref[...] += product
+        col_ref[...] += column
+
+    @pl.when(step == pl.num_programs(0) - 1)
+    def _():
+        part = keep_ref.shape[0] // 3
+        keep = place_ref[1] * part
+        for index in range(3):
+            rows = slice(index * part, (index + 1) * part)
+            first = 2 * index * part
+            keep_rows = pl.ds(pl.multiple_of(first + keep, 8), part)
+            send_rows = pl.ds(pl.multiple_of(first + part - keep, 8), part)
+            keep_ref[rows] = acc_ref[keep_rows].astype(BF16)
+            send_ref[rows] = acc_ref[send_rows].astype(BF16)
+
+
+def project_back(place, normed, d_qkv):
+    count, feat, seq = normed.shape
+    width = d_qkv.shape[1]
+    part = jax.ShapeDtypeStruct((width // 2, feat), BF16)
+    return pl.pallas_call(
+        project_back_kernel,
+        out_shape=[part, part, jax.ShapeDtypeStruct((width, 1), F32)],
+        grid_spec=pltpu.PrefetchScalarGridSpec(
+            num_scalar_prefetch=1,
+            grid=(count,),
+            in_specs=[image_block((feat, seq)), image_block((width, seq))],
+            out_specs=[
+                once((width // 2, feat)),
+                once((width // 2, feat)),
+                once((width, 1)),
+            ],
+            scratch_shapes=[pltpu.VMEM((width, feat), F32)],
+        ),
+        compiler_params=params(1),
+        cost_estimate=cost(2 * count * seq * feat * width, 20 << 20),
+        name="project_back",
+    )(place, normed, d_qkv)
+
+
+def input_back_kernel(
+    place_ref,
+    d_own_ref,
+    d_other_ref,
+    q_ref,
+    k_ref,
+    v_ref,
+    w_other_ref,
+    rows_ref,
+    low_ref,
+    gain_ref,
+    out_ref,
+    send_ref,
+    row_gain_ref,
+    row_bias_ref,
+    w_ref,
+    sum_gain_ref,
+    sum_bias_ref,
+):
+    width = q_ref.shape[0]
+
+    @pl.when(pl.program_id(0) == 0)
+    def _():
+        w_ref[:width] = q_ref[...]
+        w_ref[width : 2 * width] = k_ref[...]
+        w_ref[2 * width :] = v_ref[...]
+        sum_gain_ref[...] = jnp.zeros_like(sum_gain_ref)
+        sum_bias_ref[...] = jnp.zeros_like(sum_bias_ref)
+
+    grad_norm = dot_tn(w_ref[...], d_own_ref[0]) + dot_tn(w_other_ref[...], d_other_ref[0])
+    normed, inverse = column_stats(rows_ref[0].astype(F32))
+    scaled = grad_norm * column(gain_ref, LN1_GAIN)
+    plain = jnp.mean(scaled, axis=0, keepdims=True)
+    cross = jnp.mean(scaled * normed, axis=0, keepdims=True)
+    grad = low_ref[0].astype(F32) + inverse * (scaled - plain - normed * cross)
+    own, other = split_halves(place_ref[0] == 0, grad)
+    out_ref[0] = own.astype(BF16)
+    send_ref[0] = other.astype(BF16)
+    sum_gain_ref[...] += token_sum(grad_norm * normed)
+    sum_bias_ref[...] += token_sum(grad_norm)
+    write_rows((row_gain_ref, row_bias_ref), (sum_gain_ref, sum_bias_ref))
+
+
+def input_back(place, d_own, d_other, weights, w_other, rows, low, gain):
+    count, width, seq = d_own.shape
+    feat = rows.shape[1]
+    wide = image_block((width, seq))
+    full = image_block((feat, seq))
+    return pl.pallas_call(
+        input_back_kernel,
+        out_shape=[
+            jax.ShapeDtypeStruct((2 * count, feat // 2, seq), BF16),
+            jax.ShapeDtypeStruct((count, feat // 2, seq), BF16),
+            jax.ShapeDtypeStruct((1, feat), F32),
+            jax.ShapeDtypeStruct((1, feat), F32),
+        ],
+        grid_spec=pltpu.PrefetchScalarGridSpec(
+            num_scalar_prefetch=1,
+            grid=(count,),
+            in_specs=[wide, wide]
+            + [once((width // 3, feat))] * 3
+            + [once((width, feat)), full, full, once((feat, 8))],
+            out_specs=[
+                pl.BlockSpec((1, feat // 2, seq), lambda i, p: (p[0] * count + i, 0, 0)),
+                image_block((feat // 2, seq)),
+                once((1, feat)),
+                once((1, feat)),
+            ],
+            scratch_shapes=[
+                pltpu.VMEM((width, feat), BF16),
+                pltpu.VMEM((feat, 1), F32),
+                pltpu.VMEM((feat, 1), F32),
+            ],
+        ),
+        compiler_params=params(1),
+        cost_estimate=cost(4 * count * seq * feat * width, 40 << 20),
+        name="input_back",
+    )(place, d_own, d_other, *weights, w_other, rows, low, gain)
+
+
+def widen_kernel(place_ref, mine_ref, other_ref, out_ref):
+    mine = pl.program_id(0) == place_ref[1]
+    out_ref[...] = jnp.where(mine, mine_ref[...], other_ref[...]).astype(F32)
+
+
+def widen(place, mine, other, offset, part, total, steps):
+    feat = mine.shape[1]
+    rows = part // steps
+    spec = pl.BlockSpec((rows, feat), lambda h, i, p: (offset // rows + i, 0))
+    return pl.pallas_call(
+        widen_kernel,
+        out_shape=jax.ShapeDtypeStruct((total, feat), F32),
+        grid_spec=pltpu.PrefetchScalarGridSpec(
+            num_scalar_prefetch=1,
+            grid=(2, steps),
+            in_specs=[spec, spec],
+            out_specs=pl.BlockSpec((rows, feat), lambda h, i, p: (h * steps + i, 0)),
+        ),
+        compiler_params=params(2),
+        cost_estimate=cost(0, 8 * total * feat),
+        name="widen",
+    )(place, mine, other)
+
+
+def swap_tensor(value):
+    return lax.ppermute(value, "tensor", [(0, 1), (1, 0)])
+
+
+def swap_core(value):
+    return lax.ppermute(value, "dp", [(spot, spot ^ 1) for spot in range(lax.axis_size("dp"))])
+
+
+def other_weights(weights, spots, rows):
+    per_weight = spots // len(weights)
+    mine = lax.axis_index("dp")
+    start = mine % per_weight * rows
+    piece = None
+    for index, weight in enumerate(weights):
+        short = per_weight * rows - weight.shape[0]
+        if short:
+            weight = jnp.pad(weight, ((0, short), (0, 0)))
+        part = lax.dynamic_slice_in_dim(weight, start, rows, 0)
+        piece = part if piece is None else jnp.where(mine // per_weight == index, part, piece)
+    return piece
+
+
+def chip_groups(order):
+    spots = lax.axis_size("dp")
+    groups = [list(range(core, spots, 2)) for core in range(2)]
+    if order == 1:
+        return groups[::-1]
+    return [group[::-1] for group in groups] if order == 2 else groups
+
+
+def both(keep, send):
+    return keep.astype(F32) + swap_core(send).astype(F32)
+
+
+def after(value, *others):
+    return lax.optimization_barrier((value, *others))[0]
+
+
+def whole_device(
+    images,
+    valid_flags,
+    cotangent,
+    ln1_gain,
+    ln1_bias,
+    q_weight,
+    q_bias,
+    k_weight,
+    v_weight,
+    v_bias,
+    o_weight,
+    o_bias,
+    ln2_gain,
+    ln2_bias,
+    fc1_weight,
+    fc1_bias,
+    fc2_weight,
+    fc2_bias,
+):
+    img_local, seq, half = images.shape
+    count = img_local // 2
+    feat = 2 * half
+    spots = lax.axis_size("dp")
+    width = q_weight.shape[1]
+    hidden = fc1_weight.shape[1]
+    heads = width // HDIM
+    tensor = lax.axis_index("tensor")
+    core = lax.axis_index("dp") % 2
+    place = jnp.concatenate(
+        [jnp.stack([tensor, core]).astype(jnp.int32), valid_flags.astype(jnp.int32)]
+    )
+    images, cotangent = jnp.swapaxes(images, 1, 2), jnp.swapaxes(cotangent, 1, 2)
+    in_weights = [q_weight.T, k_weight.T, v_weight.T]
+    fc1_own = fc1_weight.T
+
+    def to_other(array, index):
+        return swap_tensor(
+            lax.dynamic_slice_in_dim(array, (1 - tensor) * count + index, 1, 0)
+        )
+
+    small = jnp.concatenate(
+        [ln1_gain, ln1_bias, o_bias, ln2_gain, ln2_bias, fc2_bias, q_bias, v_bias, fc1_bias]
+    )
+    cut_q, cut_v, cut_h = 6 * half, 6 * half + width, 6 * half + 2 * width
+    block = quarter_rows(hidden)
+
+    images_other = [to_other(images, 0)]
+    small_other = swap_tensor(small)
+    in_piece = other_weights([*in_weights, o_weight], spots, width // (spots // 4))
+    in_piece = swap_tensor(after(in_piece, images_other[0]))
+    images_other.append(to_other(after(images, images_other[0]), 1))
+    mlp_piece = other_weights([fc1_own, fc2_weight], spots, block // 2)
+
+    def features_of(source):
+        return source[:cut_q].reshape(6, half)
+
+    feature_own, feature_other = features_of(small), features_of(small_other)
+    features = jnp.where(
+        tensor == 0,
+        jnp.concatenate([feature_own, feature_other], axis=1),
+        jnp.concatenate([feature_other, feature_own], axis=1),
+    )
+    features = jnp.pad(features, ((0, 2), (0, 0))).astype(F32).T
+    head_vectors = jnp.stack([small, small_other])[:, cut_q:cut_h].reshape(4, width)
+    head_vectors = jnp.pad(head_vectors, ((0, 4), (0, 0))).astype(F32).T
+    hidden_vectors = jnp.stack([small, small_other])[:, cut_h:].astype(F32).T
+
+    state = None
+    mixed = None
+    for index in range(count):
+        state = first_norm(
+            index,
+            count,
+            place,
+            images,
+            images_other[index],
+            features,
+            in_weights,
+            head_vectors,
+            state,
+        )
+        state = list(state)
+        if index == 0:
+            in_piece, held = lax.optimization_barrier((in_piece, state[2]))
+            state[2] = held
+            in_other = lax.all_gather(in_piece, "dp", axis=0, tiled=True)
+        if index == 1:
+            mlp_piece, held = lax.optimization_barrier((mlp_piece, state[2]))
+            state[2] = held
+            mlp_other = lax.all_gather(mlp_piece, "dp", axis=0, tiled=True)
+        mixed = list(mix(state[2], 0, index, 1, mixed))
+        if index + 2 == len(images_other) and len(images_other) < count:
+            turn = lax.optimization_barrier((images, images_other[-1], mixed[0]))
+            images_other[-1], mixed[0] = turn[1:]
+            images_other.append(to_other(turn[0], index + 2))
+            if index == 0:
+                mlp_piece = swap_tensor(after(mlp_piece, turn[1]))
+        elif len(images_other) == count and index + 2 == count:
+            turn = lax.optimization_barrier((cotangent, images_other[-1], mixed[0]))
+            images_other[-1], mixed[0] = turn[1:]
+            cot_other = jnp.concatenate([to_other(turn[0], spot) for spot in range(count)])
+    rows, normed, qkv_own = state
+    qkv_other = project(normed, in_other, head_vectors, width)
+    ctx, logs = mix(qkv_other, 1, 0, count, mixed)
+    flat = (count, 2 * width, seq)
+    resid, low_second, grad_out, sum_fc2b = second_norm(
+        place, ctx.reshape(flat), o_weight, in_other, rows, features, cotangent, cot_other
+    )
+
+    def stage(keep, place, weights, offset, which, earlier):
+        return hidden_stage(
+            keep, place, low_second, grad_out, *weights, offset, hidden_vectors, which, earlier
+        )
+
+    *held, fc1_o, fc2_o = stage(False, place, (mlp_other, mlp_other), 4, 1, None)
+    *stage_other, fc1_k, fc2_k = stage(True, place, (mlp_other, mlp_other), 4, 1, held)
+    fc1_send, fc2_send = both(fc1_k, fc1_o).astype(BF16), both(fc2_k, fc2_o).astype(BF16)
+    place2, fc1_send, fc2_send = lax.optimization_barrier((place, fc1_send, fc2_send))
+    fc1_arrived = swap_tensor(fc1_send)
+    *held, fc1_o, fc2_o = stage(False, place2, (fc1_own, fc2_weight), 0, 0, None)
+    fc2_send, held[2] = lax.optimization_barrier((fc2_send, held[2]))
+    fc2_arrived = swap_tensor(fc2_send)
+    *stage_own, fc1_k, fc2_k = stage(True, place2, (fc1_own, fc2_weight), 0, 0, held)
+    g_fc1 = (both(fc1_k, fc1_o) + fc1_arrived.astype(F32)).astype(BF16)
+    fc2_pair = both(fc2_k, fc2_o).astype(BF16)
+    g_fc1, fc2_pair, back_own = lax.optimization_barrier((g_fc1, fc2_pair, stage_own[1]))
+    g_fc1 = lax.psum(g_fc1, "dp", axis_index_groups=chip_groups(0))
+    low_resid, sum_gain2, sum_bias2, sum_ob = resid_back(
+        back_own, stage_other[1], fc1_own, mlp_other, resid, grad_out, features
+    )
+    d_ctx, *o_parts = context_back(place, low_resid, ctx.reshape(flat), o_weight, in_other)
+    d_ctx, fc2_arrived, fc2_pair = lax.optimization_barrier(
+        (d_ctx.reshape(ctx.shape), fc2_arrived, fc2_pair)
+    )
+    wide = (count, 3 * width, seq)
+    d_other = mix_back(qkv_other, ctx, logs, d_ctx, 1, 0, count, None).reshape(wide)
+    o_send = both(o_parts[2], o_parts[3]).astype(BF16)
+    o_pair = both(o_parts[0], o_parts[1])
+    d_other, o_send, o_pair = lax.optimization_barrier((d_other, o_send, o_pair))
+    o_arrived = swap_tensor(o_send)
+    other_keep, other_send, column_other = project_back(place, normed, d_other)
+    o_arrived, other_keep = lax.optimization_barrier((o_arrived, other_keep))
+    g_fc2 = fc2_pair.astype(F32) + fc2_arrived.astype(F32)
+    g_late = jnp.concatenate([g_fc2, o_pair + o_arrived.astype(F32)]).astype(BF16)
+    d_ctx, g_late = lax.optimization_barrier((d_ctx, g_late))
+    g_late = lax.psum(g_late, "dp", axis_index_groups=chip_groups(1))
+
+    d_own = mix_back(qkv_own, ctx, logs, d_ctx, 0, 0, 1, None)
+    qkv_send = both(other_keep, other_send).astype(BF16)
+    d_own, qkv_send, g_fc1 = lax.optimization_barrier((d_own, qkv_send, g_fc1))
+    qkv_arrived = swap_tensor(qkv_send)
+    fc1_other = swap_core(g_fc1)
+    d_own = mix_back(qkv_own, ctx, logs, d_ctx, 0, 1, count - 1, d_own).reshape(wide)
+    own_keep, own_send, column_own = project_back(place, normed, d_own)
+    own_keep, fc1_other = lax.optimization_barrier((own_keep, fc1_other))
+    out_fc1 = widen(place, g_fc1, fc1_other, 0, 2 * block, hidden, 4)
+    own_swapped, qkv_arrived, out_fc1 = lax.optimization_barrier(
+        (swap_core(own_send), qkv_arrived, out_fc1)
+    )
+    g_qkv = own_keep.astype(F32) + own_swapped.astype(F32) + qkv_arrived.astype(F32)
+    g_qkv, d_own = lax.optimization_barrier((g_qkv.astype(BF16), d_own))
+    g_qkv = lax.psum(g_qkv, "dp", axis_index_groups=chip_groups(2))
+    in_buffer, in_send, sum_gain1, sum_bias1 = input_back(
+        place, d_own, d_other, in_weights, in_other, rows, low_resid, features
+    )
+    in_send, act_own = lax.optimization_barrier((in_send, stage_own[0]))
+    far = (1 - tensor) * count
+    in_arrived = swap_tensor(in_send)
+    out_buffer, out_send = layer_result(
+        place, act_own, stage_other[0], fc2_weight, mlp_other, resid, features
+    )
+    in_arrived, out_send = lax.optimization_barrier((in_arrived, out_send))
+    out_arrived = swap_tensor(out_send)
+    input_grad = lax.dynamic_update_slice_in_dim(in_buffer, in_arrived, far, 0)
+    layer_out = lax.dynamic_update_slice_in_dim(out_buffer, out_arrived, far, 0)
+
+    sums = jnp.concatenate([sum_gain1, sum_bias1, sum_ob, sum_gain2, sum_bias2, sum_fc2b])
+
+    def ordered(own, other):
+        return jnp.where(tensor == 0, jnp.stack([own, other]), jnp.stack([other, own]))
+
+    def heads_part(vector):
+        return vector[:width, 0], vector[2 * width :, 0]
+
+    (q_own, v_own), (q_other, v_other) = heads_part(column_own), heads_part(column_other)
+    small_grads = jnp.concatenate(
+        [
+            sums.reshape(-1),
+            ordered(
+                jnp.concatenate([q_own, v_own, stage_own[2][:, 0]]),
+                jnp.concatenate([q_other, v_other, stage_other[2][:, 0]]),
+            ).reshape(-1),
+        ]
+    )
+    step = 1
+    while step < spots:
+        small_grads += lax.ppermute(
+            small_grads, "dp", [(spot, spot ^ step) for spot in range(spots)]
+        )
+        step *= 2
+    small_grads += swap_tensor(small_grads)
+    g_feature = lax.dynamic_slice_in_dim(
+        small_grads[: 6 * feat].reshape(6, feat), tensor * half, half, 1
+    )
+    small_grads = lax.dynamic_index_in_dim(
+        small_grads[6 * feat :].reshape(2, 2 * width + hidden), tensor, 0, keepdims=False
+    )
+
+    late_other = swap_core(g_late)
+    qkv_other_core = swap_core(g_qkv)
+    g_fc2 = widen(place, g_late, late_other, 0, 2 * block, hidden, 4)
+    g_o = widen(
+        place, g_late[2 * block :], late_other[2 * block :], 0, width // 2, width, 1
+    )
+    g_q, g_k, g_v = (
+        widen(place, g_qkv, qkv_other_core, index * width // 2, width // 2, width, 1)
+        for index in range(3)
+    )
+    return (
+        jnp.swapaxes(layer_out, 1, 2),
+        jnp.swapaxes(input_grad, 1, 2),
+        g_feature[0],
+        g_feature[1],
+        g_q.T,
+        small_grads[:width],
+        g_k.T,
+        g_v.T,
+        small_grads[width : 2 * width],
+        g_o,
+        g_feature[2],
+        g_feature[3],
+        g_feature[4],
+        out_fc1.T,
+        small_grads[2 * width :],
+        g_fc2,
+        g_feature[5],
+    )
+
+
 def solution(mesh):
     in_specs = (
         P("dp", None, "tensor"),
@@ -338,6 +1376,7 @@
         P("tensor", None),
         P("tensor"),
     )
+    whole_images = mesh.shape["tensor"] == 2 and mesh.shape["dp"] == 16
     return jax.shard_map(
-        per_device, mesh=mesh, in_specs=in_specs, out_specs=out_specs, check_vma=False
-    )
+        whole_device if whole_images else split_device, mesh=mesh, in_specs=in_specs, out_specs=out_specs, check_vma=False
+    )

time: 2170 us -> 961 us (0.44)
  matrix products: 698 us -> 0 us
  Pallas kernels: 0 us -> 568 us
  waiting for transfers between devices: 765 us -> 256 us
  local copies, waits for them, and re-layouts: 323 us -> 39.3 us
  other arithmetic: 257 us -> 36.8 us
  blocking collectives: 95 us -> 0 us
  starting transfers between devices: 0.87 us -> 37.1 us
    dot_general x48 -> x0, matrix products: 698 us -> none  [the longest x12 158 us: right_transposed(): lax.dot_general(left, right, (((1,), (1,)), ((), ())), preferred_element_...]
    pallas_call x0 -> x28, Pallas kernels: none -> 568 us  [the longest x4 145 us: hidden_stage(): pl.pallas_call(functools.partial(hidden_kernel, which=which), out_shape=[...]
    all_gather x8 -> x2, waiting for transfers between devices: 325 us -> 0.02 us  [the longest x1 0.02 us: whole_device(): mlp_other = lax.all_gather(mlp_piece, 'dp', axis=0, tiled=True)]
    reduce_scatter x8 -> x0, waiting for transfers between devices: 247 us -> none  [the longest x2 118 us: per_device(): lax.psum_scatter(rounded(partial_first).astype(jnp.bfloat16), 'tensor', s...]
    convert_element_type x31 -> x0, local copies, waits for them, and re-layouts: 171 us -> none  [the longest x4 27 us: per_device(): grad_query = (jnp.einsum('nhqk,nkhd->nqhd', grad_scores, keys4, preferred...]
    convert_element_type x43 -> x7, other arithmetic: 150 us -> 23.1 us  [the longest x1 4.86 us: whole_device(): g_fc1 = (both(fc1_k, fc1_o) + fc1_arrived.astype(F32)).astype(BF16)]
    ppermute x0 -> x31, waiting for transfers between devices: none -> 121 us  [the longest x16 112 us: swap_tensor(): return lax.ppermute(value, 'tensor', [(0, 1), (1, 0)])]
    reduce_sum x10 -> x0, other arithmetic: 95.7 us -> none  [the longest x2 42.3 us: per_device(): log_total = jax.nn.logsumexp(scores, axis=-1)]
  transfers between devices with their start and end apart: 17 -> 36, of which waited for: 14 -> 16; matrix products, arithmetic and copies ran while one was open for 34% -> 6% of each run, Pallas kernels for 0% -> 52%
where the time goes in v1:
time: 961 us; the launch traced here: 951 us
  Pallas kernels  568 us (59%)
  waiting for transfers between devices  256 us (27%)
  local copies, waits for them, and re-layouts  39.3 us (4%)
  starting transfers between devices  37.1 us (4%)
  other arithmetic  36.8 us (4%)
  between operations  14.6 us (2%)
    pallas_call x4, Pallas kernels, hidden_stage(): pl.pallas_call(functools.partial(hidden_kernel, which=which), out_shape=[...  145 us
    ppermute x16, waiting for transfers between devices, swap_tensor(): return lax.ppermute(value, 'tensor', [(0, 1), (1, 0)])  112 us
    pallas_call x3, Pallas kernels, mix_back(): pl.pallas_call(functools.partial(mix_back_kernel, scale=1.0 / math.sqrt(h...  79.7 us
    psum x1, waiting for transfers between devices, whole_device(): g_qkv = lax.psum(g_qkv, 'dp', axis_index_groups=chip_groups(2))  64.8 us
    pallas_call x4, Pallas kernels, mix(): pl.pallas_call(functools.partial(mix_kernel, scale=1.0 / math.sqrt(head_d...  58.3 us
    pallas_call x1, Pallas kernels, resid_back(): pl.pallas_call(resid_back_kernel, grid=(count,), out_shape=[jax.ShapeDtyp...  45.7 us
    psum x1, waiting for transfers between devices, whole_device(): g_late = lax.psum(g_late, 'dp', axis_index_groups=chip_groups(1))  39.7 us
    pallas_call x1, Pallas kernels, input_back(): pl.pallas_call(input_back_kernel, out_shape=[jax.ShapeDtypeStruct((2 * co...  39 us
  transfers between devices with their start and end apart: 36, of which 16 were waited for; matrix products, arithmetic and copies ran while one was open for 6% of the time, Pallas kernels for 52%

profile of v1, /device:TPU:0, one launch (start us, length us, event | category | flops | bytes accessed | tf_op | source)
XLA Modules:
  0.0 951.1 jit_solution(12908319638658274928)
XLA Ops:
  7.3 6.2 concatenate.36
  13.6 3.0 collective-permute-start.3
  21.9 17.1 %collective-permute-done.other_ref = bf16[1,576,729]{2,1,0:T(8,128)(2,1)S(1)} collective-permute-done((bf16[1,576,729]{2,1,0:T(8,128)(2,1)S(1)}, bf16[1,576,729]{2,1,0:T(8,128)(2,1)S(1)}, u32[]{:S(2)}, u32[]{:S(2)}) %collective-permute-start) | collective-permute-done | bytes 839840 | tf_op jit(solution)/shard_map/ppermute | solution.py:1062
  40.9 10.0 %first_norm.3 = (bf16[3,1152,729]{2,1,0:T(8,128)(2,1)}, bf16[3,1152,729]{2,1,0:T(8,128)(2,1)}, bf16[3,24,72,729]{3,2,1,0:T(8,128)(2,1)}) custom-call(s32[8]{0:T(128)} %pad_add_fusion.place_ref, bf16[6,576,729]{2,1,0:T(8,128)(2,1)} %bitcast.37, bf16[1,576,729]{2,1,0:T(8,128)(2,1)} %copy-done.11, f32[1152,8]{1,0:T(8,128)} %convert_bitcast_fusion.feature_ref.gain_ref.b_ref, ...), custom_call_target="tpu_custom_call" | custom-call | flops 58047528 | bytes 251658 | tf_op jit(solution)/shard_map/first_norm/pallas_call | solution.py:417
  52.9 1.8 collective-permute-start.1
  56.1 10.2 %mix.4 = (bf16[3,16,72,729]{3,2,1,0:T(8,128)(2,1)}, f32[3,16,1,729]{3,2,1,0:T(1,128)}) custom-call(bf16[3,24,72,729]{3,2,1,0:T(8,128)(2,1)} %get-tuple-element.127.q_ref.k_ref.v_ref.rest_2_, bf16[3,24,72,729]{3,2,1,0:T(8,128)(2,1)} %get-tuple-element.127.q_ref.k_ref.v_ref.rest_2_, bf16[3,24,72,729]{3,2,1,0:T(8,128)(2,1)} %get-tuple-element.127.q_ref.k_ref.v_ref.rest_2_), custom_call_target="tpu_custom_call" | custom-call | flops 87071296 | bytes 67184 | tf_op jit(solution)/shard_map/mix/pallas_call | solution.py:502
  66.4 6.9 collective-permute-done.1.other_ref
  74.6 10.1 %first_norm.4 = (bf16[3,1152,729]{2,1,0:T(8,128)(2,1)}, bf16[3,1152,729]{2,1,0:T(8,128)(2,1)}, bf16[3,24,72,729]{3,2,1,0:T(8,128)(2,1)}) custom-call(s32[8]{0:T(128)} %pad_add_fusion.place_ref, bf16[6,576,729]{2,1,0:T(8,128)(2,1)} %bitcast.39, bf16[1,576,729]{2,1,0:T(8,128)(2,1)} %copy-done.9, ...), custom_call_target="tpu_custom_call", output_to_operand_aliasing={{0}: (8, {}), {1}: (9, {}), {2}: (10, {})} | custom-call | flops 58047528 | bytes 251658 | tf_op jit(solution)/shard_map/first_norm/pallas_call | solution.py:417
  84.8 2.4 collective-permute-done.5
  88.0 10.9 %all-reduce.8.cloned.1.call-start = ((), (), s32[]{:S(2)}) async-start(), calls=%async_computation.2 | async-start | bytes 5013504 | tf_op jit(solution)/shard_map/psum | solution.py:1226
  98.9 2.3 constant_dynamic-slice_fusion.5
  102.3 10.3 %mix.5 = (bf16[3,16,72,729]{3,2,1,0:T(8,128)(2,1)}, f32[3,16,1,729]{3,2,1,0:T(1,128)}) custom-call(bf16[3,24,72,729]{3,2,1,0:T(8,128)(2,1)} %get-tuple-element.135.q_ref.k_ref.v_ref.rest_2_, bf16[3,24,72,729]{3,2,1,0:T(8,128)(2,1)} %get-tuple-element.135.q_ref.k_ref.v_ref.rest_2_, ...), custom_call_target="tpu_custom_call", output_to_operand_aliasing={{0}: (3, {}), {1}: (4, {})} | custom-call | flops 87071296 | bytes 67184 | tf_op jit(solution)/shard_map/mix/pallas_call | solution.py:502
  112.6 7.4 collective-permute-done.4.other_ref
  125.9 10.1 %first_norm.5 = (bf16[3,1152,729]{2,1,0:T(8,128)(2,1)}, bf16[3,1152,729]{2,1,0:T(8,128)(2,1)}, bf16[3,24,72,729]{3,2,1,0:T(8,128)(2,1)}) custom-call(s32[8]{0:T(128)} %pad_add_fusion.place_ref, bf16[6,576,729]{2,1,0:T(8,128)(2,1)} %bitcast.41, bf16[1,576,729]{2,1,0:T(8,128)(2,1)} %copy-done.10, ...), custom_call_target="tpu_custom_call", output_to_operand_aliasing={{0}: (8, {}), {1}: (9, {}), {2}: (10, {})} | custom-call | flops 58047528 | bytes 251658 | tf_op jit(solution)/shard_map/first_norm/pallas_call | solution.py:417
  136.0 10.2 %mix.6 = (bf16[3,16,72,729]{3,2,1,0:T(8,128)(2,1)}, f32[3,16,1,729]{3,2,1,0:T(1,128)}) custom-call(bf16[3,24,72,729]{3,2,1,0:T(8,128)(2,1)} %get-tuple-element.143.q_ref.k_ref.v_ref, bf16[3,24,72,729]{3,2,1,0:T(8,128)(2,1)} %get-tuple-element.143.q_ref.k_ref.v_ref, ...), custom_call_target="tpu_custom_call", output_to_operand_aliasing={{0}: (3, {}), {1}: (4, {})} | custom-call | flops 87071296 | bytes 67184 | tf_op jit(solution)/shard_map/mix/pallas_call | solution.py:502
  146.2 17.4 %collective-permute-done.8 = bf16[1,576,729]{2,1,0:T(8,128)(2,1)S(1)} collective-permute-done((bf16[1,576,729]{2,1,0:T(8,128)(2,1)}, bf16[1,576,729]{2,1,0:T(8,128)(2,1)S(1)}, u32[]{:S(2)}, u32[]{:S(2)}) %collective-permute-start.8) | collective-permute-done | bytes 839840 | tf_op jit(solution)/shard_map/ppermute | solution.py:1062
  163.5 14.0 %collective-permute-done.7 = bf16[1,576,729]{2,1,0:T(8,128)(2,1)S(1)} collective-permute-done((bf16[1,576,729]{2,1,0:T(8,128)(2,1)}, bf16[1,576,729]{2,1,0:T(8,128)(2,1)S(1)}, u32[]{:S(2)}, u32[]{:S(2)}) %collective-permute-start.7) | collective-permute-done | bytes 839840 | tf_op jit(solution)/shard_map/ppermute | solution.py:1062
  177.6 1.8 pad_maximum_fusion.1.cot_other_ref
  179.4 15.0 %project.1.q_ref.k_ref.v_ref = bf16[3,24,72,729]{3,2,1,0:T(8,128)(2,1)} custom-call(bf16[3,1152,729]{2,1,0:T(8,128)(2,1)} %get-tuple-element.142.normed_ref, bf16[2304,1152]{1,0:T(8,128)(2,1)} %all-gather.3.cloned.1.call-done.q_ref.k_ref.v_ref.w_other_ref, bf16[2304,1152]{1,0:T(8,128)(2,1)} %all-gather.3.cloned.1.call-done.q_ref.k_ref.v_ref.w_other_ref, ...), custom_call_target="tpu_custom_call" | custom-call | flops 174142592 | bytes 419430 | tf_op jit(solution)/shard_map/project/pallas_call | solution.py:461
  194.4 27.6 %mix.7 = (bf16[3,16,72,729]{3,2,1,0:T(8,128)(2,1)}, f32[3,16,1,729]{3,2,1,0:T(1,128)}) custom-call(bf16[3,24,72,729]{3,2,1,0:T(8,128)(2,1)} %project.1.q_ref.k_ref.v_ref, bf16[3,24,72,729]{3,2,1,0:T(8,128)(2,1)} %project.1.q_ref.k_ref.v_ref, bf16[3,24,72,729]{3,2,1,0:T(8,128)(2,1)} %project.1.q_ref.k_ref.v_ref, ...), custom_call_target="tpu_custom_call", output_to_operand_aliasing={{0}: (3, {}), {1}: (4, {})} | custom-call | flops 261213888 | bytes 201553 | tf_op jit(solution)/shard_map/mix/pallas_call | solution.py:502
  222.0 22.2 %second_norm.1 = (f32[3,1152,729]{2,1,0:T(8,128)}, bf16[3,1152,729]{2,1,0:T(8,128)(2,1)}, bf16[3,1152,729]{2,1,0:T(8,128)(2,1)}, f32[1,1152]{1,0:T(1,128)}) custom-call(s32[8]{0:T(128)} %pad_add_fusion.place_ref, bf16[3,1152,729]{2,1,0:T(8,128)(2,1)} %bitcast.27, bf16[576,1152]{1,0:T(8,128)(2,1)} %w_own_ref.4, ...), custom_call_target="tpu_custom_call" | custom-call | flops 116095056 | bytes 838860 | tf_op jit(solution)/shard_map/second_norm/pallas_call | solution.py:623
  244.2 36.3 %hidden_stage.4 = (bf16[3,2152,729]{2,1,0:T(8,128)(2,1)}, bf16[3,2152,729]{2,1,0:T(8,128)(2,1)}, f32[2152,1]{1,0:T(8,128)}, bf16[1088,1152]{1,0:T(8,128)(2,1)}, bf16[1088,1152]{1,0:T(8,128)(2,1)}) custom-call(s32[8]{0:T(128)} %pad_add_fusion.place_ref, bf16[3,1152,729]{2,1,0:T(8,128)(2,1)} %get-tuple-element.153.low_ref, ...), custom_call_target="tpu_custom_call" | custom-call | flops 433744032 | bytes 629145 | tf_op jit(solution)/shard_map/hidden_stage/pallas_call | solution.py:693
  281.0 36.1 %hidden_stage.5 = (bf16[3,2152,729]{2,1,0:T(8,128)(2,1)}, bf16[3,2152,729]{2,1,0:T(8,128)(2,1)}, f32[2152,1]{1,0:T(8,128)}, bf16[1088,1152]{1,0:T(8,128)(2,1)}, bf16[1088,1152]{1,0:T(8,128)(2,1)}) custom-call(s32[8]{0:T(128)} %pad_add_fusion.place_ref, ...), custom_call_target="tpu_custom_call", output_to_operand_aliasing={{0}: (6, {}), {1}: (7, {}), {2}: (8, {})} | custom-call | flops 433744032 | bytes 629145 | tf_op jit(solution)/shard_map/hidden_stage/pallas_call | solution.py:693
  318.6 3.2 add_convert_fusion.4
  321.9 2.2 add_convert_fusion.3
  324.0 36.3 %hidden_stage.6 = (bf16[3,2152,729]{2,1,0:T(8,128)(2,1)}, bf16[3,2152,729]{2,1,0:T(8,128)(2,1)}, f32[2152,1]{1,0:T(8,128)}, bf16[1088,1152]{1,0:T(8,128)(2,1)}, bf16[1088,1152]{1,0:T(8,128)(2,1)}) custom-call(s32[8]{0:T(128)} %pad_add_fusion.place_ref, bf16[3,1152,729]{2,1,0:T(8,128)(2,1)} %get-tuple-element.153.low_ref, ...), custom_call_target="tpu_custom_call" | custom-call | flops 433744032 | bytes 629145 | tf_op jit(solution)/shard_map/hidden_stage/pallas_call | solution.py:693
  360.8 1.7 collective-permute-start.14
  362.6 36.1 %hidden_stage.7 = (bf16[3,2152,729]{2,1,0:T(8,128)(2,1)}, bf16[3,2152,729]{2,1,0:T(8,128)(2,1)}, f32[2152,1]{1,0:T(8,128)}, bf16[1088,1152]{1,0:T(8,128)(2,1)}, bf16[1088,1152]{1,0:T(8,128)(2,1)}) custom-call(s32[8]{0:T(128)} %pad_add_fusion.place_ref, ...), custom_call_target="tpu_custom_call", output_to_operand_aliasing={{0}: (6, {}), {1}: (7, {}), {2}: (8, {})} | custom-call | flops 433744032 | bytes 629145 | tf_op jit(solution)/shard_map/hidden_stage/pallas_call | solution.py:693
  400.1 3.2 add_convert_fusion.1
  403.4 14.3 %collective-permute-done.12 = bf16[1088,1152]{1,0:T(8,128)(2,1)} collective-permute-done((bf16[1088,1152]{1,0:T(8,128)(2,1)S(1)}, bf16[1088,1152]{1,0:T(8,128)(2,1)}, u32[]{:S(2)}, u32[]{:S(2)}) %collective-permute-start.12) | collective-permute-done | bytes 2506784 | tf_op jit(solution)/shard_map/ppermute | solution.py:1062
  417.7 4.9 add_convert_fusion.2
  422.6 45.7 %resid_back.1 = (bf16[3,1152,729]{2,1,0:T(8,128)(2,1)}, f32[1,1152]{1,0:T(1,128)}, f32[1,1152]{1,0:T(1,128)}, f32[1,1152]{1,0:T(1,128)}) custom-call(bf16[3,2152,729]{2,1,0:T(8,128)(2,1)} %get-tuple-element.175.back_own_ref, bf16[3,2152,729]{2,1,0:T(8,128)(2,1)} %get-tuple-element.176.back_other_ref, bf16[2152,1152]{1,0:T(8,128)(2,1)} %bitcast.34, ...), custom_call_target="tpu_custom_call" | custom-call | flops 433744032 | bytes 1048576 | tf_op jit(solution)/shard_map/resid_back/pallas_call | solution.py:818
  468.3 21.7 %context_back.1 = (bf16[3,1152,729]{2,1,0:T(8,128)(2,1)}, bf16[288,1152]{1,0:T(8,128)(2,1)}, bf16[288,1152]{1,0:T(8,128)(2,1)}, bf16[288,1152]{1,0:T(8,128)(2,1)}, bf16[288,1152]{1,0:T(8,128)(2,1)}) custom-call(s32[8]{0:T(128)} %pad_add_fusion.place_ref, bf16[3,1152,729]{2,1,0:T(8,128)(2,1)} %get-tuple-element.178.low_ref, bf16[3,1152,729]{2,1,0:T(8,128)(2,1)} %bitcast.28, ...), custom_call_target="tpu_custom_call" | custom-call | flops 232190112 | bytes 524288 | tf_op jit(solution)/shard_map/context_back/pallas_call | solution.py:884
  490.6 38.3 %mix_back.3 = bf16[3,24,72,729]{3,2,1,0:T(8,128)(2,1)} custom-call(bf16[3,24,72,729]{3,2,1,0:T(8,128)(2,1)} %project.1.q_ref.k_ref.v_ref, bf16[3,24,72,729]{3,2,1,0:T(8,128)(2,1)} %project.1.q_ref.k_ref.v_ref, bf16[3,24,72,729]{3,2,1,0:T(8,128)(2,1)} %project.1.q_ref.k_ref.v_ref, bf16[3,16,72,729]{3,2,1,0:T(8,128)(2,1)} %get-tuple-element.149.out_ref, ...), custom_call_target="tpu_custom_call" | custom-call | flops 653034688 | bytes 403107 | tf_op jit(solution)/shard_map/mix_back/pallas_call | solution.py:553
  528.8 2.1 add_convert_fusion.8
  531.4 19.2 %project_back.2 = (bf16[864,1152]{1,0:T(8,128)(2,1)}, bf16[864,1152]{1,0:T(8,128)(2,1)}, f32[1728,1]{1,0:T(8,128)}) custom-call(s32[8]{0:T(128)} %pad_add_fusion.place_ref, bf16[3,1152,729]{2,1,0:T(8,128)(2,1)} %get-tuple-element.142.normed_ref, bf16[3,1728,729]{2,1,0:T(8,128)(2,1)} %bitcast.35), custom_call_target="tpu_custom_call" | custom-call | flops 174142592 | bytes 419430 | tf_op jit(solution)/shard_map/project_back/pallas_call | solution.py:937
  550.6 2.4 add_convert_fusion
  553.1 1.9 pad_maximum_fusion
  555.0 14.8 %mix_back.4.rest_0_ = bf16[3,24,72,729]{3,2,1,0:T(8,128)(2,1)} custom-call(bf16[3,24,72,729]{3,2,1,0:T(8,128)(2,1)} %get-tuple-element.143.q_ref.k_ref.v_ref, bf16[3,24,72,729]{3,2,1,0:T(8,128)(2,1)} %get-tuple-element.143.q_ref.k_ref.v_ref, bf16[3,24,72,729]{3,2,1,0:T(8,128)(2,1)} %get-tuple-element.143.q_ref.k_ref.v_ref, ...), custom_call_target="tpu_custom_call" | custom-call | flops 217678240 | bytes 134369 | tf_op jit(solution)/shard_map/mix_back/pallas_call | solution.py:553
  569.9 3.3 add_convert_fusion.6
  573.2 30.1 %all-reduce.8.cloned.1.call-done.mine_ref = bf16[1088,1152]{1,0:T(8,128)(2,1)} async-done(((bf16[1088,1152]{1,0:T(8,128)(2,1)}), bf16[1088,1152]{1,0:T(8,128)(2,1)}) %all-reduce.8.cloned.1.call-update) | async-done | bytes 2506768 | tf_op jit(solution)/shard_map/psum | solution.py:1226
  603.4 26.6 %mix_back.5 = bf16[3,24,72,729]{3,2,1,0:T(8,128)(2,1)} custom-call(bf16[3,24,72,729]{3,2,1,0:T(8,128)(2,1)} %get-tuple-element.143.q_ref.k_ref.v_ref, bf16[3,24,72,729]{3,2,1,0:T(8,128)(2,1)} %get-tuple-element.143.q_ref.k_ref.v_ref, bf16[3,24,72,729]{3,2,1,0:T(8,128)(2,1)} %get-tuple-element.143.q_ref.k_ref.v_ref, ...), custom_call_target="tpu_custom_call", output_to_operand_aliasing={{}: (6, {})} | custom-call | flops 435356480 | bytes 268738 | tf_op jit(solution)/shard_map/mix_back/pallas_call | solution.py:553
  629.9 19.1 %project_back.3 = (bf16[864,1152]{1,0:T(8,128)(2,1)}, bf16[864,1152]{1,0:T(8,128)(2,1)}, f32[1728,1]{1,0:T(8,128)}) custom-call(s32[8]{0:T(128)} %pad_add_fusion.place_ref, bf16[3,1152,729]{2,1,0:T(8,128)(2,1)} %get-tuple-element.142.normed_ref, bf16[3,1728,729]{2,1,0:T(8,128)(2,1)} %bitcast.29), custom_call_target="tpu_custom_call" | custom-call | flops 174142592 | bytes 419430 | tf_op jit(solution)/shard_map/project_back/pallas_call | solution.py:937
  652.6 11.3 %widen.6 = f32[2152,1152]{1,0:T(8,128)} custom-call(s32[8]{0:T(128)} %pad_add_fusion.place_ref, bf16[1088,1152]{1,0:T(8,128)(2,1)} %all-reduce.8.cloned.1.call-done.mine_ref, bf16[1088,1152]{1,0:T(8,128)(2,1)} %copy-done.2), custom_call_target="tpu_custom_call" | custom-call | bytes 396656 | tf_op jit(solution)/shard_map/widen/pallas_call | solution.py:1046
  663.9 31.3 %collective-permute-done.21 = bf16[864,1152]{1,0:T(8,128)(2,1)} collective-permute-done((bf16[864,1152]{1,0:T(8,128)(2,1)}, bf16[864,1152]{1,0:T(8,128)(2,1)}, u32[]{:S(2)}, u32[]{:S(2)}) %collective-permute-start.21) | collective-permute-done | bytes 1990688 | tf_op jit(solution)/shard_map/ppermute | solution.py:1062
  695.1 4.1 add_convert_fusion.5
  699.3 39.0 %input_back.1 = (bf16[6,576,729]{2,1,0:T(8,128)(2,1)}, bf16[3,576,729]{2,1,0:T(8,128)(2,1)}, f32[1,1152]{1,0:T(1,128)}, f32[1,1152]{1,0:T(1,128)}) custom-call(s32[8]{0:T(128)} %pad_add_fusion.place_ref, bf16[3,1728,729]{2,1,0:T(8,128)(2,1)} %bitcast.30, bf16[3,1728,729]{2,1,0:T(8,128)(2,1)} %bitcast.36, bf16[576,1152]{1,0:T(8,128)(2,1)} %bitcast.52, ...), custom_call_target="tpu_custom_call" | custom-call | flops 348285184 | bytes 838860 | tf_op jit(solution)/shard_map/input_back/pallas_call | solution.py:1005
  739.8 39.7 %all-reduce.12.cloned.1.call-done.mine_ref = bf16[1376,1152]{1,0:T(8,128)(2,1)} async-done(((bf16[1376,1152]{1,0:T(8,128)(2,1)}), bf16[1376,1152]{1,0:T(8,128)(2,1)}) %all-reduce.12.cloned.1.call-update) | async-done | bytes 3170320 | tf_op jit(solution)/shard_map/psum | solution.py:1245
  779.5 36.2 %layer_result.1 = (bf16[6,576,729]{2,1,0:T(8,128)(2,1)}, bf16[3,576,729]{2,1,0:T(8,128)(2,1)}) custom-call(s32[8]{0:T(128)} %pad_add_fusion.place_ref, bf16[3,2152,729]{2,1,0:T(8,128)(2,1)} %get-tuple-element.210.act_own_ref, bf16[3,2152,729]{2,1,0:T(8,128)(2,1)} %get-tuple-element.211.act_other_ref, bf16[2152,1152]{1,0:T(8,128)(2,1)} %w_own_ref.5, ...), custom_call_target="tpu_custom_call" | custom-call | flops 433744032 | bytes 943718 | tf_op jit(solution)/shard_map/layer_result/pallas_call | solution.py:746
  817.0 64.8 %all-reduce.10.cloned.1.call-done.mine_ref = bf16[864,1152]{1,0:T(8,128)(2,1)} async-done(((bf16[864,1152]{1,0:T(8,128)(2,1)}), bf16[864,1152]{1,0:T(8,128)(2,1)}) %all-reduce.10.cloned.1.call-update) | async-done | bytes 1990672 | tf_op jit(solution)/shard_map/psum | solution.py:1261
  889.8 2.8 collective-permute-done.25
  894.1 2.7 collective-permute-done.26
  896.9 2.2 collective-permute-start.27
  899.1 3.0 collective-permute-done.27
  903.6 2.0 slice.101.mine_ref
  907.8 2.0 slice.102.other_ref
  909.8 3.6 widen.10
  913.4 10.5 %widen.11 = f32[2152,1152]{1,0:T(8,128)} custom-call(s32[8]{0:T(128)} %pad_add_fusion.place_ref, bf16[1376,1152]{1,0:T(8,128)(2,1)} %all-reduce.12.cloned.1.call-done.mine_ref, bf16[1376,1152]{1,0:T(8,128)(2,1)} %collective-permute-done.30.other_ref), custom_call_target="tpu_custom_call" | custom-call | bytes 396656 | tf_op jit(solution)/shard_map/widen/pallas_call | solution.py:1046
  923.9 3.4 constant_dynamic-update-slice_fusion.2
  928.6 3.7 widen.9
  932.3 4.1 widen.8
  936.4 3.6 widen.7
  940.0 2.1 constant_dynamic-update-slice_fusion.3
  942.1 2.4 copy-done.31
  (182 shorter events, 45.9 us)
Async XLA Ops:
  7.2 12.8 %copy-start.23 = (bf16[576]{0:T(1024)(128)(2,1)S(1)}, bf16[576]{0:T(1024)(128)(2,1)}, u32[]{:S(2)}) copy-start(bf16[576]{0:T(1024)(128)(2,1)} %param.35) | copy-start | bytes 3460
  7.2 12.8 %copy-start.22 = (bf16[576]{0:T(1024)(128)(2,1)S(1)}, bf16[576]{0:T(1024)(128)(2,1)}, u32[]{:S(2)}) copy-start(bf16[576]{0:T(1024)(128)(2,1)} %param.31) | copy-start | bytes 3460
  7.2 12.8 %copy-start.21 = (bf16[576]{0:T(1024)(128)(2,1)S(1)}, bf16[576]{0:T(1024)(128)(2,1)}, u32[]{:S(2)}) copy-start(bf16[576]{0:T(1024)(128)(2,1)} %param.30) | copy-start | bytes 3460
  7.2 12.8 %copy-start.20 = (bf16[576]{0:T(1024)(128)(2,1)S(1)}, bf16[576]{0:T(1024)(128)(2,1)}, u32[]{:S(2)}) copy-start(bf16[576]{0:T(1024)(128)(2,1)} %param.29) | copy-start | bytes 3460
  7.2 12.8 %copy-start.19 = (bf16[576]{0:T(1024)(128)(2,1)S(1)}, bf16[576]{0:T(1024)(128)(2,1)}, u32[]{:S(2)}) copy-start(bf16[576]{0:T(1024)(128)(2,1)} %param.22) | copy-start | bytes 3460
  7.2 12.8 %copy-start.18 = (bf16[576]{0:T(1024)(128)(2,1)S(1)}, bf16[576]{0:T(1024)(128)(2,1)}, u32[]{:S(2)}) copy-start(bf16[576]{0:T(1024)(128)(2,1)} %param.21) | copy-start | bytes 3460
  7.3 12.1 %copy-start.30 = (s32[6]{0:T(128)S(1)}, s32[6]{0:T(128)}, u32[]{:S(2)}) copy-start(s32[6]{0:T(128)} %param.19) | copy-start | bytes 76
  7.3 172.2 %all-gather.3.cloned.1.call-start = ((), (), s32[]{:S(2)}) async-start(), calls=%async_computation | async-start | bytes 5640192 | tf_op jit(solution)/shard_map/all_gather | solution.py:1185
  13.6 6.7 collective-permute-start.3
  17.8 21.2 %collective-permute-start = (bf16[1,576,729]{2,1,0:T(8,128)(2,1)S(1)}, bf16[1,576,729]{2,1,0:T(8,128)(2,1)S(1)}, u32[]{:S(2)}, u32[]{:S(2)}) collective-permute-start(bf16[1,576,729]{2,1,0:T(8,128)(2,1)S(1)} %dynamic-slice_bitcast_fusion), channel_id=1, source_target_pairs={{0,1},{1,0},{2,3},{3,2},{4,5},{5,4},{6,7},{7,6},{8,9},{9,8},{10,11... | collective-permute-start | bytes 2519432 | tf_op jit(solution)/shard_map/ppermute | solution.py:1062
  38.9 1.9 copy-start.11
  38.9 12.0 %collective-permute-start.2 = (bf16[144,1152]{1,0:T(8,128)(2,1)S(1)}, bf16[144,1152]{1,0:T(8,128)(2,1)S(1)}, u32[]{:S(2)}, u32[]{:S(2)}) collective-permute-start(bf16[144,1152]{1,0:T(8,128)(2,1)S(1)} %bitcast_select_fusion), channel_id=1, source_target_pairs={{0,1},{1,0},{2,3},{3,2},{4,5},{5,4},{6,7},{7,6},{8,9},{9,8},{10,11... | collective-permute-start | bytes 995336 | tf_op jit(solution)/shard_map/ppermute | solution.py:1062
  51.6 192.6 %all-gather.5.cloned.1.call-start = ((), (), s32[]{:S(2)}) async-start(), calls=%async_computation.1 | async-start | bytes 10653696 | tf_op jit(solution)/shard_map/all_gather | solution.py:1189
  52.9 20.3 %collective-permute-start.1 = (bf16[1,576,729]{2,1,0:T(8,128)(2,1)S(1)}, bf16[1,576,729]{2,1,0:T(8,128)(2,1)S(1)}, u32[]{:S(2)}, u32[]{:S(2)}) collective-permute-start(bf16[1,576,729]{2,1,0:T(8,128)(2,1)S(1)} %constant_dynamic-slice_fusion.6), channel_id=1, source_target_pairs={{0,1},{1,0},{2,3},{3,2},{4,5},{5,4},{6,7},{7,6},{8,9},{9,8},{10,11... | collective-permute-start | bytes 2519432 | tf_op jit(solution)/shard_map/ppermute | solution.py:1062
  73.2 13.9 %collective-permute-start.5 = (bf16[272,1152]{1,0:T(8,128)(2,1)S(1)}, bf16[272,1152]{1,0:T(8,128)(2,1)S(1)}, u32[]{:S(2)}, u32[]{:S(2)}) collective-permute-start(bf16[272,1152]{1,0:T(8,128)(2,1)S(1)} %fusion), channel_id=1, source_target_pairs={{0,1},{1,0},{2,3},{3,2},{4,5},{5,4},{6,7},{7,6},{8,9},{9,8},{10,11... | collective-permute-start | bytes 1880072 | tf_op jit(solution)/shard_map/ppermute | solution.py:1062
  88.0 515.4 %all-reduce.8.cloned.1.call-start = ((), (), s32[]{:S(2)}) async-start(), calls=%async_computation.2 | async-start | bytes 5013504 | tf_op jit(solution)/shard_map/psum | solution.py:1226
  98.9 21.1 %slice-start = ((s8[5308416]{0:T(1024)(128)(4,1)}), s8[4194304]{0:T(1024)(128)(4,1)S(1)}, s32[]{:S(2)}) async-start(s8[5308416]{0:T(1024)(128)(4,1)} %bitcast.62), calls=%async_computation.5 | async-start | bytes 8388608
  101.2 18.8 %collective-permute-start.4 = (bf16[1,576,729]{2,1,0:T(8,128)(2,1)}, bf16[1,576,729]{2,1,0:T(8,128)(2,1)S(1)}, u32[]{:S(2)}, u32[]{:S(2)}) collective-permute-start(bf16[1,576,729]{2,1,0:T(8,128)(2,1)} %constant_dynamic-slice_fusion.5), channel_id=1, source_target_pairs={{0,1},{1,0},{2,3},{3,2},{4,5},{5,4},{6,7},{7,6},{8,9},{9,8},{10,11... | collective-permute-start | bytes 2519432 | tf_op jit(solution)/shard_map/ppermute | solution.py:1062
  102.3 17.7 %slice-start.1 = ((s8[5308416]{0:T(1024)(128)(4,1)}), s8[1114112]{0:T(1024)(128)(4,1)S(1)}, s32[]{:S(2)}) async-start(s8[5308416]{0:T(1024)(128)(4,1)} %bitcast.62), calls=%async_computation.6 | async-start | bytes 2228224
  120.0 1.8 copy-start.10
  120.0 4.5 copy-start.17
  121.8 24.4 %collective-permute-start.6 = (bf16[1,576,729]{2,1,0:T(8,128)(2,1)}, bf16[1,576,729]{2,1,0:T(8,128)(2,1)S(1)}, u32[]{:S(2)}, u32[]{:S(2)}) collective-permute-start(bf16[1,576,729]{2,1,0:T(8,128)(2,1)} %get-tuple-element.243), channel_id=1, source_target_pairs={{0,1},{1,0},{2,3},{3,2},{4,5},{5,4},{6,7},{7,6},{8,9},{9,8},{10,11... | collective-permute-start | bytes 2519432 | tf_op jit(solution)/shard_map/ppermute | solution.py:1062
  122.5 41.1 %collective-permute-start.8 = (bf16[1,576,729]{2,1,0:T(8,128)(2,1)}, bf16[1,576,729]{2,1,0:T(8,128)(2,1)S(1)}, u32[]{:S(2)}, u32[]{:S(2)}) collective-permute-start(bf16[1,576,729]{2,1,0:T(8,128)(2,1)} %get-tuple-element.244), channel_id=1, source_target_pairs={{0,1},{1,0},{2,3},{3,2},{4,5},{5,4},{6,7},{7,6},{8,9},{9,8},{10,11... | collective-permute-start | bytes 2519432 | tf_op jit(solution)/shard_map/ppermute | solution.py:1062
  123.8 53.8 %collective-permute-start.7 = (bf16[1,576,729]{2,1,0:T(8,128)(2,1)}, bf16[1,576,729]{2,1,0:T(8,128)(2,1)S(1)}, u32[]{:S(2)}, u32[]{:S(2)}) collective-permute-start(bf16[1,576,729]{2,1,0:T(8,128)(2,1)} %get-tuple-element.245), channel_id=1, source_target_pairs={{0,1},{1,0},{2,3},{3,2},{4,5},{5,4},{6,7},{7,6},{8,9},{9,8},{10,11... | collective-permute-start | bytes 2519432 | tf_op jit(solution)/shard_map/ppermute | solution.py:1062
  280.5 36.6 %collective-permute-start.9 = (bf16[1088,1152]{1,0:T(8,128)(2,1)}, bf16[1088,1152]{1,0:T(8,128)(2,1)S(1)}, u32[]{:S(2)}, u32[]{:S(2)}) collective-permute-start(bf16[1088,1152]{1,0:T(8,128)(2,1)} %get-tuple-element.160), channel_id=1, source_target_pairs={{0,2},{2,0},{4,6},{6,4},{8,10},{10,8},{12,14},{14,12},{16,18},{18,... | collective-permute-start | bytes 7520264 | tf_op jit(solution)/shard_map/ppermute | solution.py:1066
  280.5 41.3 %collective-permute-start.10 = (bf16[1088,1152]{1,0:T(8,128)(2,1)}, bf16[1088,1152]{1,0:T(8,128)(2,1)S(1)}, u32[]{:S(2)}, u32[]{:S(2)}) collective-permute-start(bf16[1088,1152]{1,0:T(8,128)(2,1)} %get-tuple-element.162), channel_id=1, source_target_pairs={{0,2},{2,0},{4,6},{6,4},{8,10},{10,8},{12,14},{14,12},{16,18},{18,... | collective-permute-start | bytes 7520264 | tf_op jit(solution)/shard_map/ppermute | solution.py:1066
  318.6 3.2 copy-start.5
  360.3 38.4 %collective-permute-start.13 = (bf16[1088,1152]{1,0:T(8,128)(2,1)}, bf16[1088,1152]{1,0:T(8,128)(2,1)S(1)}, u32[]{:S(2)}, u32[]{:S(2)}) collective-permute-start(bf16[1088,1152]{1,0:T(8,128)(2,1)} %get-tuple-element.173), channel_id=1, source_target_pairs={{0,2},{2,0},{4,6},{6,4},{8,10},{10,8},{12,14},{14,12},{16,18},{18,... | collective-permute-start | bytes 7520264 | tf_op jit(solution)/shard_map/ppermute | solution.py:1066
  360.4 57.3 %collective-permute-start.12 = (bf16[1088,1152]{1,0:T(8,128)(2,1)S(1)}, bf16[1088,1152]{1,0:T(8,128)(2,1)}, u32[]{:S(2)}, u32[]{:S(2)}) collective-permute-start(bf16[1088,1152]{1,0:T(8,128)(2,1)S(1)} %add_convert_fusion.4), channel_id=1, source_target_pairs={{0,1},{1,0},{2,3},{3,2},{4,5},{5,4},{6,7},{7,6},{8,9},{9,8},{10,11... | collective-permute-start | bytes 7520264 | tf_op jit(solution)/shard_map/ppermute | solution.py:1062
  360.7 57.0 %collective-permute-start.11 = (bf16[1088,1152]{1,0:T(8,128)(2,1)}, bf16[1088,1152]{1,0:T(8,128)(2,1)}, u32[]{:S(2)}, u32[]{:S(2)}) collective-permute-start(bf16[1088,1152]{1,0:T(8,128)(2,1)} %get-tuple-element.170), channel_id=1, source_target_pairs={{0,2},{2,0},{4,6},{6,4},{8,10},{10,8},{12,14},{14,12},{16,18},{18,... | collective-permute-start | bytes 7520264 | tf_op jit(solution)/shard_map/ppermute | solution.py:1066
  360.8 129.7 %collective-permute-start.14 = (bf16[1088,1152]{1,0:T(8,128)(2,1)}, bf16[1088,1152]{1,0:T(8,128)(2,1)}, u32[]{:S(2)}, u32[]{:S(2)}) collective-permute-start(bf16[1088,1152]{1,0:T(8,128)(2,1)} %add_convert_fusion.3), channel_id=1, source_target_pairs={{0,1},{1,0},{2,3},{3,2},{4,5},{5,4},{6,7},{7,6},{8,9},{9,8},{10,11... | collective-permute-start | bytes 7520264 | tf_op jit(solution)/shard_map/ppermute | solution.py:1062
  400.1 17.6 %copy-start.4 = (bf16[1088,1152]{1,0:T(8,128)(2,1)S(1)}, bf16[1088,1152]{1,0:T(8,128)(2,1)}, u32[]{:S(2)}) copy-start(bf16[1088,1152]{1,0:T(8,128)(2,1)} %get-tuple-element.169) | copy-start | bytes 7520260
  489.9 38.9 %collective-permute-start.15 = (bf16[288,1152]{1,0:T(8,128)(2,1)}, bf16[288,1152]{1,0:T(8,128)(2,1)}, u32[]{:S(2)}, u32[]{:S(2)}) collective-permute-start(bf16[288,1152]{1,0:T(8,128)(2,1)} %get-tuple-element.186), channel_id=1, source_target_pairs={{0,2},{2,0},{4,6},{6,4},{8,10},{10,8},{12,14},{14,12},{16,18},{18,... | collective-permute-start | bytes 1990664 | tf_op jit(solution)/shard_map/ppermute | solution.py:1066
  490.0 41.0 %collective-permute-start.16 = (bf16[288,1152]{1,0:T(8,128)(2,1)}, bf16[288,1152]{1,0:T(8,128)(2,1)S(1)}, u32[]{:S(2)}, u32[]{:S(2)}) collective-permute-start(bf16[288,1152]{1,0:T(8,128)(2,1)} %get-tuple-element.188), channel_id=1, source_target_pairs={{0,2},{2,0},{4,6},{6,4},{8,10},{10,8},{12,14},{14,12},{16,18},{18,... | collective-permute-start | bytes 1990664 | tf_op jit(solution)/shard_map/ppermute | solution.py:1066
  490.5 289.0 %all-reduce.12.cloned.1.call-start = ((), (), s32[]{:S(2)}) async-start(), calls=%async_computation.4 | async-start | bytes 6340608 | tf_op jit(solution)/shard_map/psum | solution.py:1245
  490.5 38.3 %copy-start.13 = (bf16[288,1152]{1,0:T(8,128)(2,1)S(1)}, bf16[288,1152]{1,0:T(8,128)(2,1)}, u32[]{:S(2)}) copy-start(bf16[288,1152]{1,0:T(8,128)(2,1)} %get-tuple-element.185) | copy-start | bytes 1990660
  490.6 40.4 %copy-start.12 = (bf16[288,1152]{1,0:T(8,128)(2,1)S(1)}, bf16[288,1152]{1,0:T(8,128)(2,1)}, u32[]{:S(2)}) copy-start(bf16[288,1152]{1,0:T(8,128)(2,1)} %get-tuple-element.187) | copy-start | bytes 1990660
  531.1 21.9 %collective-permute-start.17 = (bf16[288,1152]{1,0:T(8,128)(2,1)}, bf16[288,1152]{1,0:T(8,128)(2,1)S(1)}, u32[]{:S(2)}, u32[]{:S(2)}) collective-permute-start(bf16[288,1152]{1,0:T(8,128)(2,1)} %add_convert_fusion.8), channel_id=1, source_target_pairs={{0,1},{1,0},{2,3},{3,2},{4,5},{5,4},{6,7},{7,6},{8,9},{9,8},{10,11... | collective-permute-start | bytes 1990664 | tf_op jit(solution)/shard_map/ppermute | solution.py:1062
  550.6 19.3 %collective-permute-start.18 = (bf16[864,1152]{1,0:T(8,128)(2,1)}, bf16[864,1152]{1,0:T(8,128)(2,1)}, u32[]{:S(2)}, u32[]{:S(2)}) collective-permute-start(bf16[864,1152]{1,0:T(8,128)(2,1)} %get-tuple-element.196), channel_id=1, source_target_pairs={{0,2},{2,0},{4,6},{6,4},{8,10},{10,8},{12,14},{14,12},{16,18},{18,... | collective-permute-start | bytes 5971976 | tf_op jit(solution)/shard_map/ppermute | solution.py:1066
  555.0 14.9 %copy-start.7 = (bf16[864,1152]{1,0:T(8,128)(2,1)S(1)}, bf16[864,1152]{1,0:T(8,128)(2,1)}, u32[]{:S(2)}) copy-start(bf16[864,1152]{1,0:T(8,128)(2,1)} %get-tuple-element.195) | copy-start | bytes 5971972
  603.4 47.7 %collective-permute-start.19 = (bf16[1088,1152]{1,0:T(8,128)(2,1)}, bf16[1088,1152]{1,0:T(8,128)(2,1)S(1)}, u32[]{:S(2)}, u32[]{:S(2)}) collective-permute-start(bf16[1088,1152]{1,0:T(8,128)(2,1)} %all-reduce.8.cloned.1.call-done.mine_ref), channel_id=1, source_target_pairs={{0,2},{2,0},{4,6},{6,4},{8,10},{10,8},{12,14},{14,12},{16,18},{18,... | collective-permute-start | bytes 7520264 | tf_op jit(solution)/shard_map/ppermute | solution.py:1066
  649.1 14.8 %collective-permute-start.20 = (bf16[864,1152]{1,0:T(8,128)(2,1)}, bf16[864,1152]{1,0:T(8,128)(2,1)}, u32[]{:S(2)}, u32[]{:S(2)}) collective-permute-start(bf16[864,1152]{1,0:T(8,128)(2,1)} %get-tuple-element.202), channel_id=1, source_target_pairs={{0,2},{2,0},{4,6},{6,4},{8,10},{10,8},{12,14},{14,12},{16,18},{18,... | collective-permute-start | bytes 5971976 | tf_op jit(solution)/shard_map/ppermute | solution.py:1066
  649.5 45.6 %collective-permute-start.21 = (bf16[864,1152]{1,0:T(8,128)(2,1)}, bf16[864,1152]{1,0:T(8,128)(2,1)}, u32[]{:S(2)}, u32[]{:S(2)}) collective-permute-start(bf16[864,1152]{1,0:T(8,128)(2,1)} %add_convert_fusion.6), channel_id=1, source_target_pairs={{0,1},{1,0},{2,3},{3,2},{4,5},{5,4},{6,7},{7,6},{8,9},{9,8},{10,11... | collective-permute-start | bytes 5971976 | tf_op jit(solution)/shard_map/ppermute | solution.py:1062
  651.0 230.7 %all-reduce.10.cloned.1.call-start = ((), (), s32[]{:S(2)}) async-start(), calls=%async_computation.3 | async-start | bytes 3981312 | tf_op jit(solution)/shard_map/psum | solution.py:1261
  652.6 42.6 %copy-start.8 = (bf16[864,1152]{1,0:T(8,128)(2,1)S(1)}, bf16[864,1152]{1,0:T(8,128)(2,1)}, u32[]{:S(2)}) copy-start(bf16[864,1152]{1,0:T(8,128)(2,1)} %get-tuple-element.201) | copy-start | bytes 5971972
  738.3 77.5 %collective-permute-start.22 = (bf16[3,576,729]{2,1,0:T(8,128)(2,1)}, bf16[3,576,729]{2,1,0:T(8,128)(2,1)}, u32[]{:S(2)}, u32[]{:S(2)}) collective-permute-start(bf16[3,576,729]{2,1,0:T(8,128)(2,1)} %get-tuple-element.213), channel_id=1, source_target_pairs={{0,1},{1,0},{2,3},{3,2},{4,5},{5,4},{6,7},{7,6},{8,9},{9,8},{10,11... | collective-permute-start | bytes 7558280 | tf_op jit(solution)/shard_map/ppermute | solution.py:1062
  779.5 128.4 %collective-permute-start.30 = (bf16[1376,1152]{1,0:T(8,128)(2,1)}, bf16[1376,1152]{1,0:T(8,128)(2,1)}, u32[]{:S(2)}, u32[]{:S(2)}) collective-permute-start(bf16[1376,1152]{1,0:T(8,128)(2,1)} %all-reduce.12.cloned.1.call-done.mine_ref), channel_id=1, source_target_pairs={{0,2},{2,0},{4,6},{6,4},{8,10},{10,8},{12,14},{14,12},{16,18},{18,... | collective-permute-start | bytes 9510920 | tf_op jit(solution)/shard_map/ppermute | solution.py:1066
  779.5 103.9 %copy-start.1 = (f32[2152,1]{1,0:T(8,128)S(1)}, f32[2152,1]{1,0:T(8,128)}, u32[]{:S(2)}) copy-start(f32[2152,1]{1,0:T(8,128)} %get-tuple-element.225) | copy-start | bytes 25828
  815.7 71.0 %copy-start.24 = (f32[1,1152]{1,0:T(1,128)S(1)}, f32[1,1152]{1,0:T(1,128)}, u32[]{:S(2)}) copy-start(f32[1,1152]{1,0:T(1,128)} %get-tuple-element.223) | copy-start | bytes 13828
  815.7 71.0 %copy-start.25 = (f32[1,1152]{1,0:T(1,128)S(1)}, f32[1,1152]{1,0:T(1,128)}, u32[]{:S(2)}) copy-start(f32[1,1152]{1,0:T(1,128)} %get-tuple-element.221) | copy-start | bytes 13828
  815.7 71.1 %copy-start.26 = (f32[1,1152]{1,0:T(1,128)S(1)}, f32[1,1152]{1,0:T(1,128)}, u32[]{:S(2)}) copy-start(f32[1,1152]{1,0:T(1,128)} %get-tuple-element.222) | copy-start | bytes 13828
  815.7 71.1 %copy-start.27 = (f32[1,1152]{1,0:T(1,128)S(1)}, f32[1,1152]{1,0:T(1,128)}, u32[]{:S(2)}) copy-start(f32[1,1152]{1,0:T(1,128)} %get-tuple-element.220) | copy-start | bytes 13828
  815.7 71.1 %copy-start.28 = (f32[1,1152]{1,0:T(1,128)S(1)}, f32[1,1152]{1,0:T(1,128)}, u32[]{:S(2)}) copy-start(f32[1,1152]{1,0:T(1,128)} %get-tuple-element.218) | copy-start | bytes 13828
  815.7 71.1 %copy-start.29 = (f32[1,1152]{1,0:T(1,128)S(1)}, f32[1,1152]{1,0:T(1,128)}, u32[]{:S(2)}) copy-start(f32[1,1152]{1,0:T(1,128)} %get-tuple-element.219) | copy-start | bytes 13828
  815.7 124.2 %collective-permute-start.23 = (bf16[3,576,729]{2,1,0:T(8,128)(2,1)}, bf16[3,576,729]{2,1,0:T(8,128)(2,1)}, u32[]{:S(2)}, u32[]{:S(2)}) collective-permute-start(bf16[3,576,729]{2,1,0:T(8,128)(2,1)} %get-tuple-element.215), channel_id=1, source_target_pairs={{0,1},{1,0},{2,3},{3,2},{4,5},{5,4},{6,7},{7,6},{8,9},{9,8},{10,11... | collective-permute-start | bytes 7558280 | tf_op jit(solution)/shard_map/ppermute | solution.py:1062
  881.8 45.5 %collective-permute-start.29 = (bf16[864,1152]{1,0:T(8,128)(2,1)}, bf16[864,1152]{1,0:T(8,128)(2,1)S(1)}, u32[]{:S(2)}, u32[]{:S(2)}) collective-permute-start(bf16[864,1152]{1,0:T(8,128)(2,1)} %all-reduce.10.cloned.1.call-done.mine_ref), channel_id=1, source_target_pairs={{0,2},{2,0},{4,6},{6,4},{8,10},{10,8},{12,14},{14,12},{16,18},{18,... | collective-permute-start | bytes 5971976 | tf_op jit(solution)/shard_map/ppermute | solution.py:1066
  886.9 1.5 collective-permute-start.24
  888.3 4.3 collective-permute-start.25
  892.6 4.2 collective-permute-start.26
  896.9 5.1 collective-permute-start.27
  902.0 4.2 collective-permute-start.28
  928.6 11.4 %slice-start.2 = ((s8[5308416]{0:T(1024)(128)(4,1)}), s8[1114112]{0:T(1024)(128)(4,1)S(1)}, s32[]{:S(2)}) async-start(s8[5308416]{0:T(1024)(128)(4,1)} %bitcast.70), calls=%async_computation.7 | async-start | bytes 2228224
  932.3 7.7 slice-start.3
  942.0 2.4 copy-start.31
  (8 other events, 9.2 us)
Sparse Core Ops, SparseCore 0:
  51.8 57.8 all-gather.2
  112.4 83.6 all-gather.4
  490.6 112.7 all-reduce.7
  651.2 128.2 all-reduce.11
  783.5 98.2 all-reduce.9

commit v2 on v1

--- a/solution.py
+++ b/solution.py
@@ -305,7 +305,9 @@
 BF16 = jnp.bfloat16
 LOG2E = math.log2(math.e)
 VMEM_BYTES = 58 * 1024 * 1024
-COST_SHARE = 0.02
+COST_SHARE = 0.4
+LONG = 4.0
+SHORT = 0.05
 
 
 def dot_nn(left, right):
@@ -320,11 +322,11 @@
     return lax.dot_general(left, right, (((0,), (0,)), ((), ())), preferred_element_type=F32)
 
 
-def cost(flops, moved, trans=0):
+def cost(flops, moved, trans=0, share=COST_SHARE):
     return pl.CostEstimate(
-        flops=int(flops * COST_SHARE),
-        bytes_accessed=int(moved * COST_SHARE),
-        transcendentals=int(trans * COST_SHARE),
+        flops=int(flops * share),
+        bytes_accessed=int(moved * share),
+        transcendentals=int(trans * share),
     )
 
 
@@ -570,6 +572,7 @@
             10 * steps * heads * seq * seq * 256,
             steps * heads * head_dim * seq * 16,
             steps * heads * seq * seq,
+            SHORT if steps == 1 else COST_SHARE,
         ),
         name="mix_back",
     )(qkv, qkv, qkv, out, log_total, grad, *held)
@@ -583,14 +586,9 @@
     rows_ref,
     feature_ref,
     cot_own_ref,
-    cot_other_ref,
-    resid_ref,
-    low_ref,
-    grad_ref,
-    row_ref,
-    w_ref,
-    sum_ref,
+    *rest,
 ):
+    *cot_refs, resid_ref, low_ref, grad_ref, row_ref, w_ref, sum_ref = rest
     step = pl.program_id(0)
     half = w_own_ref.shape[0]
 
@@ -608,8 +606,11 @@
         normed * column(feature_ref, LN2_GAIN) + column(feature_ref, LN2_BIAS)
     ).astype(BF16)
     flag = place_ref[2 + place_ref[0] * pl.num_programs(0) + step].astype(F32)
+    cot_other = cot_refs[0][0]
+    for index in range(1, len(cot_refs)):
+        cot_other = jnp.where(step == index, cot_refs[index][0], cot_other)
     grad = flag * join_halves(
-        place_ref[0] == 0, cot_own_ref[0].astype(F32), cot_other_ref[0].astype(F32)
+        place_ref[0] == 0, cot_own_ref[0].astype(F32), cot_other.astype(F32)
     )
     grad_ref[0] = grad.astype(BF16)
     sum_ref[...] += token_sum(grad)
@@ -638,15 +639,15 @@
                 full,
                 once((feat, 8)),
                 pl.BlockSpec((1, feat // 2, seq), lambda i, p: (p[0] * count + i, 0, 0)),
-                image_block((feat // 2, seq)),
-            ],
+            ]
+            + [once((1, feat // 2, seq))] * count,
             out_specs=[full, full, full, once((1, feat))],
             scratch_shapes=[pltpu.VMEM((feat, feat), BF16), pltpu.VMEM((feat, 1), F32)],
         ),
         compiler_params=params(1),
         cost_estimate=cost(4 * count * seq * half * feat, 40 << 20),
         name="second_norm",
-    )(place, ctx, w_own, w_other, rows, features, cot, cot_other)
+    )(place, ctx, w_own, w_other, rows, features, cot, *cot_other)
 
 
 def hidden_kernel(place_ref, low_ref, grad_ref, fc1_ref, fc2_ref, bias_ref, *rest, which):
@@ -720,55 +721,59 @@
         ),
         input_output_aliases={6 + k: k for k in range(len(held))},
         compiler_params=params(1),
-        cost_estimate=cost(4 * count * seq * feat * hidden, 30 << 20, count * seq * hidden // 2),
+        cost_estimate=cost(4 * count * seq * feat * hidden, 30 << 20, 0, LONG),
         name="hidden_stage",
     )(place, low, grad, fc1, fc2, bias, *held)
 
 
 def layer_kernel(
-    place_ref, act_own_ref, act_other_ref, w_own_ref, w_other_ref, resid_ref, b_ref, out_ref, send_ref
+    place_ref, act_own_ref, act_other_ref, w_own_ref, w_other_ref, resid_ref, b_ref, *rest, start, count
 ):
+    out_ref, send_ref = rest[-2:]
     hidden = act_own_ref.shape[1]
     branch = dot_tn(w_own_ref[:hidden], act_own_ref[0])
     branch += dot_tn(w_other_ref[:hidden], act_other_ref[0])
-    flag = place_ref[2 + place_ref[0] * pl.num_programs(0) + pl.program_id(0)].astype(F32)
+    flag = place_ref[2 + place_ref[0] * count + start + pl.program_id(0)].astype(F32)
     result = (resid_ref[0] + branch + column(b_ref, FC2_BIAS)) * flag
     own, other = split_halves(place_ref[0] == 0, result)
     out_ref[0] = own.astype(BF16)
     send_ref[0] = other.astype(BF16)
 
 
-def layer_result(place, act_own, act_other, w_own, w_other, resid, bias):
+def layer_result(place, act_own, act_other, w_own, w_other, resid, features, start, steps, held):
     count, feat, seq = resid.shape
     hidden = act_own.shape[1]
-    full = image_block((hidden, seq))
+    full = image_block((hidden, seq), start)
     padded = 4 * quarter_rows(hidden)
+    held = [] if held is None else [held]
     return pl.pallas_call(
-        layer_kernel,
+        functools.partial(layer_kernel, start=start, count=count),
         out_shape=[
             jax.ShapeDtypeStruct((2 * count, feat // 2, seq), BF16),
-            jax.ShapeDtypeStruct((count, feat // 2, seq), BF16),
+            jax.ShapeDtypeStruct((steps, feat // 2, seq), BF16),
         ],
         grid_spec=pltpu.PrefetchScalarGridSpec(
             num_scalar_prefetch=1,
-            grid=(count,),
+            grid=(steps,),
             in_specs=[
                 full,
                 full,
                 once((hidden, feat)),
                 once((padded, feat), (1, 0)),
-                image_block((feat, seq)),
+                image_block((feat, seq), start),
                 once((feat, 8)),
-            ],
+            ]
+            + [ANYWHERE] * len(held),
             out_specs=[
-                pl.BlockSpec((1, feat // 2, seq), lambda i, p: (p[0] * count + i, 0, 0)),
+                pl.BlockSpec((1, feat // 2, seq), lambda i, p: (p[0] * count + start + i, 0, 0)),
                 image_block((feat // 2, seq)),
             ],
         ),
+        input_output_aliases={7: 0} if held else {},
         compiler_params=params(1),
-        cost_estimate=cost(4 * count * seq * feat * hidden, 45 << 20),
+        cost_estimate=cost(4 * steps * seq * feat * hidden, steps * (12 << 20), 0, LONG),
         name="layer_result",
-    )(place, act_own, act_other, w_own, w_other, resid, bias)
+    )(place, act_own, act_other, w_own, w_other, resid, features, *held)
 
 
 def resid_back_kernel(
@@ -965,14 +970,9 @@
     rows_ref,
     low_ref,
     gain_ref,
-    out_ref,
-    send_ref,
-    row_gain_ref,
-    row_bias_ref,
-    w_ref,
-    sum_gain_ref,
-    sum_bias_ref,
+    *rest,
 ):
+    out_ref, send_ref, row_gain_ref, row_bias_ref, w_ref, sum_gain_ref, sum_bias_ref = rest[-7:]
     width = q_ref.shape[0]
 
     @pl.when(pl.program_id(0) == 0)
@@ -997,27 +997,29 @@
     write_rows((row_gain_ref, row_bias_ref), (sum_gain_ref, sum_bias_ref))
 
 
-def input_back(place, d_own, d_other, weights, w_other, rows, low, gain):
+def input_back(place, d_own, d_other, weights, w_other, rows, low, features, start, steps, held):
     count, width, seq = d_own.shape
     feat = rows.shape[1]
-    wide = image_block((width, seq))
-    full = image_block((feat, seq))
+    wide = image_block((width, seq), start)
+    full = image_block((feat, seq), start)
+    held = [] if held is None else [held]
     return pl.pallas_call(
         input_back_kernel,
         out_shape=[
             jax.ShapeDtypeStruct((2 * count, feat // 2, seq), BF16),
-            jax.ShapeDtypeStruct((count, feat // 2, seq), BF16),
+            jax.ShapeDtypeStruct((steps, feat // 2, seq), BF16),
             jax.ShapeDtypeStruct((1, feat), F32),
             jax.ShapeDtypeStruct((1, feat), F32),
         ],
         grid_spec=pltpu.PrefetchScalarGridSpec(
             num_scalar_prefetch=1,
-            grid=(count,),
+            grid=(steps,),
             in_specs=[wide, wide]
             + [once((width // 3, feat))] * 3
-            + [once((width, feat)), full, full, once((feat, 8))],
+            + [once((width, feat)), full, full, once((feat, 8))]
+            + [ANYWHERE] * len(held),
             out_specs=[
-                pl.BlockSpec((1, feat // 2, seq), lambda i, p: (p[0] * count + i, 0, 0)),
+                pl.BlockSpec((1, feat // 2, seq), lambda i, p: (p[0] * count + start + i, 0, 0)),
                 image_block((feat // 2, seq)),
                 once((1, feat)),
                 once((1, feat)),
@@ -1028,34 +1030,57 @@
                 pltpu.VMEM((feat, 1), F32),
             ],
         ),
+        input_output_aliases={10: 0} if held else {},
         compiler_params=params(1),
-        cost_estimate=cost(4 * count * seq * feat * width, 40 << 20),
+        cost_estimate=cost(4 * steps * seq * feat * width, steps * (11 << 20) + (8 << 20), 0, LONG),
         name="input_back",
-    )(place, d_own, d_other, *weights, w_other, rows, low, gain)
-
-
-def widen_kernel(place_ref, mine_ref, other_ref, out_ref):
-    mine = pl.program_id(0) == place_ref[1]
-    out_ref[...] = jnp.where(mine, mine_ref[...], other_ref[...]).astype(F32)
-
-
-def widen(place, mine, other, offset, part, total, steps):
+    )(place, d_own, d_other, *weights, w_other, rows, low, features, *held)
+
+
+def widen_kernel(place_ref, mine_ref, other_ref, *out_refs, steps):
+    half, step = pl.program_id(1), pl.program_id(2)
+    mine = half == place_ref[1]
+    value = jnp.where(mine, mine_ref[...], other_ref[...]).astype(F32)
+    for index, out_ref in enumerate(out_refs):
+
+        @pl.when(pl.program_id(0) == index)
+        def _():
+            out_ref[...] = value
+
+
+def widen(place, mine, other, part, total, steps, count=1):
     feat = mine.shape[1]
     rows = part // steps
-    spec = pl.BlockSpec((rows, feat), lambda h, i, p: (offset // rows + i, 0))
-    return pl.pallas_call(
-        widen_kernel,
-        out_shape=jax.ShapeDtypeStruct((total, feat), F32),
+    last = 2 * steps - 1
+
+    def mine_spot(w, h, i, p):
+        used = 1 - (h - p[1]) * (h - p[1])
+        return (w * steps + i * used, 0)
+
+    def other_spot(w, h, i, p):
+        used = (h - p[1]) * (h - p[1])
+        return (w * steps + i * used, 0)
+
+    def out_spot(index):
+        return lambda w, h, i, p: (jnp.clip((w - index) * 2 * steps + h * steps + i, 0, last), 0)
+
+    out = pl.pallas_call(
+        functools.partial(widen_kernel, steps=steps),
+        out_shape=[jax.ShapeDtypeStruct((total, feat), F32)] * count,
         grid_spec=pltpu.PrefetchScalarGridSpec(
             num_scalar_prefetch=1,
-            grid=(2, steps),
-            in_specs=[spec, spec],
-            out_specs=pl.BlockSpec((rows, feat), lambda h, i, p: (h * steps + i, 0)),
+            grid=(count, 2, steps),
+            in_specs=[
+                pl.BlockSpec((rows, feat), mine_spot),
+                pl.BlockSpec((rows, feat), other_spot),
+            ],
+            out_specs=[pl.BlockSpec((rows, feat), out_spot(index)) for index in range(count)],
         ),
-        compiler_params=params(2),
-        cost_estimate=cost(0, 8 * total * feat),
+        compiler_params=params(3),
+        cost_estimate=cost(0, 8 * total * feat * count, 0, SHORT),
         name="widen",
     )(place, mine, other)
+    return out if count > 1 else out[0]
 
 
 def swap_tensor(value):
@@ -1064,6 +1089,14 @@
 
 def swap_core(value):
     return lax.ppermute(value, "dp", [(spot, spot ^ 1) for spot in range(lax.axis_size("dp"))])
+
+
+def exchange_sum(value, steps):
+    total = value
+    for step in steps:
+        pairs = [(spot, spot ^ step) for spot in range(lax.axis_size("dp"))]
+        total += lax.ppermute(value, "dp", pairs)
+    return total
 
 
 def other_weights(weights, spots, rows):
@@ -1083,9 +1116,31 @@
 def chip_groups(order):
     spots = lax.axis_size("dp")
     groups = [list(range(core, spots, 2)) for core in range(2)]
-    if order == 1:
-        return groups[::-1]
-    return [group[::-1] for group in groups] if order == 2 else groups
+    return groups[::-1] if order else groups
+
+
+def swap_step(value, step):
+    return lax.ppermute(value, "dp", [(spot, spot ^ step) for spot in range(lax.axis_size("dp"))])
+
+
+def side(step):
+    return lax.axis_index("dp") // step % 2
+
+
+def halves(value, step):
+    rows = value.shape[0] // 2
+    mine = side(step)
+    keep = lax.dynamic_slice_in_dim(value, mine * rows, rows, 0)
+    return keep, lax.dynamic_slice_in_dim(value, (1 - mine) * rows, rows, 0)
+
+
+def ranked(mine, other, step):
+    first = side(step) == 0
+    return jnp.concatenate([jnp.where(first, mine, other), jnp.where(first, other, mine)])
+
+
+def added(left, right):
+    return (left.astype(F32) + right.astype(F32)).astype(BF16)
 
 
 def both(keep, send):
@@ -1132,10 +1187,8 @@
     in_weights = [q_weight.T, k_weight.T, v_weight.T]
     fc1_own = fc1_weight.T
 
-    def to_other(array, index):
-        return swap_tensor(
-            lax.dynamic_slice_in_dim(array, (1 - tensor) * count + index, 1, 0)
-        )
+    def to_send(array, index, images=1):
+        return lax.dynamic_slice_in_dim(array, (1 - tensor) * count + index, images, 0)
 
     small = jnp.concatenate(
         [ln1_gain, ln1_bias, o_bias, ln2_gain, ln2_bias, fc2_bias, q_bias, v_bias, fc1_bias]
@@ -1143,12 +1196,18 @@
     cut_q, cut_v, cut_h = 6 * half, 6 * half + width, 6 * half + 2 * width
     block = quarter_rows(hidden)
 
-    images_other = [to_other(images, 0)]
-    small_other = swap_tensor(small)
     in_piece = other_weights([*in_weights, o_weight], spots, width // (spots // 4))
-    in_piece = swap_tensor(after(in_piece, images_other[0]))
-    images_other.append(to_other(after(images, images_other[0]), 1))
+    first, in_piece = lax.optimization_barrier((to_send(images, 0), in_piece))
+    in_piece = swap_tensor(in_piece)
+    images_other = [swap_tensor(first)]
+    small_other = swap_tensor(after(small, first))
     mlp_piece = other_weights([fc1_own, fc2_weight], spots, block // 2)
+    next_image = to_send(images, 1)
+    next_image, mlp_piece, images_other[0] = lax.optimization_barrier(
+        (next_image, mlp_piece, images_other[0])
+    )
+    images_other.append(swap_tensor(next_image))
+    mlp_piece = swap_tensor(mlp_piece)
 
     def features_of(source):
         return source[:cut_q].reshape(6, half)
@@ -1180,27 +1239,28 @@
         )
         state = list(state)
         if index == 0:
-            in_piece, held = lax.optimization_barrier((in_piece, state[2]))
-            state[2] = held
+            in_piece, state[2] = lax.optimization_barrier((in_piece, state[2]))
             in_other = lax.all_gather(in_piece, "dp", axis=0, tiled=True)
         if index == 1:
-            mlp_piece, held = lax.optimization_barrier((mlp_piece, state[2]))
-            state[2] = held
+            mlp_piece, state[2] = lax.optimization_barrier((mlp_piece, state[2]))
             mlp_other = lax.all_gather(mlp_piece, "dp", axis=0, tiled=True)
         mixed = list(mix(state[2], 0, index, 1, mixed))
-        if index + 2 == len(images_other) and len(images_other) < count:
-            turn = lax.optimization_barrier((images, images_other[-1], mixed[0]))
-            images_other[-1], mixed[0] = turn[1:]
-            images_other.append(to_other(turn[0], index + 2))
-            if index == 0:
-                mlp_piece = swap_tensor(after(mlp_piece, turn[1]))
-        elif len(images_other) == count and index + 2 == count:
-            turn = lax.optimization_barrier((cotangent, images_other[-1], mixed[0]))
-            images_other[-1], mixed[0] = turn[1:]
-            cot_other = jnp.concatenate([to_other(turn[0], spot) for spot in range(count)])
+        if index + 2 < count:
+            next_image = to_send(images, index + 2)
+            next_image, images_other[-1], mixed[0] = lax.optimization_barrier(
+                (next_image, images_other[-1], mixed[0])
+            )
+            images_other.append(swap_tensor(next_image))
+        elif index + 2 == count:
+            late = [to_send(cotangent, spot) for spot in range(count)]
+            images_other[-1], mixed[0], *late = lax.optimization_barrier(
+                (images_other[-1], mixed[0], *late)
+            )
+            cot_other = [swap_tensor(value) for value in late]
     rows, normed, qkv_own = state
     qkv_other = project(normed, in_other, head_vectors, width)
     ctx, logs = mix(qkv_other, 1, 0, count, mixed)
+    ctx, *cot_other = lax.optimization_barrier((ctx, *cot_other))
     flat = (count, 2 * width, seq)
     resid, low_second, grad_out, sum_fc2b = second_norm(
         place, ctx.reshape(flat), o_weight, in_other, rows, features, cotangent, cot_other
@@ -1213,67 +1273,98 @@
 
     *held, fc1_o, fc2_o = stage(False, place, (mlp_other, mlp_other), 4, 1, None)
     *stage_other, fc1_k, fc2_k = stage(True, place, (mlp_other, mlp_other), 4, 1, held)
-    fc1_send, fc2_send = both(fc1_k, fc1_o).astype(BF16), both(fc2_k, fc2_o).astype(BF16)
-    place2, fc1_send, fc2_send = lax.optimization_barrier((place, fc1_send, fc2_send))
-    fc1_arrived = swap_tensor(fc1_send)
+    rows_a = 4 * block // 3 // 8 * 8
+    rows_b = 2 * block - rows_a
+    fc1_r, fc2_r = swap_core(fc1_o), swap_core(fc2_o)
+
+    def summed(keep, arrived, low, high):
+        return (keep[low:high].astype(F32) + arrived[low:high].astype(F32)).astype(BF16)
+
+    piece = summed(fc1_k, fc1_r, 0, rows_a)
+    later = (
+        summed(fc1_k, fc1_r, rows_a, 2 * block),
+        summed(fc2_k, fc2_r, 0, rows_a - rows_b),
+        summed(fc2_k, fc2_r, rows_a - rows_b, 2 * block),
+    )
+    place2, piece, *later = lax.optimization_barrier((place, piece, *later))
+    fc1_arrived = [swap_tensor(piece)]
     *held, fc1_o, fc2_o = stage(False, place2, (fc1_own, fc2_weight), 0, 0, None)
-    fc2_send, held[2] = lax.optimization_barrier((fc2_send, held[2]))
-    fc2_arrived = swap_tensor(fc2_send)
+    held[2], fc1_arrived[0], *later = lax.optimization_barrier((held[2], fc1_arrived[0], *later))
+    fc1_arrived.append(swap_tensor(later[0]))
+    fc2_arrived = [swap_tensor(later[1])]
     *stage_own, fc1_k, fc2_k = stage(True, place2, (fc1_own, fc2_weight), 0, 0, held)
-    g_fc1 = (both(fc1_k, fc1_o) + fc1_arrived.astype(F32)).astype(BF16)
-    fc2_pair = both(fc2_k, fc2_o).astype(BF16)
-    g_fc1, fc2_pair, back_own = lax.optimization_barrier((g_fc1, fc2_pair, stage_own[1]))
+    back_own = stage_own[1]
+    back_own, fc1_arrived[1], fc2_arrived[0], last = lax.optimization_barrier(
+        (back_own, fc1_arrived[1], fc2_arrived[0], later[2])
+    )
+    g_fc1 = (both(fc1_k, fc1_o) + jnp.concatenate(fc1_arrived).astype(F32)).astype(BF16)
+    fc2_r = swap_core(fc2_o)
+    g_fc1, fc2_r, back_own = lax.optimization_barrier((g_fc1, fc2_r, back_own))
+    fc2_arrived.append(swap_tensor(last))
     g_fc1 = lax.psum(g_fc1, "dp", axis_index_groups=chip_groups(0))
     low_resid, sum_gain2, sum_bias2, sum_ob = resid_back(
         back_own, stage_other[1], fc1_own, mlp_other, resid, grad_out, features
     )
+    low_resid, fc2_arrived[1] = lax.optimization_barrier((low_resid, fc2_arrived[1]))
+    g_late = fc2_k.astype(F32) + fc2_r.astype(F32) + jnp.concatenate(fc2_arrived).astype(F32)
+    g_late = g_late.astype(BF16)
+    x_keep, x_send = halves(g_late, 2)
+    low_resid, x_keep, x_send = lax.optimization_barrier((low_resid, x_keep, x_send))
     d_ctx, *o_parts = context_back(place, low_resid, ctx.reshape(flat), o_weight, in_other)
-    d_ctx, fc2_arrived, fc2_pair = lax.optimization_barrier(
-        (d_ctx.reshape(ctx.shape), fc2_arrived, fc2_pair)
-    )
+    d_ctx = d_ctx.reshape(ctx.shape)
+    d_ctx, x_send = lax.optimization_barrier((d_ctx, x_send))
+    x_recv = swap_step(x_send, 2)
     wide = (count, 3 * width, seq)
     d_other = mix_back(qkv_other, ctx, logs, d_ctx, 1, 0, count, None).reshape(wide)
     o_send = both(o_parts[2], o_parts[3]).astype(BF16)
     o_pair = both(o_parts[0], o_parts[1])
-    d_other, o_send, o_pair = lax.optimization_barrier((d_other, o_send, o_pair))
+    d_other, x_recv = lax.optimization_barrier((d_other, x_recv))
+    z_keep, z_send = halves(added(x_keep, x_recv), 4)
+    d_other, o_send, o_pair, z_keep, z_send = lax.optimization_barrier(
+        (d_other, o_send, o_pair, z_keep, z_send)
+    )
+    z_recv = swap_step(z_send, 4)
     o_arrived = swap_tensor(o_send)
     other_keep, other_send, column_other = project_back(place, normed, d_other)
-    o_arrived, other_keep = lax.optimization_barrier((o_arrived, other_keep))
-    g_fc2 = fc2_pair.astype(F32) + fc2_arrived.astype(F32)
-    g_late = jnp.concatenate([g_fc2, o_pair + o_arrived.astype(F32)]).astype(BF16)
-    d_ctx, g_late = lax.optimization_barrier((d_ctx, g_late))
-    g_late = lax.psum(g_late, "dp", axis_index_groups=chip_groups(1))
+    o_arrived, other_keep, g_fc1, z_recv = lax.optimization_barrier(
+        (o_arrived, other_keep, g_fc1, z_recv)
+    )
+    far_keep, far_send = halves(added(z_keep, z_recv), 8)
+    g_o = (o_pair + o_arrived.astype(F32)).astype(BF16)
+    d_ctx, g_o, far_keep, far_send = lax.optimization_barrier((d_ctx, g_o, far_keep, far_send))
+    far_recv = swap_step(far_send, 8)
+    fc1_other = swap_core(g_fc1)
 
     d_own = mix_back(qkv_own, ctx, logs, d_ctx, 0, 0, 1, None)
-    qkv_send = both(other_keep, other_send).astype(BF16)
-    d_own, qkv_send, g_fc1 = lax.optimization_barrier((d_own, qkv_send, g_fc1))
-    qkv_arrived = swap_tensor(qkv_send)
-    fc1_other = swap_core(g_fc1)
-    d_own = mix_back(qkv_own, ctx, logs, d_ctx, 0, 1, count - 1, d_own).reshape(wide)
+    other_recv = swap_core(other_send)
+    third = 3 * width // 2 * 3 // 10 // 8 * 8
+    cuts = [0, third, 2 * third, 3 * width // 2]
+    pieces = [summed(other_keep, other_recv, *cuts[k : k + 2]) for k in range(3)]
+    d_own, far_recv = lax.optimization_barrier((d_own, far_recv))
+    block_sum = added(far_keep, far_recv)
+    d_own, fc1_other, block_sum, *pieces = lax.optimization_barrier(
+        (d_own, fc1_other, block_sum, *pieces)
+    )
+    qkv_arrived = []
+    for index in range(1, count):
+        step = 16 >> index
+        block_recv = swap_step(block_sum, step)
+        qkv_arrived.append(swap_tensor(pieces[index - 1]))
+        d_own = mix_back(qkv_own, ctx, logs, d_ctx, 0, index, 1, d_own)
+        d_own, qkv_arrived[-1], block_recv, *pieces = lax.optimization_barrier(
+            (d_own, qkv_arrived[-1], block_recv, *pieces)
+        )
+        block_sum = ranked(block_sum, block_recv, step)
+        d_own, block_sum = lax.optimization_barrier((d_own, block_sum))
+    qkv_arrived += [swap_tensor(value) for value in pieces[count - 1 :]]
+    d_own = d_own.reshape(wide)
     own_keep, own_send, column_own = project_back(place, normed, d_own)
-    own_keep, fc1_other = lax.optimization_barrier((own_keep, fc1_other))
-    out_fc1 = widen(place, g_fc1, fc1_other, 0, 2 * block, hidden, 4)
-    own_swapped, qkv_arrived, out_fc1 = lax.optimization_barrier(
-        (swap_core(own_send), qkv_arrived, out_fc1)
-    )
-    g_qkv = own_keep.astype(F32) + own_swapped.astype(F32) + qkv_arrived.astype(F32)
-    g_qkv, d_own = lax.optimization_barrier((g_qkv.astype(BF16), d_own))
-    g_qkv = lax.psum(g_qkv, "dp", axis_index_groups=chip_groups(2))
-    in_buffer, in_send, sum_gain1, sum_bias1 = input_back(
-        place, d_own, d_other, in_weights, in_other, rows, low_resid, features
-    )
-    in_send, act_own = lax.optimization_barrier((in_send, stage_own[0]))
-    far = (1 - tensor) * count
-    in_arrived = swap_tensor(in_send)
-    out_buffer, out_send = layer_result(
-        place, act_own, stage_other[0], fc2_weight, mlp_other, resid, features
-    )
-    in_arrived, out_send = lax.optimization_barrier((in_arrived, out_send))
-    out_arrived = swap_tensor(out_send)
-    input_grad = lax.dynamic_update_slice_in_dim(in_buffer, in_arrived, far, 0)
-    layer_out = lax.dynamic_update_slice_in_dim(out_buffer, out_arrived, far, 0)
-
-    sums = jnp.concatenate([sum_gain1, sum_bias1, sum_ob, sum_gain2, sum_bias2, sum_fc2b])
+    own_keep, d_own, *qkv_arrived = lax.optimization_barrier((own_keep, d_own, *qkv_arrived))
+
+    def inputs(start, steps, held):
+        return input_back(
+            place, d_own, d_other, in_weights, in_other, rows, low_resid, features, start, steps, held
+        )
 
     def ordered(own, other):
         return jnp.where(tensor == 0, jnp.stack([own, other]), jnp.stack([other, own]))
@@ -1282,22 +1373,66 @@
         return vector[:width, 0], vector[2 * width :, 0]
 
     (q_own, v_own), (q_other, v_other) = heads_part(column_own), heads_part(column_other)
-    small_grads = jnp.concatenate(
+    early_sums = jnp.concatenate(
         [
-            sums.reshape(-1),
+            jnp.concatenate([sum_ob, sum_gain2, sum_bias2, sum_fc2b], axis=1)[0],
             ordered(
                 jnp.concatenate([q_own, v_own, stage_own[2][:, 0]]),
                 jnp.concatenate([q_other, v_other, stage_other[2][:, 0]]),
             ).reshape(-1),
         ]
     )
-    step = 1
-    while step < spots:
-        small_grads += lax.ppermute(
-            small_grads, "dp", [(spot, spot ^ step) for spot in range(spots)]
+    d_own, early_sums = lax.optimization_barrier((d_own, early_sums))
+    in_buffer, in_send, gain_a, bias_a = inputs(0, 1, None)
+    block_recv = swap_step(block_sum, 2)
+    own_recv, in_buffer, in_send = lax.optimization_barrier(
+        (swap_core(own_send), in_buffer, in_send)
+    )
+    in_arrived = [swap_tensor(in_send)]
+    g_qkv = own_keep.astype(F32) + own_recv.astype(F32) + jnp.concatenate(qkv_arrived).astype(F32)
+    g_qkv = jnp.concatenate([g_qkv.astype(BF16), g_o])
+    g_qkv, in_buffer = lax.optimization_barrier((g_qkv, in_buffer))
+    g_qkv = lax.psum(g_qkv, "dp", axis_index_groups=chip_groups(1))
+    in_buffer, in_send, gain_b, bias_b = inputs(1, count - 1, in_buffer)
+    norm_sums = jnp.concatenate([gain_a + gain_b, bias_a + bias_b], axis=1)
+    small_grads = jnp.concatenate([norm_sums[0], early_sums])
+    small_swapped = swap_tensor(small_grads)
+    in_send, in_arrived[0], act_own, block_recv = lax.optimization_barrier(
+        (in_send, in_arrived[0], stage_own[0], block_recv)
+    )
+    g_late = ranked(block_sum, block_recv, 2)
+    act_own, g_late = lax.optimization_barrier((act_own, g_late))
+    far = (1 - tensor) * count
+    in_arrived.append(swap_tensor(in_send))
+    late_other = swap_core(g_late)
+
+    def layers(start, steps, held):
+        return layer_result(
+            place, act_own, stage_other[0], fc2_weight, mlp_other, resid, features, start, steps, held
         )
-        step *= 2
-    small_grads += swap_tensor(small_grads)
+
+    out_buffer, out_send, = layers(0, count - 1, None)
+    in_arrived[1], out_send, out_buffer, small_swapped = lax.optimization_barrier(
+        (in_arrived[1], out_send, out_buffer, small_swapped)
+    )
+    small_grads += small_swapped
+    out_arrived = [swap_tensor(out_send)]
+    out_buffer, out_send = layers(count - 1, 1, out_buffer)
+    out_send, late_other, fc1_other = lax.optimization_barrier((out_send, late_other, fc1_other))
+    out_arrived.append(swap_tensor(out_send))
+
+    out_fc1 = widen(place, g_fc1, fc1_other, 2 * block, hidden, 4)
+    input_grad = lax.dynamic_update_slice_in_dim(in_buffer, jnp.concatenate(in_arrived), far, 0)
+    out_fc2 = widen(place, g_late, late_other, 2 * block, hidden, 4)
+
+    out_fc2, out_fc1, out_arrived[0] = lax.optimization_barrier((out_fc2, out_fc1, out_arrived[0]))
+    small_grads = exchange_sum(small_grads, (1, 2, 3))
+    out_fc2, input_grad = lax.optimization_barrier((out_fc2, input_grad))
+    out_fc2, out_arrived[1] = lax.optimization_barrier((out_fc2, out_arrived[1]))
+    g_qkv, small_grads, out_fc2 = lax.optimization_barrier((g_qkv, small_grads, out_fc2))
+    qkv_other_core = swap_core(g_qkv)
+    layer_out = lax.dynamic_update_slice_in_dim(out_buffer, jnp.concatenate(out_arrived), far, 0)
+    small_grads = exchange_sum(small_grads, range(4, spots, 4))
     g_feature = lax.dynamic_slice_in_dim(
         small_grads[: 6 * feat].reshape(6, feat), tensor * half, half, 1
     )
@@ -1305,16 +1440,7 @@
         small_grads[6 * feat :].reshape(2, 2 * width + hidden), tensor, 0, keepdims=False
     )
 
-    late_other = swap_core(g_late)
-    qkv_other_core = swap_core(g_qkv)
-    g_fc2 = widen(place, g_late, late_other, 0, 2 * block, hidden, 4)
-    g_o = widen(
-        place, g_late[2 * block :], late_other[2 * block :], 0, width // 2, width, 1
-    )
-    g_q, g_k, g_v = (
-        widen(place, g_qkv, qkv_other_core, index * width // 2, width // 2, width, 1)
-        for index in range(3)
-    )
+    g_q, g_k, g_v, g_o = widen(place, g_qkv, qkv_other_core, width // 2, width, 1, 4)
     return (
         jnp.swapaxes(layer_out, 1, 2),
         jnp.swapaxes(input_grad, 1, 2),
@@ -1331,7 +1457,7 @@
         g_feature[4],
         out_fc1.T,
         small_grads[2 * width :],
-        g_fc2,
+        out_fc2,
         g_feature[5],
     )
 

time: 961 us -> 787 us (0.82)
  waiting for transfers between devices: 256 us -> 57.1 us
  Pallas kernels: 568 us -> 592 us
  local copies, waits for them, and re-layouts: 39.3 us -> 20.4 us
  other arithmetic: 36.8 us -> 48.7 us
    psum x2 -> x1, waiting for transfers between devices: 104 us -> 0.01 us  [whole_device(): g_qkv = lax.psum(g_qkv, 'dp', axis_index_groups=chip_groups(1))]
    ppermute x16 -> x22, waiting for transfers between devices: 112 us -> 54.3 us  [swap_tensor(): return lax.ppermute(value, 'tensor', [(0, 1), (1, 0)])]
    psum x1, waiting for transfers between devices: 30.1 us -> 0.01 us  [whole_device(): g_fc1 = lax.psum(g_fc1, 'dp', axis_index_groups=chip_groups(0))]
    psum x1, starting transfers between devices: 10.9 us -> 0.3 us  [whole_device(): g_fc1 = lax.psum(g_fc1, 'dp', axis_index_groups=chip_groups(0))]
    pallas_call x1 -> x2, Pallas kernels: 39 us -> 49.4 us  [input_back(): pl.pallas_call(input_back_kernel, out_shape=[jax.ShapeDtypeStruct((2 * co...]
    ppermute x16 -> x22, starting transfers between devices: 18.6 us -> 27.1 us  [swap_tensor(): return lax.ppermute(value, 'tensor', [(0, 1), (1, 0)])]
    convert_element_type x6 -> x13, other arithmetic: 21 us -> 24.4 us  [the longest x6 12.7 us: summed(): (keep[low:high].astype(F32) + arrived[low:high].astype(F32)).astype(BF16)]
    pallas_call x3 -> x4, Pallas kernels: 79.7 us -> 82.1 us  [mix_back(): pl.pallas_call(functools.partial(mix_back_kernel, scale=1.0 / math.sqrt(h...]
  transfers between devices with their start and end apart: 36 -> 49, of which waited for: 16 -> 9; matrix products, arithmetic and copies ran while one was open for 6% -> 7% of each run, Pallas kernels for 52% -> 69%
where the time goes in v2:
time: 787 us; the launch traced here: 777 us
  Pallas kernels  592 us (75%)
  waiting for transfers between devices  57.1 us (7%)
  other arithmetic  48.7 us (6%)
  starting transfers between devices  43.6 us (6%)
  local copies, waits for them, and re-layouts  20.4 us (3%)
  between operations  15.1 us (2%)
    pallas_call x4, Pallas kernels, hidden_stage(): pl.pallas_call(functools.partial(hidden_kernel, which=which), out_shape=[...  153 us
    pallas_call x4, Pallas kernels, mix_back(): pl.pallas_call(functools.partial(mix_back_kernel, scale=1.0 / math.sqrt(h...  82.1 us
    pallas_call x4, Pallas kernels, mix(): pl.pallas_call(functools.partial(mix_kernel, scale=1.0 / math.sqrt(head_d...  58.2 us
    ppermute x22, waiting for transfers between devices, swap_tensor(): return lax.ppermute(value, 'tensor', [(0, 1), (1, 0)])  54.3 us
    pallas_call x2, Pallas kernels, input_back(): pl.pallas_call(input_back_kernel, out_shape=[jax.ShapeDtypeStruct((2 * co...  49.4 us
    pallas_call x1, Pallas kernels, resid_back(): pl.pallas_call(resid_back_kernel, grid=(count,), out_shape=[jax.ShapeDtyp...  46.6 us
    pallas_call x2, Pallas kernels, layer_result(): pl.pallas_call(functools.partial(layer_kernel, start=start, count=count),...  45.5 us
    pallas_call x2, Pallas kernels, project_back(): pl.pallas_call(project_back_kernel, out_shape=[part, part, jax.ShapeDtype...  38.8 us
  transfers between devices with their start and end apart: 49, of which 9 were waited for; matrix products, arithmetic and copies ran while one was open for 7% of the time, Pallas kernels for 69%

profile of v2, /device:TPU:0, one launch (start us, length us, event | category | flops | bytes accessed | tf_op | source)
XLA Modules:
  0.0 776.6 jit_solution(5237455146068338897)
XLA Ops:
  7.4 1.9 dynamic-slice_bitcast_fusion.3
  9.3 2.2 bitcast_select_fusion
  11.5 3.0 collective-permute-start
  14.6 2.0 collective-permute-start.2
  16.7 2.3 fusion
  19.8 15.4 %collective-permute-done.3 = bf16[6760]{0:T(1024)(128)(2,1)S(1)} collective-permute-done((bf16[6760]{0:T(1024)(128)(2,1)S(1)}, bf16[6760]{0:T(1024)(128)(2,1)S(1)}, u32[]{:S(2)}, u32[]{:S(2)}) %collective-permute-start.3) | collective-permute-done | bytes 13552 | tf_op jit(solution)/shard_map/ppermute | solution.py:1087
  38.0 10.2 %first_norm.3 = (bf16[3,1152,729]{2,1,0:T(8,128)(2,1)}, bf16[3,1152,729]{2,1,0:T(8,128)(2,1)}, bf16[3,24,72,729]{3,2,1,0:T(8,128)(2,1)}) custom-call(s32[8]{0:T(128)} %pad_add_fusion.place_ref, bf16[6,576,729]{2,1,0:T(8,128)(2,1)} %bitcast.42, bf16[1,576,729]{2,1,0:T(8,128)(2,1)} %collective-permute-done.other_ref, ...), custom_call_target="tpu_custom_call" | custom-call | flops 1160950528 | bytes 5033164 | tf_op jit(solution)/shard_map/first_norm/pallas_call | solution.py:419
  48.3 2.1 collective-permute-start.1
  50.5 10.2 %mix.4 = (bf16[3,16,72,729]{3,2,1,0:T(8,128)(2,1)}, f32[3,16,1,729]{3,2,1,0:T(1,128)}) custom-call(bf16[3,24,72,729]{3,2,1,0:T(8,128)(2,1)} %get-tuple-element.212.q_ref.k_ref.v_ref.rest_2_, bf16[3,24,72,729]{3,2,1,0:T(8,128)(2,1)} %get-tuple-element.212.q_ref.k_ref.v_ref.rest_2_, bf16[3,24,72,729]{3,2,1,0:T(8,128)(2,1)} %get-tuple-element.212.q_ref.k_ref.v_ref.rest_2_), custom_call_target="tpu_custom_call" | custom-call | flops 1741425920 | bytes 1343692 | tf_op jit(solution)/shard_map/mix/pallas_call | solution.py:504
  60.7 10.3 %collective-permute-done.1.other_ref = bf16[1,576,729]{2,1,0:T(8,128)(2,1)S(1)} collective-permute-done((bf16[1,576,729]{2,1,0:T(8,128)(2,1)S(1)}, bf16[1,576,729]{2,1,0:T(8,128)(2,1)S(1)}, u32[]{:S(2)}, u32[]{:S(2)}) %collective-permute-start.1) | collective-permute-done | bytes 839840 | tf_op jit(solution)/shard_map/ppermute | solution.py:1087
  71.9 10.1 %first_norm.4 = (bf16[3,1152,729]{2,1,0:T(8,128)(2,1)}, bf16[3,1152,729]{2,1,0:T(8,128)(2,1)}, bf16[3,24,72,729]{3,2,1,0:T(8,128)(2,1)}) custom-call(s32[8]{0:T(128)} %pad_add_fusion.place_ref, bf16[6,576,729]{2,1,0:T(8,128)(2,1)} %bitcast.43, bf16[1,576,729]{2,1,0:T(8,128)(2,1)} %copy-done.9, ...), custom_call_target="tpu_custom_call", output_to_operand_aliasing={{0}: (8, {}), {1}: (9, {}), {2}: (10, {})} | custom-call | flops 1160950528 | bytes 5033164 | tf_op jit(solution)/shard_map/first_norm/pallas_call | solution.py:419
  83.2 2.1 collective-permute-start.4
  85.3 2.8 dynamic-slice_bitcast_fusion
  88.7 2.1 copy.68
  90.8 10.2 %mix.5 = (bf16[3,16,72,729]{3,2,1,0:T(8,128)(2,1)}, f32[3,16,1,729]{3,2,1,0:T(1,128)}) custom-call(bf16[3,24,72,729]{3,2,1,0:T(8,128)(2,1)} %get-tuple-element.220.q_ref.k_ref.v_ref.rest_2_, bf16[3,24,72,729]{3,2,1,0:T(8,128)(2,1)} %get-tuple-element.220.q_ref.k_ref.v_ref.rest_2_, ...), custom_call_target="tpu_custom_call", output_to_operand_aliasing={{0}: (3, {}), {1}: (4, {})} | custom-call | flops 1741425920 | bytes 1343692 | tf_op jit(solution)/shard_map/mix/pallas_call | solution.py:504
  101.0 1.7 collective-permute-done.4.other_ref
  106.1 10.0 %first_norm.5 = (bf16[3,1152,729]{2,1,0:T(8,128)(2,1)}, bf16[3,1152,729]{2,1,0:T(8,128)(2,1)}, bf16[3,24,72,729]{3,2,1,0:T(8,128)(2,1)}) custom-call(s32[8]{0:T(128)} %pad_add_fusion.place_ref, bf16[6,576,729]{2,1,0:T(8,128)(2,1)} %bitcast.44, bf16[1,576,729]{2,1,0:T(8,128)(2,1)} %copy-done.8, ...), custom_call_target="tpu_custom_call", output_to_operand_aliasing={{0}: (8, {}), {1}: (9, {}), {2}: (10, {})} | custom-call | flops 1160950528 | bytes 5033164 | tf_op jit(solution)/shard_map/first_norm/pallas_call | solution.py:419
  116.2 10.2 %mix.6 = (bf16[3,16,72,729]{3,2,1,0:T(8,128)(2,1)}, f32[3,16,1,729]{3,2,1,0:T(1,128)}) custom-call(bf16[3,24,72,729]{3,2,1,0:T(8,128)(2,1)} %get-tuple-element.228.q_ref.k_ref.v_ref, bf16[3,24,72,729]{3,2,1,0:T(8,128)(2,1)} %get-tuple-element.228.q_ref.k_ref.v_ref, ...), custom_call_target="tpu_custom_call", output_to_operand_aliasing={{0}: (3, {}), {1}: (4, {})} | custom-call | flops 1741425920 | bytes 1343692 | tf_op jit(solution)/shard_map/mix/pallas_call | solution.py:504
  126.4 15.0 %project.1.q_ref.k_ref.v_ref = bf16[3,24,72,729]{3,2,1,0:T(8,128)(2,1)} custom-call(bf16[3,1152,729]{2,1,0:T(8,128)(2,1)} %get-tuple-element.227.normed_ref, bf16[2304,1152]{1,0:T(8,128)(2,1)} %all-gather.3.cloned.1.call-done.q_ref.k_ref.v_ref.w_other_ref, bf16[2304,1152]{1,0:T(8,128)(2,1)} %all-gather.3.cloned.1.call-done.q_ref.k_ref.v_ref.w_other_ref, ...), custom_call_target="tpu_custom_call" | custom-call | flops 3482851840 | bytes 8388608 | tf_op jit(solution)/shard_map/project/pallas_call | solution.py:463
  141.4 27.6 %mix.7 = (bf16[3,16,72,729]{3,2,1,0:T(8,128)(2,1)}, f32[3,16,1,729]{3,2,1,0:T(1,128)}) custom-call(bf16[3,24,72,729]{3,2,1,0:T(8,128)(2,1)} %project.1.q_ref.k_ref.v_ref, bf16[3,24,72,729]{3,2,1,0:T(8,128)(2,1)} %project.1.q_ref.k_ref.v_ref, bf16[3,24,72,729]{3,2,1,0:T(8,128)(2,1)} %project.1.q_ref.k_ref.v_ref, ...), custom_call_target="tpu_custom_call", output_to_operand_aliasing={{0}: (3, {}), {1}: (4, {})} | custom-call | flops 5224277504 | bytes 4031078 | tf_op jit(solution)/shard_map/mix/pallas_call | solution.py:504
  169.9 22.7 %second_norm.1 = (f32[3,1152,729]{2,1,0:T(8,128)}, bf16[3,1152,729]{2,1,0:T(8,128)(2,1)}, bf16[3,1152,729]{2,1,0:T(8,128)(2,1)}, f32[1,1152]{1,0:T(1,128)}) custom-call(s32[8]{0:T(128)} %pad_add_fusion.place_ref, bf16[3,1152,729]{2,1,0:T(8,128)(2,1)} %bitcast.37, bf16[576,1152]{1,0:T(8,128)(2,1)} %w_own_ref.5, ...), custom_call_target="tpu_custom_call" | custom-call | flops 2321901056 | bytes 16777216 | tf_op jit(solution)/shard_map/second_norm/pallas_call | solution.py:624
  193.1 44.2 %hidden_stage.4 = (bf16[3,2152,729]{2,1,0:T(8,128)(2,1)}, bf16[3,2152,729]{2,1,0:T(8,128)(2,1)}, f32[2152,1]{1,0:T(8,128)}, bf16[1088,1152]{1,0:T(8,128)(2,1)}, bf16[1088,1152]{1,0:T(8,128)(2,1)}) custom-call(s32[8]{0:T(128)} %pad_add_fusion.place_ref, bf16[3,1152,729]{2,1,0:T(8,128)(2,1)} %get-tuple-element.244.low_ref, ...), custom_call_target="tpu_custom_call" | custom-call | flops 86748807168 | bytes 125829120 | tf_op jit(solution)/shard_map/hidden_stage/pallas_call | solution.py:694
  237.8 36.2 %hidden_stage.5 = (bf16[3,2152,729]{2,1,0:T(8,128)(2,1)}, bf16[3,2152,729]{2,1,0:T(8,128)(2,1)}, f32[2152,1]{1,0:T(8,128)}, bf16[1088,1152]{1,0:T(8,128)(2,1)}, bf16[1088,1152]{1,0:T(8,128)(2,1)}) custom-call(s32[8]{0:T(128)} %pad_add_fusion.place_ref, ...), custom_call_target="tpu_custom_call", output_to_operand_aliasing={{0}: (6, {}), {1}: (7, {}), {2}: (8, {})} | custom-call | flops 86748807168 | bytes 125829120 | tf_op jit(solution)/shard_map/hidden_stage/pallas_call | solution.py:694
  274.0 2.2 add_convert_fusion.8
  276.2 3.2 add_convert_fusion.3
  280.5 1.6 add_convert_fusion.4
  283.6 36.3 %hidden_stage.6 = (bf16[3,2152,729]{2,1,0:T(8,128)(2,1)}, bf16[3,2152,729]{2,1,0:T(8,128)(2,1)}, f32[2152,1]{1,0:T(8,128)}, bf16[1088,1152]{1,0:T(8,128)(2,1)}, bf16[1088,1152]{1,0:T(8,128)(2,1)}) custom-call(s32[8]{0:T(128)} %pad_add_fusion.place_ref, bf16[3,1152,729]{2,1,0:T(8,128)(2,1)} %get-tuple-element.244.low_ref, ...), custom_call_target="tpu_custom_call" | custom-call | flops 86748807168 | bytes 125829120 | tf_op jit(solution)/shard_map/hidden_stage/pallas_call | solution.py:694
  322.9 36.1 %hidden_stage.7 = (bf16[3,2152,729]{2,1,0:T(8,128)(2,1)}, bf16[3,2152,729]{2,1,0:T(8,128)(2,1)}, f32[2152,1]{1,0:T(8,128)}, bf16[1088,1152]{1,0:T(8,128)(2,1)}, bf16[1088,1152]{1,0:T(8,128)(2,1)}) custom-call(s32[8]{0:T(128)} %pad_add_fusion.place_ref, ...), custom_call_target="tpu_custom_call", output_to_operand_aliasing={{0}: (6, {}), {1}: (7, {}), {2}: (8, {})} | custom-call | flops 86748807168 | bytes 125829120 | tf_op jit(solution)/shard_map/hidden_stage/pallas_call | solution.py:694
  359.0 1.5 collective-permute-start.16
  360.5 4.5 add_convert_fusion.1
  365.1 46.6 %resid_back.1 = (bf16[3,1152,729]{2,1,0:T(8,128)(2,1)}, f32[1,1152]{1,0:T(1,128)}, f32[1,1152]{1,0:T(1,128)}, f32[1,1152]{1,0:T(1,128)}) custom-call(bf16[3,2152,729]{2,1,0:T(8,128)(2,1)} %get-tuple-element.273.back_own_ref, bf16[3,2152,729]{2,1,0:T(8,128)(2,1)} %get-tuple-element.274.back_other_ref, bf16[2152,1152]{1,0:T(8,128)(2,1)} %bitcast.52, ...), custom_call_target="tpu_custom_call" | custom-call | flops 8674880512 | bytes 20971520 | tf_op jit(solution)/shard_map/resid_back/pallas_call | solution.py:823
  411.8 2.6 add_convert_fusion
  414.5 21.6 %context_back.1 = (bf16[3,1152,729]{2,1,0:T(8,128)(2,1)}, bf16[288,1152]{1,0:T(8,128)(2,1)}, bf16[288,1152]{1,0:T(8,128)(2,1)}, bf16[288,1152]{1,0:T(8,128)(2,1)}, bf16[288,1152]{1,0:T(8,128)(2,1)}) custom-call(s32[8]{0:T(128)} %pad_add_fusion.place_ref, bf16[3,1152,729]{2,1,0:T(8,128)(2,1)} %get-tuple-element.283.low_ref, bf16[3,1152,729]{2,1,0:T(8,128)(2,1)} %bitcast.38, ...), custom_call_target="tpu_custom_call" | custom-call | flops 4643802112 | bytes 10485760 | tf_op jit(solution)/shard_map/context_back/pallas_call | solution.py:889
  437.7 38.2 %mix_back.4 = bf16[3,24,72,729]{3,2,1,0:T(8,128)(2,1)} custom-call(bf16[3,24,72,729]{3,2,1,0:T(8,128)(2,1)} %project.1.q_ref.k_ref.v_ref, bf16[3,24,72,729]{3,2,1,0:T(8,128)(2,1)} %project.1.q_ref.k_ref.v_ref, bf16[3,24,72,729]{3,2,1,0:T(8,128)(2,1)} %project.1.q_ref.k_ref.v_ref, bf16[3,16,72,729]{3,2,1,0:T(8,128)(2,1)} %get-tuple-element.238.out_ref, ...), custom_call_target="tpu_custom_call" | custom-call | flops 13060694016 | bytes 8062156 | tf_op jit(solution)/shard_map/mix_back/pallas_call | solution.py:555
  483.0 1.5 collective-permute-start.21
  484.5 19.3 %project_back.2 = (bf16[864,1152]{1,0:T(8,128)(2,1)}, bf16[864,1152]{1,0:T(8,128)(2,1)}, f32[1728,1]{1,0:T(8,128)}) custom-call(s32[8]{0:T(128)} %pad_add_fusion.place_ref, bf16[3,1152,729]{2,1,0:T(8,128)(2,1)} %get-tuple-element.227.normed_ref, bf16[3,1728,729]{2,1,0:T(8,128)(2,1)} %bitcast.70), custom_call_target="tpu_custom_call" | custom-call | flops 3482851840 | bytes 8388608 | tf_op jit(solution)/shard_map/project_back/pallas_call | solution.py:942
  505.8 2.6 collective-permute-start.22
  508.4 14.5 %mix_back.5.rest_0_ = bf16[3,24,72,729]{3,2,1,0:T(8,128)(2,1)} custom-call(bf16[3,24,72,729]{3,2,1,0:T(8,128)(2,1)} %get-tuple-element.228.q_ref.k_ref.v_ref, bf16[3,24,72,729]{3,2,1,0:T(8,128)(2,1)} %get-tuple-element.228.q_ref.k_ref.v_ref, bf16[3,24,72,729]{3,2,1,0:T(8,128)(2,1)} %get-tuple-element.228.q_ref.k_ref.v_ref, ...), custom_call_target="tpu_custom_call" | custom-call | flops 544195584 | bytes 335923 | tf_op jit(solution)/shard_map/mix_back/pallas_call | solution.py:555
  523.1 2.3 add_convert_fusion.12
  525.4 2.2 add_convert_fusion.7
  528.8 14.7 %mix_back.6.rest_0_ = bf16[3,24,72,729]{3,2,1,0:T(8,128)(2,1)} custom-call(bf16[3,24,72,729]{3,2,1,0:T(8,128)(2,1)} %get-tuple-element.228.q_ref.k_ref.v_ref, bf16[3,24,72,729]{3,2,1,0:T(8,128)(2,1)} %get-tuple-element.228.q_ref.k_ref.v_ref, bf16[3,24,72,729]{3,2,1,0:T(8,128)(2,1)} %get-tuple-element.228.q_ref.k_ref.v_ref, ...), custom_call_target="tpu_custom_call", output_to_operand_aliasing={{}: (6, {})} | custom-call | flops 544195584 | bytes 335923 | tf_op jit(solution)/shard_map/mix_back/pallas_call | solution.py:555
  544.7 1.5 collective-permute-start.28
  547.6 1.6 reduce.6
  551.1 14.6 %mix_back.7 = bf16[3,24,72,729]{3,2,1,0:T(8,128)(2,1)} custom-call(bf16[3,24,72,729]{3,2,1,0:T(8,128)(2,1)} %get-tuple-element.228.q_ref.k_ref.v_ref, bf16[3,24,72,729]{3,2,1,0:T(8,128)(2,1)} %get-tuple-element.228.q_ref.k_ref.v_ref, bf16[3,24,72,729]{3,2,1,0:T(8,128)(2,1)} %get-tuple-element.228.q_ref.k_ref.v_ref, ...), custom_call_target="tpu_custom_call", output_to_operand_aliasing={{}: (6, {})} | custom-call | flops 544195584 | bytes 335923 | tf_op jit(solution)/shard_map/mix_back/pallas_call | solution.py:555
  566.7 19.5 %project_back.3 = (bf16[864,1152]{1,0:T(8,128)(2,1)}, bf16[864,1152]{1,0:T(8,128)(2,1)}, f32[1728,1]{1,0:T(8,128)}) custom-call(s32[8]{0:T(128)} %pad_add_fusion.place_ref, bf16[3,1152,729]{2,1,0:T(8,128)(2,1)} %get-tuple-element.227.normed_ref, bf16[3,1728,729]{2,1,0:T(8,128)(2,1)} %bitcast.39), custom_call_target="tpu_custom_call" | custom-call | flops 3482851840 | bytes 8388608 | tf_op jit(solution)/shard_map/project_back/pallas_call | solution.py:942
  588.3 19.5 %input_back.2 = (bf16[6,576,729]{2,1,0:T(8,128)(2,1)}, bf16[1,576,729]{2,1,0:T(8,128)(2,1)}, f32[1,1152]{1,0:T(1,128)}, f32[1,1152]{1,0:T(1,128)}) custom-call(s32[8]{0:T(128)} %pad_add_fusion.place_ref, bf16[3,1728,729]{2,1,0:T(8,128)(2,1)} %bitcast.40, bf16[3,1728,729]{2,1,0:T(8,128)(2,1)} %bitcast.71, bf16[576,1152]{1,0:T(8,128)(2,1)} %bitcast.56, ...), custom_call_target="tpu_custom_call" | custom-call | flops 23219011584 | bytes 79691776 | tf_op jit(solution)/shard_map/input_back/pallas_call | solution.py:1006
  607.8 2.8 add_convert_fusion.2
  610.6 1.7 pad_maximum_fusion
  612.3 1.5 collective-permute-start.31
  613.8 29.9 %input_back.3 = (bf16[6,576,729]{2,1,0:T(8,128)(2,1)}, bf16[2,576,729]{2,1,0:T(8,128)(2,1)}, f32[1,1152]{1,0:T(1,128)}, f32[1,1152]{1,0:T(1,128)}) custom-call(s32[8]{0:T(128)} %pad_add_fusion.place_ref, bf16[3,1728,729]{2,1,0:T(8,128)(2,1)} %bitcast.41, bf16[3,1728,729]{2,1,0:T(8,128)(2,1)} %bitcast.72, ...), custom_call_target="tpu_custom_call", output_to_operand_aliasing={{0}: (10, {})} | custom-call | flops 46438023168 | bytes 125829120 | tf_op jit(solution)/shard_map/input_back/pallas_call | solution.py:1006
  647.0 1.5 collective-permute-start.33
  648.5 27.5 %layer_result.2 = (bf16[6,576,729]{2,1,0:T(8,128)(2,1)}, bf16[2,576,729]{2,1,0:T(8,128)(2,1)}) custom-call(s32[8]{0:T(128)} %pad_add_fusion.place_ref, bf16[3,2152,729]{2,1,0:T(8,128)(2,1)} %get-tuple-element.357.act_own_ref, bf16[3,2152,729]{2,1,0:T(8,128)(2,1)} %get-tuple-element.358.act_other_ref, bf16[2152,1152]{1,0:T(8,128)(2,1)} %w_own_ref.7, ...), custom_call_target="tpu_custom_call" | custom-call | flops 57832538112 | bytes 100663296 | tf_op jit(solution)/shard_map/layer_result/pallas_call | solution.py:749
  676.0 11.8 %collective-permute-done.33 = bf16[2,576,729]{2,1,0:T(8,128)(2,1)} collective-permute-done((bf16[2,576,729]{2,1,0:T(8,128)(2,1)}, bf16[2,576,729]{2,1,0:T(8,128)(2,1)}, u32[]{:S(2)}, u32[]{:S(2)}) %collective-permute-start.33) | collective-permute-done | bytes 1679648 | tf_op jit(solution)/shard_map/ppermute | solution.py:1087
  689.2 18.0 %layer_result.3 = (bf16[6,576,729]{2,1,0:T(8,128)(2,1)}, bf16[1,576,729]{2,1,0:T(8,128)(2,1)}) custom-call(s32[8]{0:T(128)} %pad_add_fusion.place_ref, bf16[3,2152,729]{2,1,0:T(8,128)(2,1)} %get-tuple-element.357.act_own_ref, bf16[3,2152,729]{2,1,0:T(8,128)(2,1)} %get-tuple-element.358.act_other_ref, ...), custom_call_target="tpu_custom_call", output_to_operand_aliasing={{0}: (7, {})} | custom-call | flops 28916269056 | bytes 50331648 | tf_op jit(solution)/shard_map/layer_result/pallas_call | solution.py:749
  708.5 1.7 collective-permute-start.39
  710.3 3.5 maximum_dynamic-update-slice_fusion
  714.5 8.8 %widen.3 = f32[2152,1152]{1,0:T(8,128)} custom-call(s32[8]{0:T(128)} %pad_add_fusion.place_ref, bf16[1088,1152]{1,0:T(8,128)(2,1)} %copy-done, bf16[1088,1152]{1,0:T(8,128)(2,1)} %copy-done.2), custom_call_target="tpu_custom_call" | custom-call | bytes 991641 | tf_op jit(solution)/shard_map/widen/pallas_call | solution.py:1067
  723.2 8.7 %widen.4 = f32[2152,1152]{1,0:T(8,128)} custom-call(s32[8]{0:T(128)} %pad_add_fusion.place_ref, bf16[1088,1152]{1,0:T(8,128)(2,1)} %all-reduce.7.cloned.1.call-done.mine_ref, bf16[1088,1152]{1,0:T(8,128)(2,1)} %collective-permute-done.23.other_ref), custom_call_target="tpu_custom_call" | custom-call | bytes 991641 | tf_op jit(solution)/shard_map/widen/pallas_call | solution.py:1067
  732.0 14.6 %collective-permute-done.37 = bf16[1,576,729]{2,1,0:T(8,128)(2,1)S(1)} collective-permute-done((bf16[1,576,729]{2,1,0:T(8,128)(2,1)}, bf16[1,576,729]{2,1,0:T(8,128)(2,1)S(1)}, u32[]{:S(2)}, u32[]{:S(2)}) %collective-permute-start.37) | collective-permute-done | bytes 839840 | tf_op jit(solution)/shard_map/ppermute | solution.py:1087
  746.6 1.5 collective-permute-start.43
  748.7 2.3 collective-permute-start.41
  751.0 3.2 maximum_dynamic-update-slice_fusion.1
  757.0 1.5 copy-done.1
  758.5 11.1 %widen.5 = (f32[576,1152]{1,0:T(8,128)}, f32[576,1152]{1,0:T(8,128)}, f32[576,1152]{1,0:T(8,128)}, f32[576,1152]{1,0:T(8,128)}) custom-call(s32[8]{0:T(128)} %pad_add_fusion.place_ref, bf16[1152,1152]{1,0:T(8,128)(2,1)} %all-reduce.9.cloned.1.call-done.mine_ref, bf16[1152,1152]{1,0:T(8,128)(2,1)} %copy-done.1), custom_call_target="tpu_custom_call" | custom-call | bytes 1061683 | tf_op jit(solution)/shard_map/widen/pallas_call | solution.py:1067
  (223 shorter events, 46.9 us)
Async XLA Ops:
  7.2 119.2 %all-gather.3.cloned.1.call-start = ((), (), s32[]{:S(2)}) async-start(), calls=%async_computation | async-start | bytes 5640192 | tf_op jit(solution)/shard_map/all_gather | solution.py:1243
  7.3 7.2 copy-start.25
  7.3 7.2 copy-start.26
  7.3 7.1 copy-start.27
  11.5 26.6 %collective-permute-start = (bf16[1,576,729]{2,1,0:T(8,128)(2,1)S(1)}, bf16[1,576,729]{2,1,0:T(8,128)(2,1)}, u32[]{:S(2)}, u32[]{:S(2)}) collective-permute-start(bf16[1,576,729]{2,1,0:T(8,128)(2,1)S(1)} %get-tuple-element.206), channel_id=1, source_target_pairs={{0,1},{1,0},{2,3},{3,2},{4,5},{5,4},{6,7},{7,6},{8,9},{9,8},{10,11... | collective-permute-start | bytes 2519432 | tf_op jit(solution)/shard_map/ppermute | solution.py:1087
  14.6 20.6 %collective-permute-start.3 = (bf16[6760]{0:T(1024)(128)(2,1)S(1)}, bf16[6760]{0:T(1024)(128)(2,1)S(1)}, u32[]{:S(2)}, u32[]{:S(2)}) collective-permute-start(bf16[6760]{0:T(1024)(128)(2,1)S(1)} %concatenate.62), channel_id=1, source_target_pairs={{0,1},{1,0},{2,3},{3,2},{4,5},{5,4},{6,7},{7,6},{8,9},{9,8},{10,11... | collective-permute-start | bytes 40568 | tf_op jit(solution)/shard_map/ppermute | solution.py:1087
  14.6 33.6 %collective-permute-start.2 = (bf16[144,1152]{1,0:T(8,128)(2,1)}, bf16[144,1152]{1,0:T(8,128)(2,1)}, u32[]{:S(2)}, u32[]{:S(2)}) collective-permute-start(bf16[144,1152]{1,0:T(8,128)(2,1)} %bitcast_select_fusion), channel_id=1, source_target_pairs={{0,1},{1,0},{2,3},{3,2},{4,5},{5,4},{6,7},{7,6},{8,9},{9,8},{10,11... | collective-permute-start | bytes 995336 | tf_op jit(solution)/shard_map/ppermute | solution.py:1087
  19.7 16.1 %copy-start.19 = (bf16[1,6760]{1,0:T(2,128)(2,1)}, bf16[1,6760]{1,0:T(2,128)(2,1)S(1)}, u32[]{:S(2)}) copy-start(bf16[1,6760]{1,0:T(2,128)(2,1)S(1)} %stack.34) | copy-start | bytes 40564
  38.0 12.4 %copy-start.16 = (bf16[272,1152]{1,0:T(8,128)(2,1)S(1)}, bf16[272,1152]{1,0:T(8,128)(2,1)}, u32[]{:S(2)}) copy-start(bf16[272,1152]{1,0:T(8,128)(2,1)} %fusion) | copy-start | bytes 1880068
  48.2 144.9 %all-gather.5.cloned.1.call-start = ((), (), s32[]{:S(2)}) async-start(), calls=%async_computation.1 | async-start | bytes 10653696 | tf_op jit(solution)/shard_map/all_gather | solution.py:1246
  48.3 22.7 %collective-permute-start.1 = (bf16[1,576,729]{2,1,0:T(8,128)(2,1)S(1)}, bf16[1,576,729]{2,1,0:T(8,128)(2,1)S(1)}, u32[]{:S(2)}, u32[]{:S(2)}) collective-permute-start(bf16[1,576,729]{2,1,0:T(8,128)(2,1)S(1)} %get-tuple-element.207), channel_id=1, source_target_pairs={{0,1},{1,0},{2,3},{3,2},{4,5},{5,4},{6,7},{7,6},{8,9},{9,8},{10,11... | collective-permute-start | bytes 2519432 | tf_op jit(solution)/shard_map/ppermute | solution.py:1087
  50.4 31.6 %collective-permute-start.5 = (bf16[272,1152]{1,0:T(8,128)(2,1)S(1)}, bf16[272,1152]{1,0:T(8,128)(2,1)S(1)}, u32[]{:S(2)}, u32[]{:S(2)}) collective-permute-start(bf16[272,1152]{1,0:T(8,128)(2,1)S(1)} %copy-done.16), channel_id=1, source_target_pairs={{0,1},{1,0},{2,3},{3,2},{4,5},{5,4},{6,7},{7,6},{8,9},{9,8},{10,11... | collective-permute-start | bytes 1880072 | tf_op jit(solution)/shard_map/ppermute | solution.py:1087
  82.9 420.9 %all-reduce.7.cloned.1.call-start = ((), (), s32[]{:S(2)}) async-start(), calls=%async_computation.2 | async-start | bytes 5013504 | tf_op jit(solution)/shard_map/psum | solution.py:1304
  83.2 19.6 %collective-permute-start.4 = (bf16[1,576,729]{2,1,0:T(8,128)(2,1)S(1)}, bf16[1,576,729]{2,1,0:T(8,128)(2,1)S(1)}, u32[]{:S(2)}, u32[]{:S(2)}) collective-permute-start(bf16[1,576,729]{2,1,0:T(8,128)(2,1)S(1)} %get-tuple-element.214), channel_id=1, source_target_pairs={{0,1},{1,0},{2,3},{3,2},{4,5},{5,4},{6,7},{7,6},{8,9},{9,8},{10,11... | collective-permute-start | bytes 2519432 | tf_op jit(solution)/shard_map/ppermute | solution.py:1087
  102.7 66.2 %collective-permute-start.6 = (bf16[1,576,729]{2,1,0:T(8,128)(2,1)}, bf16[1,576,729]{2,1,0:T(8,128)(2,1)S(1)}, u32[]{:S(2)}, u32[]{:S(2)}) collective-permute-start(bf16[1,576,729]{2,1,0:T(8,128)(2,1)} %get-tuple-element.235), channel_id=1, source_target_pairs={{0,1},{1,0},{2,3},{3,2},{4,5},{5,4},{6,7},{7,6},{8,9},{9,8},{10,11... | collective-permute-start | bytes 2519432 | tf_op jit(solution)/shard_map/ppermute | solution.py:1087
  104.1 64.9 %collective-permute-start.7 = (bf16[1,576,729]{2,1,0:T(8,128)(2,1)S(1)}, bf16[1,576,729]{2,1,0:T(8,128)(2,1)}, u32[]{:S(2)}, u32[]{:S(2)}) collective-permute-start(bf16[1,576,729]{2,1,0:T(8,128)(2,1)S(1)} %get-tuple-element.236), channel_id=1, source_target_pairs={{0,1},{1,0},{2,3},{3,2},{4,5},{5,4},{6,7},{7,6},{8,9},{9,8},{10,11... | collective-permute-start | bytes 2519432 | tf_op jit(solution)/shard_map/ppermute | solution.py:1087
  104.8 64.2 %collective-permute-start.8 = (bf16[1,576,729]{2,1,0:T(8,128)(2,1)S(1)}, bf16[1,576,729]{2,1,0:T(8,128)(2,1)}, u32[]{:S(2)}, u32[]{:S(2)}) collective-permute-start(bf16[1,576,729]{2,1,0:T(8,128)(2,1)S(1)} %get-tuple-element.237), channel_id=1, source_target_pairs={{0,1},{1,0},{2,3},{3,2},{4,5},{5,4},{6,7},{7,6},{8,9},{9,8},{10,11... | collective-permute-start | bytes 2519432 | tf_op jit(solution)/shard_map/ppermute | solution.py:1087
  237.3 42.1 %collective-permute-start.9 = (bf16[1088,1152]{1,0:T(8,128)(2,1)}, bf16[1088,1152]{1,0:T(8,128)(2,1)S(1)}, u32[]{:S(2)}, u32[]{:S(2)}) collective-permute-start(bf16[1088,1152]{1,0:T(8,128)(2,1)} %get-tuple-element.251), channel_id=1, source_target_pairs={{0,2},{2,0},{4,6},{6,4},{8,10},{10,8},{12,14},{14,12},{16,18},{18,... | collective-permute-start | bytes 7520264 | tf_op jit(solution)/shard_map/ppermute | solution.py:1091
  237.6 36.3 %collective-permute-start.10 = (bf16[1088,1152]{1,0:T(8,128)(2,1)}, bf16[1088,1152]{1,0:T(8,128)(2,1)S(1)}, u32[]{:S(2)}, u32[]{:S(2)}) collective-permute-start(bf16[1088,1152]{1,0:T(8,128)(2,1)} %get-tuple-element.253), channel_id=1, source_target_pairs={{0,2},{2,0},{4,6},{6,4},{8,10},{10,8},{12,14},{14,12},{16,18},{18,... | collective-permute-start | bytes 7520264 | tf_op jit(solution)/shard_map/ppermute | solution.py:1091
  282.1 38.7 %collective-permute-start.11 = (bf16[720,1152]{1,0:T(8,128)(2,1)}, bf16[720,1152]{1,0:T(8,128)(2,1)}, u32[]{:S(2)}, u32[]{:S(2)}) collective-permute-start(bf16[720,1152]{1,0:T(8,128)(2,1)} %add_convert_fusion.4), channel_id=1, source_target_pairs={{0,1},{1,0},{2,3},{3,2},{4,5},{5,4},{6,7},{7,6},{8,9},{9,8},{10,11... | collective-permute-start | bytes 4976648 | tf_op jit(solution)/shard_map/ppermute | solution.py:1087
  319.9 40.6 %collective-permute-start.12 = (bf16[1088,1152]{1,0:T(8,128)(2,1)}, bf16[1088,1152]{1,0:T(8,128)(2,1)S(1)}, u32[]{:S(2)}, u32[]{:S(2)}) collective-permute-start(bf16[1088,1152]{1,0:T(8,128)(2,1)} %get-tuple-element.264), channel_id=1, source_target_pairs={{0,2},{2,0},{4,6},{6,4},{8,10},{10,8},{12,14},{14,12},{16,18},{18,... | collective-permute-start | bytes 7520264 | tf_op jit(solution)/shard_map/ppermute | solution.py:1091
  320.0 45.1 %collective-permute-start.15 = (bf16[1088,1152]{1,0:T(8,128)(2,1)}, bf16[1088,1152]{1,0:T(8,128)(2,1)S(1)}, u32[]{:S(2)}, u32[]{:S(2)}) collective-permute-start(bf16[1088,1152]{1,0:T(8,128)(2,1)} %get-tuple-element.271), channel_id=1, source_target_pairs={{0,2},{2,0},{4,6},{6,4},{8,10},{10,8},{12,14},{14,12},{16,18},{18,... | collective-permute-start | bytes 7520264 | tf_op jit(solution)/shard_map/ppermute | solution.py:1091
  320.8 38.1 %collective-permute-start.14 = (bf16[352,1152]{1,0:T(8,128)(2,1)}, bf16[352,1152]{1,0:T(8,128)(2,1)}, u32[]{:S(2)}, u32[]{:S(2)}) collective-permute-start(bf16[352,1152]{1,0:T(8,128)(2,1)} %add_convert_fusion.8), channel_id=1, source_target_pairs={{0,1},{1,0},{2,3},{3,2},{4,5},{5,4},{6,7},{7,6},{8,9},{9,8},{10,11... | collective-permute-start | bytes 2433032 | tf_op jit(solution)/shard_map/ppermute | solution.py:1087
  322.3 36.7 %collective-permute-start.13 = (bf16[368,1152]{1,0:T(8,128)(2,1)}, bf16[368,1152]{1,0:T(8,128)(2,1)S(1)}, u32[]{:S(2)}, u32[]{:S(2)}) collective-permute-start(bf16[368,1152]{1,0:T(8,128)(2,1)} %add_convert_fusion.6), channel_id=1, source_target_pairs={{0,1},{1,0},{2,3},{3,2},{4,5},{5,4},{6,7},{7,6},{8,9},{9,8},{10,11... | collective-permute-start | bytes 2543624 | tf_op jit(solution)/shard_map/ppermute | solution.py:1087
  359.0 52.8 %collective-permute-start.16 = (bf16[736,1152]{1,0:T(8,128)(2,1)}, bf16[736,1152]{1,0:T(8,128)(2,1)}, u32[]{:S(2)}, u32[]{:S(2)}) collective-permute-start(bf16[736,1152]{1,0:T(8,128)(2,1)} %add_convert_fusion.3), channel_id=1, source_target_pairs={{0,1},{1,0},{2,3},{3,2},{4,5},{5,4},{6,7},{7,6},{8,9},{9,8},{10,11... | collective-permute-start | bytes 5087240 | tf_op jit(solution)/shard_map/ppermute | solution.py:1087
  365.1 381.5 %all-reduce.9.cloned.1.call-start = ((), (), s32[]{:S(2)}) async-start(), calls=%async_computation.3 | async-start | bytes 5308416 | tf_op jit(solution)/shard_map/psum | solution.py:1395
  365.1 46.6 %copy-start.3 = (bf16[1088,1152]{1,0:T(8,128)(2,1)S(1)}, bf16[1088,1152]{1,0:T(8,128)(2,1)}, u32[]{:S(2)}) copy-start(bf16[1088,1152]{1,0:T(8,128)(2,1)} %get-tuple-element.279) | copy-start | bytes 7520260
  436.1 39.8 %collective-permute-start.18 = (bf16[288,1152]{1,0:T(8,128)(2,1)}, bf16[288,1152]{1,0:T(8,128)(2,1)S(1)}, u32[]{:S(2)}, u32[]{:S(2)}) collective-permute-start(bf16[288,1152]{1,0:T(8,128)(2,1)} %get-tuple-element.290), channel_id=1, source_target_pairs={{0,2},{2,0},{4,6},{6,4},{8,10},{10,8},{12,14},{14,12},{16,18},{18,... | collective-permute-start | bytes 1990664 | tf_op jit(solution)/shard_map/ppermute | solution.py:1091
  436.1 41.9 %collective-permute-start.19 = (bf16[288,1152]{1,0:T(8,128)(2,1)}, bf16[288,1152]{1,0:T(8,128)(2,1)S(1)}, u32[]{:S(2)}, u32[]{:S(2)}) collective-permute-start(bf16[288,1152]{1,0:T(8,128)(2,1)} %get-tuple-element.292), channel_id=1, source_target_pairs={{0,2},{2,0},{4,6},{6,4},{8,10},{10,8},{12,14},{14,12},{16,18},{18,... | collective-permute-start | bytes 1990664 | tf_op jit(solution)/shard_map/ppermute | solution.py:1091
  436.6 43.7 %collective-permute-start.17 = (bf16[544,1152]{1,0:T(8,128)(2,1)S(1)}, bf16[544,1152]{1,0:T(8,128)(2,1)S(1)}, u32[]{:S(2)}, u32[]{:S(2)}) collective-permute-start(bf16[544,1152]{1,0:T(8,128)(2,1)S(1)} %get-tuple-element.287), channel_id=1, source_target_pairs={{0,4},{2,6},{4,0},{6,2},{8,12},{10,14},{12,8},{14,10},{16,20},{18,... | collective-permute-start | bytes 3760136 | tf_op jit(solution)/shard_map/ppermute | solution.py:1123
  437.7 39.1 %copy-start.12 = (bf16[288,1152]{1,0:T(8,128)(2,1)S(1)}, bf16[288,1152]{1,0:T(8,128)(2,1)}, u32[]{:S(2)}) copy-start(bf16[288,1152]{1,0:T(8,128)(2,1)} %get-tuple-element.289) | copy-start | bytes 1990660
  481.6 22.2 %collective-permute-start.20 = (bf16[288,1152]{1,0:T(8,128)(2,1)S(1)}, bf16[288,1152]{1,0:T(8,128)(2,1)}, u32[]{:S(2)}, u32[]{:S(2)}) collective-permute-start(bf16[288,1152]{1,0:T(8,128)(2,1)S(1)} %add_convert_fusion.10), channel_id=1, source_target_pairs={{0,1},{1,0},{2,3},{3,2},{4,5},{5,4},{6,7},{7,6},{8,9},{9,8},{10,11... | collective-permute-start | bytes 1990664 | tf_op jit(solution)/shard_map/ppermute | solution.py:1087
  483.0 20.8 %collective-permute-start.21 = (bf16[272,1152]{1,0:T(8,128)(2,1)}, bf16[272,1152]{1,0:T(8,128)(2,1)S(1)}, u32[]{:S(2)}, u32[]{:S(2)}) collective-permute-start(bf16[272,1152]{1,0:T(8,128)(2,1)} %get-tuple-element.300), channel_id=1, source_target_pairs={{0,8},{2,10},{4,12},{6,14},{8,0},{10,2},{12,4},{14,6},{16,24},{18,... | collective-permute-start | bytes 1880072 | tf_op jit(solution)/shard_map/ppermute | solution.py:1123
  503.8 19.3 %collective-permute-start.24 = (bf16[864,1152]{1,0:T(8,128)(2,1)}, bf16[864,1152]{1,0:T(8,128)(2,1)}, u32[]{:S(2)}, u32[]{:S(2)}) collective-permute-start(bf16[864,1152]{1,0:T(8,128)(2,1)} %get-tuple-element.311), channel_id=1, source_target_pairs={{0,2},{2,0},{4,6},{6,4},{8,10},{10,8},{12,14},{14,12},{16,18},{18,... | collective-permute-start | bytes 5971976 | tf_op jit(solution)/shard_map/ppermute | solution.py:1091
  503.8 23.9 %collective-permute-start.23 = (bf16[1088,1152]{1,0:T(8,128)(2,1)}, bf16[1088,1152]{1,0:T(8,128)(2,1)}, u32[]{:S(2)}, u32[]{:S(2)}) collective-permute-start(bf16[1088,1152]{1,0:T(8,128)(2,1)} %all-reduce.7.cloned.1.call-done.mine_ref), channel_id=1, source_target_pairs={{0,2},{2,0},{4,6},{6,4},{8,10},{10,8},{12,14},{14,12},{16,18},{18,... | collective-permute-start | bytes 7520264 | tf_op jit(solution)/shard_map/ppermute | solution.py:1091
  505.8 17.3 %copy-start.5 = (bf16[864,1152]{1,0:T(8,128)(2,1)S(1)}, bf16[864,1152]{1,0:T(8,128)(2,1)}, u32[]{:S(2)}) copy-start(bf16[864,1152]{1,0:T(8,128)(2,1)} %get-tuple-element.310) | copy-start | bytes 5971972
  505.8 17.2 %collective-permute-start.22 = (bf16[136,1152]{1,0:T(8,128)(2,1)S(1)}, bf16[136,1152]{1,0:T(8,128)(2,1)S(1)}, u32[]{:S(2)}, u32[]{:S(2)}) collective-permute-start(bf16[136,1152]{1,0:T(8,128)(2,1)S(1)} %get-tuple-element.305), channel_id=1, source_target_pairs={{0,16},{2,18},{4,20},{6,22},{8,24},{10,26},{12,28},{14,30},{16,0},... | collective-permute-start | bytes 940040 | tf_op jit(solution)/shard_map/ppermute | solution.py:1123
  527.7 17.0 %collective-permute-start.25 = (bf16[256,1152]{1,0:T(8,128)(2,1)S(1)}, bf16[256,1152]{1,0:T(8,128)(2,1)}, u32[]{:S(2)}, u32[]{:S(2)}) collective-permute-start(bf16[256,1152]{1,0:T(8,128)(2,1)S(1)} %get-tuple-element.313), channel_id=1, source_target_pairs={{0,1},{1,0},{2,3},{3,2},{4,5},{5,4},{6,7},{7,6},{8,9},{9,8},{10,11... | collective-permute-start | bytes 1769480 | tf_op jit(solution)/shard_map/ppermute | solution.py:1087
  528.3 16.3 %collective-permute-start.26 = (bf16[136,1152]{1,0:T(8,128)(2,1)S(1)}, bf16[136,1152]{1,0:T(8,128)(2,1)S(1)}, u32[]{:S(2)}, u32[]{:S(2)}) collective-permute-start(bf16[136,1152]{1,0:T(8,128)(2,1)S(1)} %add_convert_fusion.14), channel_id=1, source_target_pairs={{0,16},{2,18},{4,20},{6,22},{8,24},{10,26},{12,28},{14,30},{16,0},... | collective-permute-start | bytes 940040 | tf_op jit(solution)/shard_map/ppermute | solution.py:1123
  544.7 21.0 %collective-permute-start.28 = (bf16[272,1152]{1,0:T(8,128)(2,1)S(1)}, bf16[272,1152]{1,0:T(8,128)(2,1)S(1)}, u32[]{:S(2)}, u32[]{:S(2)}) collective-permute-start(bf16[272,1152]{1,0:T(8,128)(2,1)S(1)} %pad_maximum_fusion.3), channel_id=1, source_target_pairs={{0,8},{2,10},{4,12},{6,14},{8,0},{10,2},{12,4},{14,6},{16,24},{18,... | collective-permute-start | bytes 1880072 | tf_op jit(solution)/shard_map/ppermute | solution.py:1123
  546.2 19.5 %collective-permute-start.27 = (bf16[256,1152]{1,0:T(8,128)(2,1)}, bf16[256,1152]{1,0:T(8,128)(2,1)}, u32[]{:S(2)}, u32[]{:S(2)}) collective-permute-start(bf16[256,1152]{1,0:T(8,128)(2,1)} %get-tuple-element.320), channel_id=1, source_target_pairs={{0,1},{1,0},{2,3},{3,2},{4,5},{5,4},{6,7},{7,6},{8,9},{9,8},{10,11... | collective-permute-start | bytes 1769480 | tf_op jit(solution)/shard_map/ppermute | solution.py:1087
  566.0 22.3 %collective-permute-start.29 = (bf16[352,1152]{1,0:T(8,128)(2,1)}, bf16[352,1152]{1,0:T(8,128)(2,1)}, u32[]{:S(2)}, u32[]{:S(2)}) collective-permute-start(bf16[352,1152]{1,0:T(8,128)(2,1)} %add_convert_fusion.7), channel_id=1, source_target_pairs={{0,1},{1,0},{2,3},{3,2},{4,5},{5,4},{6,7},{7,6},{8,9},{9,8},{10,11... | collective-permute-start | bytes 2433032 | tf_op jit(solution)/shard_map/ppermute | solution.py:1087
  587.8 58.1 %collective-permute-start.32 = (bf16[544,1152]{1,0:T(8,128)(2,1)S(1)}, bf16[544,1152]{1,0:T(8,128)(2,1)S(1)}, u32[]{:S(2)}, u32[]{:S(2)}) collective-permute-start(bf16[544,1152]{1,0:T(8,128)(2,1)S(1)} %pad_maximum_fusion.2), channel_id=1, source_target_pairs={{0,4},{2,6},{4,0},{6,2},{8,12},{10,14},{12,8},{14,10},{16,20},{18,... | collective-permute-start | bytes 3760136 | tf_op jit(solution)/shard_map/ppermute | solution.py:1123
  588.2 19.5 %collective-permute-start.30 = (bf16[864,1152]{1,0:T(8,128)(2,1)}, bf16[864,1152]{1,0:T(8,128)(2,1)}, u32[]{:S(2)}, u32[]{:S(2)}) collective-permute-start(bf16[864,1152]{1,0:T(8,128)(2,1)} %get-tuple-element.341), channel_id=1, source_target_pairs={{0,2},{2,0},{4,6},{6,4},{8,10},{10,8},{12,14},{14,12},{16,18},{18,... | collective-permute-start | bytes 5971976 | tf_op jit(solution)/shard_map/ppermute | solution.py:1091
  588.3 56.9 %copy-start.17 = (f32[11216]{0:T(1024)}, f32[11216]{0:T(1024)S(1)}, u32[]{:S(2)}) copy-start(f32[11216]{0:T(1024)S(1)} %pad_maximum_fusion.5) | copy-start | bytes 134596
  588.3 19.5 %copy-start.6 = (bf16[864,1152]{1,0:T(8,128)(2,1)S(1)}, bf16[864,1152]{1,0:T(8,128)(2,1)}, u32[]{:S(2)}) copy-start(bf16[864,1152]{1,0:T(8,128)(2,1)} %get-tuple-element.340) | copy-start | bytes 5971972
  612.3 31.4 %copy-start.37 = (f32[1,1152]{1,0:T(1,128)S(1)}, f32[1,1152]{1,0:T(1,128)}, u32[]{:S(2)}) copy-start(f32[1,1152]{1,0:T(1,128)} %get-tuple-element.364) | copy-start | bytes 13828
  612.3 32.1 %copy-start.36 = (f32[1,1152]{1,0:T(1,128)S(1)}, f32[1,1152]{1,0:T(1,128)}, u32[]{:S(2)}) copy-start(f32[1,1152]{1,0:T(1,128)} %get-tuple-element.362) | copy-start | bytes 13828
  612.3 33.6 %collective-permute-start.31 = (bf16[1,576,729]{2,1,0:T(8,128)(2,1)}, bf16[1,576,729]{2,1,0:T(8,128)(2,1)S(1)}, u32[]{:S(2)}, u32[]{:S(2)}) collective-permute-start(bf16[1,576,729]{2,1,0:T(8,128)(2,1)} %get-tuple-element.352), channel_id=1, source_target_pairs={{0,1},{1,0},{2,3},{3,2},{4,5},{5,4},{6,7},{7,6},{8,9},{9,8},{10,11... | collective-permute-start | bytes 2519432 | tf_op jit(solution)/shard_map/ppermute | solution.py:1087
  645.2 30.8 %collective-permute-start.34 = (f32[13520]{0:T(1024)S(1)}, f32[13520]{0:T(1024)S(1)}, u32[]{:S(2)}, u32[]{:S(2)}) collective-permute-start(f32[13520]{0:T(1024)S(1)} %pad_maximum_fusion.4), channel_id=1, source_target_pairs={{0,1},{1,0},{2,3},{3,2},{4,5},{5,4},{6,7},{7,6},{8,9},{9,8},{10,11... | collective-permute-start | bytes 162248 | tf_op jit(solution)/shard_map/ppermute | solution.py:1087
  647.0 29.0 %copy-start = (bf16[1088,1152]{1,0:T(8,128)(2,1)}, bf16[1088,1152]{1,0:T(8,128)(2,1)S(1)}, u32[]{:S(2)}) copy-start(bf16[1088,1152]{1,0:T(8,128)(2,1)S(1)} %pad_maximum_fusion.1.mine_ref) | copy-start | bytes 7520260
  647.0 40.8 %collective-permute-start.33 = (bf16[2,576,729]{2,1,0:T(8,128)(2,1)}, bf16[2,576,729]{2,1,0:T(8,128)(2,1)}, u32[]{:S(2)}, u32[]{:S(2)}) collective-permute-start(bf16[2,576,729]{2,1,0:T(8,128)(2,1)} %get-tuple-element.359), channel_id=1, source_target_pairs={{0,1},{1,0},{2,3},{3,2},{4,5},{5,4},{6,7},{7,6},{8,9},{9,8},{10,11... | collective-permute-start | bytes 5038856 | tf_op jit(solution)/shard_map/ppermute | solution.py:1087
  648.5 58.8 %collective-permute-start.35 = (bf16[1088,1152]{1,0:T(8,128)(2,1)S(1)}, bf16[1088,1152]{1,0:T(8,128)(2,1)S(1)}, u32[]{:S(2)}, u32[]{:S(2)}) collective-permute-start(bf16[1088,1152]{1,0:T(8,128)(2,1)S(1)} %pad_maximum_fusion.1.mine_ref), channel_id=1, source_target_pairs={{0,2},{2,0},{4,6},{6,4},{8,10},{10,8},{12,14},{14,12},{16,18},{18,... | collective-permute-start | bytes 7520264 | tf_op jit(solution)/shard_map/ppermute | solution.py:1091
  676.0 31.2 %copy-start.24 = (f32[13520]{0:T(1024)}, f32[13520]{0:T(1024)S(1)}, u32[]{:S(2)}) copy-start(f32[13520]{0:T(1024)S(1)} %collective-permute-done.34) | copy-start | bytes 162244
  687.8 19.7 %copy-start.18 = (f32[11216]{0:T(1024)S(1)}, f32[11216]{0:T(1024)}, u32[]{:S(2)}) copy-start(f32[11216]{0:T(1024)} %copy-done.17) | copy-start | bytes 134596
  687.8 44.1 %collective-permute-start.36 = (bf16[2,576,729]{2,1,0:T(8,128)(2,1)}, bf16[2,576,729]{2,1,0:T(8,128)(2,1)}, u32[]{:S(2)}, u32[]{:S(2)}) collective-permute-start(bf16[2,576,729]{2,1,0:T(8,128)(2,1)} %get-tuple-element.374), channel_id=1, source_target_pairs={{0,1},{1,0},{2,3},{3,2},{4,5},{5,4},{6,7},{7,6},{8,9},{9,8},{10,11... | collective-permute-start | bytes 5038856 | tf_op jit(solution)/shard_map/ppermute | solution.py:1087
  707.2 39.4 %collective-permute-start.37 = (bf16[1,576,729]{2,1,0:T(8,128)(2,1)}, bf16[1,576,729]{2,1,0:T(8,128)(2,1)S(1)}, u32[]{:S(2)}, u32[]{:S(2)}) collective-permute-start(bf16[1,576,729]{2,1,0:T(8,128)(2,1)} %get-tuple-element.381), channel_id=1, source_target_pairs={{0,1},{1,0},{2,3},{3,2},{4,5},{5,4},{6,7},{7,6},{8,9},{9,8},{10,11... | collective-permute-start | bytes 2519432 | tf_op jit(solution)/shard_map/ppermute | solution.py:1087
  708.4 5.4 collective-permute-start.40
  708.5 5.3 collective-permute-start.39
  710.1 3.7 collective-permute-start.38
  746.6 10.4 %collective-permute-start.44 = (bf16[1152,1152]{1,0:T(8,128)(2,1)}, bf16[1152,1152]{1,0:T(8,128)(2,1)S(1)}, u32[]{:S(2)}, u32[]{:S(2)}) collective-permute-start(bf16[1152,1152]{1,0:T(8,128)(2,1)} %all-reduce.9.cloned.1.call-done.mine_ref), channel_id=1, source_target_pairs={{0,2},{2,0},{4,6},{6,4},{8,10},{10,8},{12,14},{14,12},{16,18},{18,... | collective-permute-start | bytes 7962632 | tf_op jit(solution)/shard_map/ppermute | solution.py:1091
  746.6 7.6 collective-permute-start.43
  748.1 7.3 collective-permute-start.42
  748.7 6.7 collective-permute-start.41
  (26 other events, 105.6 us)
Sparse Core Ops, SparseCore 0:
  48.4 58.1 all-gather.2
  109.3 83.7 all-gather.4
  365.2 118.0 all-reduce.6
  612.4 115.2 all-reduce.8

commit v3 on v2

--- a/solution.py
+++ b/solution.py
@@ -444,7 +444,7 @@
         ),
         input_output_aliases={8 + k: k for k in range(len(held))},
         compiler_params=params(1),
-        cost_estimate=cost(6 * seq * feat * width, 12 << 20),
+        cost_estimate=cost(6 * seq * feat * width, 12 << 20, 0, SHORT),
         name="first_norm",
     )(place, images, other, features, *weights, head_vectors, *held)
 
@@ -521,6 +521,7 @@
             4 * steps * heads * seq * seq * 256,
             steps * heads * head_dim * seq * 8,
             steps * heads * seq * seq,
+            SHORT if steps == 1 else COST_SHARE,
         ),
         name="mix",
     )(qkv, qkv, qkv, *held)
@@ -600,7 +601,7 @@
 
     resid = rows_ref[0].astype(F32) + dot_tn(w_ref[...], ctx_ref[0])
     resid += column(feature_ref, O_BIAS)
-    resid_ref[0] = resid
+    resid_ref[0] = resid.astype(BF16)
     normed, _ = column_stats(resid)
     low_ref[0] = (
         normed * column(feature_ref, LN2_GAIN) + column(feature_ref, LN2_BIAS)
@@ -624,7 +625,7 @@
     return pl.pallas_call(
         second_norm_kernel,
         out_shape=[
-            jax.ShapeDtypeStruct((count, feat, seq), F32),
+            jax.ShapeDtypeStruct((count, feat, seq), BF16),
             jax.ShapeDtypeStruct((count, feat, seq), BF16),
             jax.ShapeDtypeStruct((count, feat, seq), BF16),
             jax.ShapeDtypeStruct((1, feat), F32),
@@ -727,53 +728,70 @@
 
 
 def layer_kernel(
-    place_ref, act_own_ref, act_other_ref, w_own_ref, w_other_ref, resid_ref, b_ref, *rest, start, count
+    place_ref,
+    act_own_ref,
+    act_other_ref,
+    w_own_ref,
+    w_other_ref,
+    resid_ref,
+    b_ref,
+    out_ref,
+    send_ref,
+    last_ref,
 ):
-    out_ref, send_ref = rest[-2:]
+    step, count = pl.program_id(0), pl.num_programs(0)
     hidden = act_own_ref.shape[1]
     branch = dot_tn(w_own_ref[:hidden], act_own_ref[0])
     branch += dot_tn(w_other_ref[:hidden], act_other_ref[0])
-    flag = place_ref[2 + place_ref[0] * count + start + pl.program_id(0)].astype(F32)
-    result = (resid_ref[0] + branch + column(b_ref, FC2_BIAS)) * flag
+    flag = place_ref[2 + place_ref[0] * count + step].astype(F32)
+    result = (resid_ref[0].astype(F32) + branch + column(b_ref, FC2_BIAS)) * flag
     own, other = split_halves(place_ref[0] == 0, result)
     out_ref[0] = own.astype(BF16)
-    send_ref[0] = other.astype(BF16)
-
-
-def layer_result(place, act_own, act_other, w_own, w_other, resid, features, start, steps, held):
+    other = other.astype(BF16)
+
+    @pl.when(step < count - 1)
+    def _():
+        send_ref[0] = other
+
+    @pl.when(step == count - 1)
+    def _():
+        last_ref[0] = other
+
+
+def layer_result(place, act_own, act_other, w_own, w_other, resid, features):
     count, feat, seq = resid.shape
     hidden = act_own.shape[1]
-    full = image_block((hidden, seq), start)
+    full = image_block((hidden, seq))
     padded = 4 * quarter_rows(hidden)
-    held = [] if held is None else [held]
+    part = (1, feat // 2, seq)
     return pl.pallas_call(
-        functools.partial(layer_kernel, start=start, count=count),
+        layer_kernel,
         out_shape=[
             jax.ShapeDtypeStruct((2 * count, feat // 2, seq), BF16),
-            jax.ShapeDtypeStruct((steps, feat // 2, seq), BF16),
+            jax.ShapeDtypeStruct((count - 1, feat // 2, seq), BF16),
+            jax.ShapeDtypeStruct(part, BF16),
         ],
         grid_spec=pltpu.PrefetchScalarGridSpec(
             num_scalar_prefetch=1,
-            grid=(steps,),
+            grid=(count,),
             in_specs=[
                 full,
                 full,
                 once((hidden, feat)),
                 once((padded, feat), (1, 0)),
-                image_block((feat, seq), start),
+                image_block((feat, seq)),
                 once((feat, 8)),
-            ]
-            + [ANYWHERE] * len(held),
+            ],
             out_specs=[
-                pl.BlockSpec((1, feat // 2, seq), lambda i, p: (p[0] * count + start + i, 0, 0)),
-                image_block((feat // 2, seq)),
+                pl.BlockSpec(part, lambda i, p: (p[0] * count + i, 0, 0)),
+                pl.BlockSpec(part, lambda i, p: (jnp.minimum(i, count - 2), 0, 0)),
+                once(part),
             ],
         ),
-        input_output_aliases={7: 0} if held else {},
         compiler_params=params(1),
-        cost_estimate=cost(4 * steps * seq * feat * hidden, steps * (12 << 20), 0, LONG),
+        cost_estimate=cost(4 * count * seq * feat * hidden, count * (12 << 20), 0, LONG),
         name="layer_result",
-    )(place, act_own, act_other, w_own, w_other, resid, features, *held)
+    )(place, act_own, act_other, w_own, w_other, resid, features)
 
 
 def resid_back_kernel(
@@ -795,7 +813,7 @@
     hidden = back_own_ref.shape[1]
     grad_norm = dot_tn(w_own_ref[:hidden], back_own_ref[0])
     grad_norm += dot_tn(w_other_ref[:hidden], back_other_ref[0])
-    normed, inverse = column_stats(resid_ref[0])
+    normed, inverse = column_stats(resid_ref[0].astype(F32))
     scaled = grad_norm * column(gain_ref, LN2_GAIN)
     plain = jnp.mean(scaled, axis=0, keepdims=True)
     cross = jnp.mean(scaled * normed, axis=0, keepdims=True)
@@ -1197,17 +1215,17 @@
     block = quarter_rows(hidden)
 
     in_piece = other_weights([*in_weights, o_weight], spots, width // (spots // 4))
-    first, in_piece = lax.optimization_barrier((to_send(images, 0), in_piece))
-    in_piece = swap_tensor(in_piece)
+    first = to_send(images, 0)
+    in_piece, first = lax.optimization_barrier((in_piece, first))
     images_other = [swap_tensor(first)]
-    small_other = swap_tensor(after(small, first))
+    in_piece, small_other = swap_tensor(in_piece), swap_tensor(after(small, first))
     mlp_piece = other_weights([fc1_own, fc2_weight], spots, block // 2)
     next_image = to_send(images, 1)
-    next_image, mlp_piece, images_other[0] = lax.optimization_barrier(
-        (next_image, mlp_piece, images_other[0])
-    )
+    next_image, images_other[0], in_piece = lax.optimization_barrier(
+        (next_image, images_other[0], in_piece)
+    )
+    in_other = lax.all_gather(in_piece, "dp", axis=0, tiled=True)
     images_other.append(swap_tensor(next_image))
-    mlp_piece = swap_tensor(mlp_piece)
 
     def features_of(source):
         return source[:cut_q].reshape(6, half)
@@ -1239,8 +1257,8 @@
         )
         state = list(state)
         if index == 0:
-            in_piece, state[2] = lax.optimization_barrier((in_piece, state[2]))
-            in_other = lax.all_gather(in_piece, "dp", axis=0, tiled=True)
+            mlp_piece, state[2] = lax.optimization_barrier((mlp_piece, state[2]))
+            mlp_piece = swap_tensor(mlp_piece)
         if index == 1:
             mlp_piece, state[2] = lax.optimization_barrier((mlp_piece, state[2]))
             mlp_other = lax.all_gather(mlp_piece, "dp", axis=0, tiled=True)
@@ -1406,33 +1424,27 @@
     in_arrived.append(swap_tensor(in_send))
     late_other = swap_core(g_late)
 
-    def layers(start, steps, held):
-        return layer_result(
-            place, act_own, stage_other[0], fc2_weight, mlp_other, resid, features, start, steps, held
-        )
-
-    out_buffer, out_send, = layers(0, count - 1, None)
-    in_arrived[1], out_send, out_buffer, small_swapped = lax.optimization_barrier(
-        (in_arrived[1], out_send, out_buffer, small_swapped)
+    out_buffer, out_send, last_send = layer_result(
+        place, act_own, stage_other[0], fc2_weight, mlp_other, resid, features
+    )
+    in_arrived[1], out_send, out_buffer, small_swapped, late_other = lax.optimization_barrier(
+        (in_arrived[1], out_send, out_buffer, small_swapped, late_other)
     )
     small_grads += small_swapped
     out_arrived = [swap_tensor(out_send)]
-    out_buffer, out_send = layers(count - 1, 1, out_buffer)
-    out_send, late_other, fc1_other = lax.optimization_barrier((out_send, late_other, fc1_other))
-    out_arrived.append(swap_tensor(out_send))
-
     out_fc1 = widen(place, g_fc1, fc1_other, 2 * block, hidden, 4)
     input_grad = lax.dynamic_update_slice_in_dim(in_buffer, jnp.concatenate(in_arrived), far, 0)
     out_fc2 = widen(place, g_late, late_other, 2 * block, hidden, 4)
 
-    out_fc2, out_fc1, out_arrived[0] = lax.optimization_barrier((out_fc2, out_fc1, out_arrived[0]))
-    small_grads = exchange_sum(small_grads, (1, 2, 3))
-    out_fc2, input_grad = lax.optimization_barrier((out_fc2, input_grad))
-    out_fc2, out_arrived[1] = lax.optimization_barrier((out_fc2, out_arrived[1]))
-    g_qkv, small_grads, out_fc2 = lax.optimization_barrier((g_qkv, small_grads, out_fc2))
+    out_fc1, input_grad, small_grads = lax.optimization_barrier((out_fc1, input_grad, small_grads))
+    near = exchange_sum(small_grads, (1, 2, 3))
+    out_fc2, near = lax.optimization_barrier((out_fc2, near))
+    small_grads = exchange_sum(near, range(4, spots, 4))
+    g_qkv, small_grads, out_fc2, out_arrived[0] = lax.optimization_barrier(
+        (g_qkv, small_grads, out_fc2, out_arrived[0])
+    )
     qkv_other_core = swap_core(g_qkv)
-    layer_out = lax.dynamic_update_slice_in_dim(out_buffer, jnp.concatenate(out_arrived), far, 0)
-    small_grads = exchange_sum(small_grads, range(4, spots, 4))
+    out_arrived.append(swap_tensor(after(last_send, g_qkv)))
     g_feature = lax.dynamic_slice_in_dim(
         small_grads[: 6 * feat].reshape(6, feat), tensor * half, half, 1
     )
@@ -1441,6 +1453,8 @@
     )
 
     g_q, g_k, g_v, g_o = widen(place, g_qkv, qkv_other_core, width // 2, width, 1, 4)
+    g_q, out_arrived[1] = lax.optimization_barrier((g_q, out_arrived[1]))
+    layer_out = lax.dynamic_update_slice_in_dim(out_buffer, jnp.concatenate(out_arrived), far, 0)
     return (
         jnp.swapaxes(layer_out, 1, 2),
         jnp.swapaxes(input_grad, 1, 2),

time: 787 us -> 770 us (0.978)
  Pallas kernels: 592 us -> 574 us
  local copies, waits for them, and re-layouts: 20.4 us -> 31 us
    ppermute x22, waiting for transfers between devices: 54.3 us -> 34.4 us  [swap_tensor(): return lax.ppermute(value, 'tensor', [(0, 1), (1, 0)])]
    pallas_call x2 -> x1, Pallas kernels: 45.5 us -> 36.2 us  [layer_result(): pl.pallas_call(layer_kernel, out_shape=[jax.ShapeDtypeStruct((2 * count,...]
    ppermute x6, waiting for transfers between devices: 1.17 us -> 9.91 us  [exchange_sum(): total += lax.ppermute(value, 'dp', pairs)]
    pallas_call x4, Pallas kernels: 153 us -> 145 us  [hidden_stage(): pl.pallas_call(functools.partial(hidden_kernel, which=which), out_shape=[...]
  transfers between devices with their start and end apart: 49 -> 49, of which waited for: 9 -> 9; matrix products, arithmetic and copies ran while one was open for 7% -> 8% of each run, Pallas kernels for 69% -> 71%
where the time goes in v3:
time: 770 us; the launch traced here: 759 us
  Pallas kernels  574 us (75%)
  waiting for transfers between devices  50.6 us (7%)
  other arithmetic  47.1 us (6%)
  starting transfers between devices  41.1 us (5%)
  local copies, waits for them, and re-layouts  31 us (4%)
  between operations  14.7 us (2%)
    pallas_call x4, Pallas kernels, hidden_stage(): pl.pallas_call(functools.partial(hidden_kernel, which=which), out_shape=[...  145 us
    pallas_call x4, Pallas kernels, mix_back(): pl.pallas_call(functools.partial(mix_back_kernel, scale=1.0 / math.sqrt(h...  82.1 us
    pallas_call x4, Pallas kernels, mix(): pl.pallas_call(functools.partial(mix_kernel, scale=1.0 / math.sqrt(head_d...  58.2 us
    pallas_call x2, Pallas kernels, input_back(): pl.pallas_call(input_back_kernel, out_shape=[jax.ShapeDtypeStruct((2 * co...  49.4 us
    pallas_call x1, Pallas kernels, resid_back(): pl.pallas_call(resid_back_kernel, grid=(count,), out_shape=[jax.ShapeDtyp...  46.3 us
    pallas_call x2, Pallas kernels, project_back(): pl.pallas_call(project_back_kernel, out_shape=[part, part, jax.ShapeDtype...  38.8 us
    pallas_call x1, Pallas kernels, layer_result(): pl.pallas_call(layer_kernel, out_shape=[jax.ShapeDtypeStruct((2 * count,...  36.2 us
    ppermute x22, waiting for transfers between devices, swap_tensor(): return lax.ppermute(value, 'tensor', [(0, 1), (1, 0)])  34.4 us
  transfers between devices with their start and end apart: 49, of which 9 were waited for; matrix products, arithmetic and copies ran while one was open for 8% of the time, Pallas kernels for 71%

profile of v3, /device:TPU:0, one launch (start us, length us, event | category | flops | bytes accessed | tf_op | source)
XLA Modules:
  0.0 758.9 jit_solution(12916368001245348796)
XLA Ops:
  7.3 1.9 dynamic-slice_bitcast_fusion.3
  10.7 3.0 collective-permute-start
  13.8 26.8 %collective-permute-done.1 = bf16[144,1152]{1,0:T(8,128)(2,1)} collective-permute-done((bf16[144,1152]{1,0:T(8,128)(2,1)S(1)}, bf16[144,1152]{1,0:T(8,128)(2,1)}, u32[]{:S(2)}, u32[]{:S(2)}) %collective-permute-start.1) | collective-permute-done | bytes 331808 | tf_op jit(solution)/shard_map/ppermute | solution.py:1105
  40.7 3.5 concatenate.62
  44.2 1.8 collective-permute-start.3
  46.0 2.3 fusion
  52.6 10.2 %first_norm.3 = (bf16[3,1152,729]{2,1,0:T(8,128)(2,1)}, bf16[3,1152,729]{2,1,0:T(8,128)(2,1)}, bf16[3,24,72,729]{3,2,1,0:T(8,128)(2,1)}) custom-call(s32[8]{0:T(128)} %pad_add_fusion.place_ref, bf16[6,576,729]{2,1,0:T(8,128)(2,1)} %bitcast.42, bf16[1,576,729]{2,1,0:T(8,128)(2,1)} %copy-done.10, f32[1152,8]{1,0:T(8,128)} %convert_bitcast_fusion.feature_ref.gain_ref.b_ref, ...), custom_call_target="tpu_custom_call" | custom-call | flops 145118816 | bytes 629145 | tf_op jit(solution)/shard_map/first_norm/pallas_call | solution.py:419
  62.8 1.5 collective-permute-start.5
  64.3 10.3 %mix.4 = (bf16[3,16,72,729]{3,2,1,0:T(8,128)(2,1)}, f32[3,16,1,729]{3,2,1,0:T(1,128)}) custom-call(bf16[3,24,72,729]{3,2,1,0:T(8,128)(2,1)} %get-tuple-element.211.q_ref.k_ref.v_ref.rest_2_, bf16[3,24,72,729]{3,2,1,0:T(8,128)(2,1)} %get-tuple-element.211.q_ref.k_ref.v_ref.rest_2_, bf16[3,24,72,729]{3,2,1,0:T(8,128)(2,1)} %get-tuple-element.211.q_ref.k_ref.v_ref.rest_2_), custom_call_target="tpu_custom_call" | custom-call | flops 217678240 | bytes 167961 | tf_op jit(solution)/shard_map/mix/pallas_call | solution.py:504
  75.5 10.2 %first_norm.4 = (bf16[3,1152,729]{2,1,0:T(8,128)(2,1)}, bf16[3,1152,729]{2,1,0:T(8,128)(2,1)}, bf16[3,24,72,729]{3,2,1,0:T(8,128)(2,1)}) custom-call(s32[8]{0:T(128)} %pad_add_fusion.place_ref, bf16[6,576,729]{2,1,0:T(8,128)(2,1)} %bitcast.43, bf16[1,576,729]{2,1,0:T(8,128)(2,1)} %copy-done.9, ...), custom_call_target="tpu_custom_call", output_to_operand_aliasing={{0}: (8, {}), {1}: (9, {}), {2}: (10, {})} | custom-call | flops 145118816 | bytes 629145 | tf_op jit(solution)/shard_map/first_norm/pallas_call | solution.py:419
  87.2 2.9 dynamic-slice_bitcast_fusion
  90.8 2.1 copy.67
  92.9 10.2 %mix.5 = (bf16[3,16,72,729]{3,2,1,0:T(8,128)(2,1)}, f32[3,16,1,729]{3,2,1,0:T(1,128)}) custom-call(bf16[3,24,72,729]{3,2,1,0:T(8,128)(2,1)} %get-tuple-element.219.q_ref.k_ref.v_ref.rest_2_, bf16[3,24,72,729]{3,2,1,0:T(8,128)(2,1)} %get-tuple-element.219.q_ref.k_ref.v_ref.rest_2_, ...), custom_call_target="tpu_custom_call", output_to_operand_aliasing={{0}: (3, {}), {1}: (4, {})} | custom-call | flops 217678240 | bytes 167961 | tf_op jit(solution)/shard_map/mix/pallas_call | solution.py:504
  103.1 3.3 collective-permute-done.4.other_ref
  107.0 1.5 collective-permute-start.7
  109.0 10.1 %first_norm.5 = (bf16[3,1152,729]{2,1,0:T(8,128)(2,1)}, bf16[3,1152,729]{2,1,0:T(8,128)(2,1)}, bf16[3,24,72,729]{3,2,1,0:T(8,128)(2,1)}) custom-call(s32[8]{0:T(128)} %pad_add_fusion.place_ref, bf16[6,576,729]{2,1,0:T(8,128)(2,1)} %bitcast.44, bf16[1,576,729]{2,1,0:T(8,128)(2,1)} %copy-done.8, ...), custom_call_target="tpu_custom_call", output_to_operand_aliasing={{0}: (8, {}), {1}: (9, {}), {2}: (10, {})} | custom-call | flops 145118816 | bytes 629145 | tf_op jit(solution)/shard_map/first_norm/pallas_call | solution.py:419
  119.1 10.2 %mix.6 = (bf16[3,16,72,729]{3,2,1,0:T(8,128)(2,1)}, f32[3,16,1,729]{3,2,1,0:T(1,128)}) custom-call(bf16[3,24,72,729]{3,2,1,0:T(8,128)(2,1)} %get-tuple-element.227.q_ref.k_ref.v_ref, bf16[3,24,72,729]{3,2,1,0:T(8,128)(2,1)} %get-tuple-element.227.q_ref.k_ref.v_ref, ...), custom_call_target="tpu_custom_call", output_to_operand_aliasing={{0}: (3, {}), {1}: (4, {})} | custom-call | flops 217678240 | bytes 167961 | tf_op jit(solution)/shard_map/mix/pallas_call | solution.py:504
  129.3 15.1 %project.1.q_ref.k_ref.v_ref = bf16[3,24,72,729]{3,2,1,0:T(8,128)(2,1)} custom-call(bf16[3,1152,729]{2,1,0:T(8,128)(2,1)} %get-tuple-element.226.normed_ref, bf16[2304,1152]{1,0:T(8,128)(2,1)} %all-gather.3.cloned.1.call-done.q_ref.k_ref.v_ref.w_other_ref, bf16[2304,1152]{1,0:T(8,128)(2,1)} %all-gather.3.cloned.1.call-done.q_ref.k_ref.v_ref.w_other_ref, ...), custom_call_target="tpu_custom_call" | custom-call | flops 3482851840 | bytes 8388608 | tf_op jit(solution)/shard_map/project/pallas_call | solution.py:463
  144.3 27.5 %mix.7 = (bf16[3,16,72,729]{3,2,1,0:T(8,128)(2,1)}, f32[3,16,1,729]{3,2,1,0:T(1,128)}) custom-call(bf16[3,24,72,729]{3,2,1,0:T(8,128)(2,1)} %project.1.q_ref.k_ref.v_ref, bf16[3,24,72,729]{3,2,1,0:T(8,128)(2,1)} %project.1.q_ref.k_ref.v_ref, bf16[3,24,72,729]{3,2,1,0:T(8,128)(2,1)} %project.1.q_ref.k_ref.v_ref, ...), custom_call_target="tpu_custom_call", output_to_operand_aliasing={{0}: (3, {}), {1}: (4, {})} | custom-call | flops 5224277504 | bytes 4031078 | tf_op jit(solution)/shard_map/mix/pallas_call | solution.py:504
  172.8 22.4 %second_norm.1 = (bf16[3,1152,729]{2,1,0:T(8,128)(2,1)}, bf16[3,1152,729]{2,1,0:T(8,128)(2,1)}, bf16[3,1152,729]{2,1,0:T(8,128)(2,1)}, f32[1,1152]{1,0:T(1,128)}) custom-call(s32[8]{0:T(128)} %pad_add_fusion.place_ref, bf16[3,1152,729]{2,1,0:T(8,128)(2,1)} %bitcast.37, bf16[576,1152]{1,0:T(8,128)(2,1)} %w_own_ref.4, ...), custom_call_target="tpu_custom_call" | custom-call | flops 2321901056 | bytes 16777216 | tf_op jit(solution)/shard_map/second_norm/pallas_call | solution.py:625
  195.2 36.3 %hidden_stage.4 = (bf16[3,2152,729]{2,1,0:T(8,128)(2,1)}, bf16[3,2152,729]{2,1,0:T(8,128)(2,1)}, f32[2152,1]{1,0:T(8,128)}, bf16[1088,1152]{1,0:T(8,128)(2,1)}, bf16[1088,1152]{1,0:T(8,128)(2,1)}) custom-call(s32[8]{0:T(128)} %pad_add_fusion.place_ref, bf16[3,1152,729]{2,1,0:T(8,128)(2,1)} %get-tuple-element.243.low_ref, ...), custom_call_target="tpu_custom_call" | custom-call | flops 86748807168 | bytes 125829120 | tf_op jit(solution)/shard_map/hidden_stage/pallas_call | solution.py:695
  232.0 36.1 %hidden_stage.5 = (bf16[3,2152,729]{2,1,0:T(8,128)(2,1)}, bf16[3,2152,729]{2,1,0:T(8,128)(2,1)}, f32[2152,1]{1,0:T(8,128)}, bf16[1088,1152]{1,0:T(8,128)(2,1)}, bf16[1088,1152]{1,0:T(8,128)(2,1)}) custom-call(s32[8]{0:T(128)} %pad_add_fusion.place_ref, ...), custom_call_target="tpu_custom_call", output_to_operand_aliasing={{0}: (6, {}), {1}: (7, {}), {2}: (8, {})} | custom-call | flops 86748807168 | bytes 125829120 | tf_op jit(solution)/shard_map/hidden_stage/pallas_call | solution.py:695
  268.2 2.3 add_convert_fusion.8
  270.5 3.2 add_convert_fusion.3
  274.8 1.6 add_convert_fusion.4
  276.4 1.5 collective-permute-start.11
  277.9 36.3 %hidden_stage.6 = (bf16[3,2152,729]{2,1,0:T(8,128)(2,1)}, bf16[3,2152,729]{2,1,0:T(8,128)(2,1)}, f32[2152,1]{1,0:T(8,128)}, bf16[1088,1152]{1,0:T(8,128)(2,1)}, bf16[1088,1152]{1,0:T(8,128)(2,1)}) custom-call(s32[8]{0:T(128)} %pad_add_fusion.place_ref, bf16[3,1152,729]{2,1,0:T(8,128)(2,1)} %get-tuple-element.243.low_ref, ...), custom_call_target="tpu_custom_call" | custom-call | flops 86748807168 | bytes 125829120 | tf_op jit(solution)/shard_map/hidden_stage/pallas_call | solution.py:695
  314.8 1.5 collective-permute-start.14
  316.9 36.1 %hidden_stage.7 = (bf16[3,2152,729]{2,1,0:T(8,128)(2,1)}, bf16[3,2152,729]{2,1,0:T(8,128)(2,1)}, f32[2152,1]{1,0:T(8,128)}, bf16[1088,1152]{1,0:T(8,128)(2,1)}, bf16[1088,1152]{1,0:T(8,128)(2,1)}) custom-call(s32[8]{0:T(128)} %pad_add_fusion.place_ref, ...), custom_call_target="tpu_custom_call", output_to_operand_aliasing={{0}: (6, {}), {1}: (7, {}), {2}: (8, {})} | custom-call | flops 86748807168 | bytes 125829120 | tf_op jit(solution)/shard_map/hidden_stage/pallas_call | solution.py:695
  354.6 4.5 add_convert_fusion.1
  359.2 46.3 %resid_back.1 = (bf16[3,1152,729]{2,1,0:T(8,128)(2,1)}, f32[1,1152]{1,0:T(1,128)}, f32[1,1152]{1,0:T(1,128)}, f32[1,1152]{1,0:T(1,128)}) custom-call(bf16[3,2152,729]{2,1,0:T(8,128)(2,1)} %get-tuple-element.272.back_own_ref, bf16[3,2152,729]{2,1,0:T(8,128)(2,1)} %get-tuple-element.273.back_other_ref, bf16[2152,1152]{1,0:T(8,128)(2,1)} %bitcast.52, ...), custom_call_target="tpu_custom_call" | custom-call | flops 8674880512 | bytes 20971520 | tf_op jit(solution)/shard_map/resid_back/pallas_call | solution.py:841
  405.5 2.6 add_convert_fusion
  408.3 21.6 %context_back.1 = (bf16[3,1152,729]{2,1,0:T(8,128)(2,1)}, bf16[288,1152]{1,0:T(8,128)(2,1)}, bf16[288,1152]{1,0:T(8,128)(2,1)}, bf16[288,1152]{1,0:T(8,128)(2,1)}, bf16[288,1152]{1,0:T(8,128)(2,1)}) custom-call(s32[8]{0:T(128)} %pad_add_fusion.place_ref, bf16[3,1152,729]{2,1,0:T(8,128)(2,1)} %get-tuple-element.282.low_ref, bf16[3,1152,729]{2,1,0:T(8,128)(2,1)} %bitcast.38, ...), custom_call_target="tpu_custom_call" | custom-call | flops 4643802112 | bytes 10485760 | tf_op jit(solution)/shard_map/context_back/pallas_call | solution.py:907
  430.4 1.6 collective-permute-start.17
  432.0 38.2 %mix_back.4 = bf16[3,24,72,729]{3,2,1,0:T(8,128)(2,1)} custom-call(bf16[3,24,72,729]{3,2,1,0:T(8,128)(2,1)} %project.1.q_ref.k_ref.v_ref, bf16[3,24,72,729]{3,2,1,0:T(8,128)(2,1)} %project.1.q_ref.k_ref.v_ref, bf16[3,24,72,729]{3,2,1,0:T(8,128)(2,1)} %project.1.q_ref.k_ref.v_ref, bf16[3,16,72,729]{3,2,1,0:T(8,128)(2,1)} %get-tuple-element.237.out_ref, ...), custom_call_target="tpu_custom_call" | custom-call | flops 13060694016 | bytes 8062156 | tf_op jit(solution)/shard_map/mix_back/pallas_call | solution.py:556
  477.8 19.3 %project_back.2 = (bf16[864,1152]{1,0:T(8,128)(2,1)}, bf16[864,1152]{1,0:T(8,128)(2,1)}, f32[1728,1]{1,0:T(8,128)}) custom-call(s32[8]{0:T(128)} %pad_add_fusion.place_ref, bf16[3,1152,729]{2,1,0:T(8,128)(2,1)} %get-tuple-element.226.normed_ref, bf16[3,1728,729]{2,1,0:T(8,128)(2,1)} %bitcast.70), custom_call_target="tpu_custom_call" | custom-call | flops 3482851840 | bytes 8388608 | tf_op jit(solution)/shard_map/project_back/pallas_call | solution.py:960
  499.2 2.7 collective-permute-start.22
  501.9 14.5 %mix_back.5.rest_0_ = bf16[3,24,72,729]{3,2,1,0:T(8,128)(2,1)} custom-call(bf16[3,24,72,729]{3,2,1,0:T(8,128)(2,1)} %get-tuple-element.227.q_ref.k_ref.v_ref, bf16[3,24,72,729]{3,2,1,0:T(8,128)(2,1)} %get-tuple-element.227.q_ref.k_ref.v_ref, bf16[3,24,72,729]{3,2,1,0:T(8,128)(2,1)} %get-tuple-element.227.q_ref.k_ref.v_ref, ...), custom_call_target="tpu_custom_call" | custom-call | flops 544195584 | bytes 335923 | tf_op jit(solution)/shard_map/mix_back/pallas_call | solution.py:556
  516.6 2.3 add_convert_fusion.12
  518.9 2.3 add_convert_fusion.7
  523.1 14.8 %mix_back.6.rest_0_ = bf16[3,24,72,729]{3,2,1,0:T(8,128)(2,1)} custom-call(bf16[3,24,72,729]{3,2,1,0:T(8,128)(2,1)} %get-tuple-element.227.q_ref.k_ref.v_ref, bf16[3,24,72,729]{3,2,1,0:T(8,128)(2,1)} %get-tuple-element.227.q_ref.k_ref.v_ref, bf16[3,24,72,729]{3,2,1,0:T(8,128)(2,1)} %get-tuple-element.227.q_ref.k_ref.v_ref, ...), custom_call_target="tpu_custom_call", output_to_operand_aliasing={{}: (6, {})} | custom-call | flops 544195584 | bytes 335923 | tf_op jit(solution)/shard_map/mix_back/pallas_call | solution.py:556
  541.1 1.6 reduce.6
  544.6 14.6 %mix_back.7 = bf16[3,24,72,729]{3,2,1,0:T(8,128)(2,1)} custom-call(bf16[3,24,72,729]{3,2,1,0:T(8,128)(2,1)} %get-tuple-element.227.q_ref.k_ref.v_ref, bf16[3,24,72,729]{3,2,1,0:T(8,128)(2,1)} %get-tuple-element.227.q_ref.k_ref.v_ref, bf16[3,24,72,729]{3,2,1,0:T(8,128)(2,1)} %get-tuple-element.227.q_ref.k_ref.v_ref, ...), custom_call_target="tpu_custom_call", output_to_operand_aliasing={{}: (6, {})} | custom-call | flops 544195584 | bytes 335923 | tf_op jit(solution)/shard_map/mix_back/pallas_call | solution.py:556
  559.5 1.5 collective-permute-start.29
  561.0 19.5 %project_back.3 = (bf16[864,1152]{1,0:T(8,128)(2,1)}, bf16[864,1152]{1,0:T(8,128)(2,1)}, f32[1728,1]{1,0:T(8,128)}) custom-call(s32[8]{0:T(128)} %pad_add_fusion.place_ref, bf16[3,1152,729]{2,1,0:T(8,128)(2,1)} %get-tuple-element.226.normed_ref, bf16[3,1728,729]{2,1,0:T(8,128)(2,1)} %bitcast.39), custom_call_target="tpu_custom_call" | custom-call | flops 3482851840 | bytes 8388608 | tf_op jit(solution)/shard_map/project_back/pallas_call | solution.py:960
  582.6 19.5 %input_back.2 = (bf16[6,576,729]{2,1,0:T(8,128)(2,1)}, bf16[1,576,729]{2,1,0:T(8,128)(2,1)}, f32[1,1152]{1,0:T(1,128)}, f32[1,1152]{1,0:T(1,128)}) custom-call(s32[8]{0:T(128)} %pad_add_fusion.place_ref, bf16[3,1728,729]{2,1,0:T(8,128)(2,1)} %bitcast.40, bf16[3,1728,729]{2,1,0:T(8,128)(2,1)} %bitcast.71, bf16[576,1152]{1,0:T(8,128)(2,1)} %bitcast.56, ...), custom_call_target="tpu_custom_call" | custom-call | flops 23219011584 | bytes 79691776 | tf_op jit(solution)/shard_map/input_back/pallas_call | solution.py:1024
  602.1 2.8 add_convert_fusion.2
  604.9 1.7 pad_maximum_fusion
  607.3 29.9 %input_back.3 = (bf16[6,576,729]{2,1,0:T(8,128)(2,1)}, bf16[2,576,729]{2,1,0:T(8,128)(2,1)}, f32[1,1152]{1,0:T(1,128)}, f32[1,1152]{1,0:T(1,128)}) custom-call(s32[8]{0:T(128)} %pad_add_fusion.place_ref, bf16[3,1728,729]{2,1,0:T(8,128)(2,1)} %bitcast.41, bf16[3,1728,729]{2,1,0:T(8,128)(2,1)} %bitcast.72, ...), custom_call_target="tpu_custom_call", output_to_operand_aliasing={{0}: (10, {})} | custom-call | flops 46438023168 | bytes 125829120 | tf_op jit(solution)/shard_map/input_back/pallas_call | solution.py:1024
  638.7 1.5 collective-permute-start.34
  642.0 36.2 %layer_result.1 = (bf16[6,576,729]{2,1,0:T(8,128)(2,1)}, bf16[2,576,729]{2,1,0:T(8,128)(2,1)}, bf16[1,576,729]{2,1,0:T(8,128)(2,1)}) custom-call(s32[8]{0:T(128)} %pad_add_fusion.place_ref, bf16[3,2152,729]{2,1,0:T(8,128)(2,1)} %get-tuple-element.357.act_own_ref, bf16[3,2152,729]{2,1,0:T(8,128)(2,1)} %get-tuple-element.358.act_other_ref, ...), custom_call_target="tpu_custom_call" | custom-call | flops 86748807168 | bytes 150994944 | tf_op jit(solution)/shard_map/layer_result/pallas_call | solution.py:767
  678.2 4.0 collective-permute-done.33
  682.8 9.1 %widen.4 = f32[2152,1152]{1,0:T(8,128)} custom-call(s32[8]{0:T(128)} %pad_add_fusion.place_ref, bf16[1088,1152]{1,0:T(8,128)(2,1)} %all-reduce.7.cloned.1.call-done.mine_ref, bf16[1088,1152]{1,0:T(8,128)(2,1)} %collective-permute-done.23.other_ref), custom_call_target="tpu_custom_call" | custom-call | bytes 991641 | tf_op jit(solution)/shard_map/widen/pallas_call | solution.py:1085
  692.0 3.2 maximum_dynamic-update-slice_fusion
  695.3 1.5 collective-permute-start.37
  697.1 8.8 %widen.3 = f32[2152,1152]{1,0:T(8,128)} custom-call(s32[8]{0:T(128)} %pad_add_fusion.place_ref, bf16[1088,1152]{1,0:T(8,128)(2,1)} %copy-done, bf16[1088,1152]{1,0:T(8,128)(2,1)} %copy-done.3), custom_call_target="tpu_custom_call" | custom-call | bytes 991641 | tf_op jit(solution)/shard_map/widen/pallas_call | solution.py:1085
  706.0 1.5 collective-permute-start.41
  708.0 2.4 collective-permute-start.39
  710.4 3.4 collective-permute-done.41
  713.8 6.5 collective-permute-done.40
  721.0 5.1 all-reduce.9.cloned.1.call-done.mine_ref
  734.6 1.7 dynamic-slice_reduce_fusion.1
  737.7 11.1 %widen.5 = (f32[576,1152]{1,0:T(8,128)}, f32[576,1152]{1,0:T(8,128)}, f32[576,1152]{1,0:T(8,128)}, f32[576,1152]{1,0:T(8,128)}) custom-call(s32[8]{0:T(128)} %pad_add_fusion.place_ref, bf16[1152,1152]{1,0:T(8,128)(2,1)} %all-reduce.9.cloned.1.call-done.mine_ref, bf16[1152,1152]{1,0:T(8,128)(2,1)} %copy-done.1), custom_call_target="tpu_custom_call" | custom-call | bytes 1061683 | tf_op jit(solution)/shard_map/widen/pallas_call | solution.py:1085
  748.9 3.2 maximum_dynamic-update-slice_fusion.1
  (212 shorter events, 51.2 us)
Async XLA Ops:
  7.2 122.1 %all-gather.3.cloned.1.call-start = ((), (), s32[]{:S(2)}) async-start(), calls=%async_computation | async-start | bytes 5640192 | tf_op jit(solution)/shard_map/all_gather | solution.py:1227
  7.3 33.4 %copy-start.23 = (bf16[576]{0:T(1024)(128)(2,1)S(1)}, bf16[576]{0:T(1024)(128)(2,1)}, u32[]{:S(2)}) copy-start(bf16[576]{0:T(1024)(128)(2,1)} %param.21) | copy-start | bytes 3460
  7.3 33.4 %copy-start.24 = (bf16[576]{0:T(1024)(128)(2,1)S(1)}, bf16[576]{0:T(1024)(128)(2,1)}, u32[]{:S(2)}) copy-start(bf16[576]{0:T(1024)(128)(2,1)} %param.22) | copy-start | bytes 3460
  7.3 33.4 %copy-start.25 = (bf16[576]{0:T(1024)(128)(2,1)S(1)}, bf16[576]{0:T(1024)(128)(2,1)}, u32[]{:S(2)}) copy-start(bf16[576]{0:T(1024)(128)(2,1)} %param.29) | copy-start | bytes 3460
  7.3 33.4 %copy-start.26 = (bf16[576]{0:T(1024)(128)(2,1)S(1)}, bf16[576]{0:T(1024)(128)(2,1)}, u32[]{:S(2)}) copy-start(bf16[576]{0:T(1024)(128)(2,1)} %param.30) | copy-start | bytes 3460
  10.7 29.9 %collective-permute-start = (bf16[1,576,729]{2,1,0:T(8,128)(2,1)S(1)}, bf16[1,576,729]{2,1,0:T(8,128)(2,1)S(1)}, u32[]{:S(2)}, u32[]{:S(2)}) collective-permute-start(bf16[1,576,729]{2,1,0:T(8,128)(2,1)S(1)} %get-tuple-element.205), channel_id=1, source_target_pairs={{0,1},{1,0},{2,3},{3,2},{4,5},{5,4},{6,7},{7,6},{8,9},{9,8},{10,11... | collective-permute-start | bytes 2519432 | tf_op jit(solution)/shard_map/ppermute | solution.py:1105
  13.7 26.9 %collective-permute-start.1 = (bf16[144,1152]{1,0:T(8,128)(2,1)S(1)}, bf16[144,1152]{1,0:T(8,128)(2,1)}, u32[]{:S(2)}, u32[]{:S(2)}) collective-permute-start(bf16[144,1152]{1,0:T(8,128)(2,1)S(1)} %bitcast_select_fusion), channel_id=1, source_target_pairs={{0,1},{1,0},{2,3},{3,2},{4,5},{5,4},{6,7},{7,6},{8,9},{9,8},{10,11... | collective-permute-start | bytes 995336 | tf_op jit(solution)/shard_map/ppermute | solution.py:1105
  40.6 7.7 %copy-start.10 = (bf16[1,576,729]{2,1,0:T(8,128)(2,1)}, bf16[1,576,729]{2,1,0:T(8,128)(2,1)S(1)}, u32[]{:S(2)}) copy-start(bf16[1,576,729]{2,1,0:T(8,128)(2,1)S(1)} %collective-permute-done.other_ref) | copy-start | bytes 2519428
  40.6 154.6 %all-gather.5.cloned.1.call-start = ((), (), s32[]{:S(2)}) async-start(), calls=%async_computation.1 | async-start | bytes 10653696 | tf_op jit(solution)/shard_map/all_gather | solution.py:1264
  44.2 4.9 collective-permute-start.3
  51.1 23.4 %collective-permute-start.2 = (bf16[1,576,729]{2,1,0:T(8,128)(2,1)S(1)}, bf16[1,576,729]{2,1,0:T(8,128)(2,1)S(1)}, u32[]{:S(2)}, u32[]{:S(2)}) collective-permute-start(bf16[1,576,729]{2,1,0:T(8,128)(2,1)S(1)} %get-tuple-element.207), channel_id=1, source_target_pairs={{0,1},{1,0},{2,3},{3,2},{4,5},{5,4},{6,7},{7,6},{8,9},{9,8},{10,11... | collective-permute-start | bytes 2519432 | tf_op jit(solution)/shard_map/ppermute | solution.py:1105
  52.6 10.2 %copy-start.18 = (bf16[272,1152]{1,0:T(8,128)(2,1)S(1)}, bf16[272,1152]{1,0:T(8,128)(2,1)}, u32[]{:S(2)}) copy-start(bf16[272,1152]{1,0:T(8,128)(2,1)} %fusion) | copy-start | bytes 1880068
  62.8 22.9 %collective-permute-start.5 = (bf16[272,1152]{1,0:T(8,128)(2,1)S(1)}, bf16[272,1152]{1,0:T(8,128)(2,1)S(1)}, u32[]{:S(2)}, u32[]{:S(2)}) collective-permute-start(bf16[272,1152]{1,0:T(8,128)(2,1)S(1)} %copy-done.18), channel_id=1, source_target_pairs={{0,1},{1,0},{2,3},{3,2},{4,5},{5,4},{6,7},{7,6},{8,9},{9,8},{10,11... | collective-permute-start | bytes 1880072 | tf_op jit(solution)/shard_map/ppermute | solution.py:1105
  86.5 410.7 %all-reduce.7.cloned.1.call-start = ((), (), s32[]{:S(2)}) async-start(), calls=%async_computation.2 | async-start | bytes 5013504 | tf_op jit(solution)/shard_map/psum | solution.py:1322
  86.7 19.7 %collective-permute-start.4 = (bf16[1,576,729]{2,1,0:T(8,128)(2,1)S(1)}, bf16[1,576,729]{2,1,0:T(8,128)(2,1)S(1)}, u32[]{:S(2)}, u32[]{:S(2)}) collective-permute-start(bf16[1,576,729]{2,1,0:T(8,128)(2,1)S(1)} %get-tuple-element.213), channel_id=1, source_target_pairs={{0,1},{1,0},{2,3},{3,2},{4,5},{5,4},{6,7},{7,6},{8,9},{9,8},{10,11... | collective-permute-start | bytes 2519432 | tf_op jit(solution)/shard_map/ppermute | solution.py:1105
  106.4 65.4 %collective-permute-start.6 = (bf16[1,576,729]{2,1,0:T(8,128)(2,1)}, bf16[1,576,729]{2,1,0:T(8,128)(2,1)S(1)}, u32[]{:S(2)}, u32[]{:S(2)}) collective-permute-start(bf16[1,576,729]{2,1,0:T(8,128)(2,1)} %get-tuple-element.234), channel_id=1, source_target_pairs={{0,1},{1,0},{2,3},{3,2},{4,5},{5,4},{6,7},{7,6},{8,9},{9,8},{10,11... | collective-permute-start | bytes 2519432 | tf_op jit(solution)/shard_map/ppermute | solution.py:1105
  107.0 64.9 %collective-permute-start.7 = (bf16[1,576,729]{2,1,0:T(8,128)(2,1)S(1)}, bf16[1,576,729]{2,1,0:T(8,128)(2,1)}, u32[]{:S(2)}, u32[]{:S(2)}) collective-permute-start(bf16[1,576,729]{2,1,0:T(8,128)(2,1)S(1)} %get-tuple-element.235), channel_id=1, source_target_pairs={{0,1},{1,0},{2,3},{3,2},{4,5},{5,4},{6,7},{7,6},{8,9},{9,8},{10,11... | collective-permute-start | bytes 2519432 | tf_op jit(solution)/shard_map/ppermute | solution.py:1105
  108.5 63.4 %collective-permute-start.8 = (bf16[1,576,729]{2,1,0:T(8,128)(2,1)S(1)}, bf16[1,576,729]{2,1,0:T(8,128)(2,1)}, u32[]{:S(2)}, u32[]{:S(2)}) collective-permute-start(bf16[1,576,729]{2,1,0:T(8,128)(2,1)S(1)} %get-tuple-element.236), channel_id=1, source_target_pairs={{0,1},{1,0},{2,3},{3,2},{4,5},{5,4},{6,7},{7,6},{8,9},{9,8},{10,11... | collective-permute-start | bytes 2519432 | tf_op jit(solution)/shard_map/ppermute | solution.py:1105
  231.5 42.1 %collective-permute-start.9 = (bf16[1088,1152]{1,0:T(8,128)(2,1)}, bf16[1088,1152]{1,0:T(8,128)(2,1)S(1)}, u32[]{:S(2)}, u32[]{:S(2)}) collective-permute-start(bf16[1088,1152]{1,0:T(8,128)(2,1)} %get-tuple-element.250), channel_id=1, source_target_pairs={{0,2},{2,0},{4,6},{6,4},{8,10},{10,8},{12,14},{14,12},{16,18},{18,... | collective-permute-start | bytes 7520264 | tf_op jit(solution)/shard_map/ppermute | solution.py:1109
  231.5 36.6 %collective-permute-start.10 = (bf16[1088,1152]{1,0:T(8,128)(2,1)}, bf16[1088,1152]{1,0:T(8,128)(2,1)S(1)}, u32[]{:S(2)}, u32[]{:S(2)}) collective-permute-start(bf16[1088,1152]{1,0:T(8,128)(2,1)} %get-tuple-element.252), channel_id=1, source_target_pairs={{0,2},{2,0},{4,6},{6,4},{8,10},{10,8},{12,14},{14,12},{16,18},{18,... | collective-permute-start | bytes 7520264 | tf_op jit(solution)/shard_map/ppermute | solution.py:1109
  276.4 38.5 %collective-permute-start.11 = (bf16[720,1152]{1,0:T(8,128)(2,1)}, bf16[720,1152]{1,0:T(8,128)(2,1)}, u32[]{:S(2)}, u32[]{:S(2)}) collective-permute-start(bf16[720,1152]{1,0:T(8,128)(2,1)} %add_convert_fusion.4), channel_id=1, source_target_pairs={{0,1},{1,0},{2,3},{3,2},{4,5},{5,4},{6,7},{7,6},{8,9},{9,8},{10,11... | collective-permute-start | bytes 4976648 | tf_op jit(solution)/shard_map/ppermute | solution.py:1105
  314.2 40.4 %collective-permute-start.12 = (bf16[1088,1152]{1,0:T(8,128)(2,1)}, bf16[1088,1152]{1,0:T(8,128)(2,1)S(1)}, u32[]{:S(2)}, u32[]{:S(2)}) collective-permute-start(bf16[1088,1152]{1,0:T(8,128)(2,1)} %get-tuple-element.263), channel_id=1, source_target_pairs={{0,2},{2,0},{4,6},{6,4},{8,10},{10,8},{12,14},{14,12},{16,18},{18,... | collective-permute-start | bytes 7520264 | tf_op jit(solution)/shard_map/ppermute | solution.py:1109
  314.2 44.9 %collective-permute-start.15 = (bf16[1088,1152]{1,0:T(8,128)(2,1)}, bf16[1088,1152]{1,0:T(8,128)(2,1)S(1)}, u32[]{:S(2)}, u32[]{:S(2)}) collective-permute-start(bf16[1088,1152]{1,0:T(8,128)(2,1)} %get-tuple-element.270), channel_id=1, source_target_pairs={{0,2},{2,0},{4,6},{6,4},{8,10},{10,8},{12,14},{14,12},{16,18},{18,... | collective-permute-start | bytes 7520264 | tf_op jit(solution)/shard_map/ppermute | solution.py:1109
  314.8 38.1 %collective-permute-start.14 = (bf16[352,1152]{1,0:T(8,128)(2,1)}, bf16[352,1152]{1,0:T(8,128)(2,1)}, u32[]{:S(2)}, u32[]{:S(2)}) collective-permute-start(bf16[352,1152]{1,0:T(8,128)(2,1)} %add_convert_fusion.8), channel_id=1, source_target_pairs={{0,1},{1,0},{2,3},{3,2},{4,5},{5,4},{6,7},{7,6},{8,9},{9,8},{10,11... | collective-permute-start | bytes 2433032 | tf_op jit(solution)/shard_map/ppermute | solution.py:1105
  316.3 36.8 %collective-permute-start.13 = (bf16[368,1152]{1,0:T(8,128)(2,1)}, bf16[368,1152]{1,0:T(8,128)(2,1)S(1)}, u32[]{:S(2)}, u32[]{:S(2)}) collective-permute-start(bf16[368,1152]{1,0:T(8,128)(2,1)} %add_convert_fusion.6), channel_id=1, source_target_pairs={{0,1},{1,0},{2,3},{3,2},{4,5},{5,4},{6,7},{7,6},{8,9},{9,8},{10,11... | collective-permute-start | bytes 2543624 | tf_op jit(solution)/shard_map/ppermute | solution.py:1105
  353.1 52.4 %collective-permute-start.16 = (bf16[736,1152]{1,0:T(8,128)(2,1)}, bf16[736,1152]{1,0:T(8,128)(2,1)}, u32[]{:S(2)}, u32[]{:S(2)}) collective-permute-start(bf16[736,1152]{1,0:T(8,128)(2,1)} %add_convert_fusion.3), channel_id=1, source_target_pairs={{0,1},{1,0},{2,3},{3,2},{4,5},{5,4},{6,7},{7,6},{8,9},{9,8},{10,11... | collective-permute-start | bytes 5087240 | tf_op jit(solution)/shard_map/ppermute | solution.py:1105
  359.1 367.0 %all-reduce.9.cloned.1.call-start = ((), (), s32[]{:S(2)}) async-start(), calls=%async_computation.3 | async-start | bytes 5308416 | tf_op jit(solution)/shard_map/psum | solution.py:1413
  359.2 46.4 %copy-start.2 = (bf16[1088,1152]{1,0:T(8,128)(2,1)S(1)}, bf16[1088,1152]{1,0:T(8,128)(2,1)}, u32[]{:S(2)}) copy-start(bf16[1088,1152]{1,0:T(8,128)(2,1)} %get-tuple-element.278) | copy-start | bytes 7520260
  429.9 40.3 %collective-permute-start.18 = (bf16[288,1152]{1,0:T(8,128)(2,1)}, bf16[288,1152]{1,0:T(8,128)(2,1)S(1)}, u32[]{:S(2)}, u32[]{:S(2)}) collective-permute-start(bf16[288,1152]{1,0:T(8,128)(2,1)} %get-tuple-element.289), channel_id=1, source_target_pairs={{0,2},{2,0},{4,6},{6,4},{8,10},{10,8},{12,14},{14,12},{16,18},{18,... | collective-permute-start | bytes 1990664 | tf_op jit(solution)/shard_map/ppermute | solution.py:1109
  429.9 42.4 %collective-permute-start.19 = (bf16[288,1152]{1,0:T(8,128)(2,1)}, bf16[288,1152]{1,0:T(8,128)(2,1)S(1)}, u32[]{:S(2)}, u32[]{:S(2)}) collective-permute-start(bf16[288,1152]{1,0:T(8,128)(2,1)} %get-tuple-element.291), channel_id=1, source_target_pairs={{0,2},{2,0},{4,6},{6,4},{8,10},{10,8},{12,14},{14,12},{16,18},{18,... | collective-permute-start | bytes 1990664 | tf_op jit(solution)/shard_map/ppermute | solution.py:1109
  430.4 44.2 %collective-permute-start.17 = (bf16[544,1152]{1,0:T(8,128)(2,1)S(1)}, bf16[544,1152]{1,0:T(8,128)(2,1)S(1)}, u32[]{:S(2)}, u32[]{:S(2)}) collective-permute-start(bf16[544,1152]{1,0:T(8,128)(2,1)S(1)} %get-tuple-element.286), channel_id=1, source_target_pairs={{0,4},{2,6},{4,0},{6,2},{8,12},{10,14},{12,8},{14,10},{16,20},{18,... | collective-permute-start | bytes 3760136 | tf_op jit(solution)/shard_map/ppermute | solution.py:1141
  432.0 39.1 %copy-start.14 = (bf16[288,1152]{1,0:T(8,128)(2,1)S(1)}, bf16[288,1152]{1,0:T(8,128)(2,1)}, u32[]{:S(2)}) copy-start(bf16[288,1152]{1,0:T(8,128)(2,1)} %get-tuple-element.288) | copy-start | bytes 1990660
  475.9 21.3 %collective-permute-start.20 = (bf16[288,1152]{1,0:T(8,128)(2,1)S(1)}, bf16[288,1152]{1,0:T(8,128)(2,1)}, u32[]{:S(2)}, u32[]{:S(2)}) collective-permute-start(bf16[288,1152]{1,0:T(8,128)(2,1)S(1)} %add_convert_fusion.10), channel_id=1, source_target_pairs={{0,1},{1,0},{2,3},{3,2},{4,5},{5,4},{6,7},{7,6},{8,9},{9,8},{10,11... | collective-permute-start | bytes 1990664 | tf_op jit(solution)/shard_map/ppermute | solution.py:1105
  476.4 20.7 %collective-permute-start.21 = (bf16[272,1152]{1,0:T(8,128)(2,1)}, bf16[272,1152]{1,0:T(8,128)(2,1)S(1)}, u32[]{:S(2)}, u32[]{:S(2)}) collective-permute-start(bf16[272,1152]{1,0:T(8,128)(2,1)} %get-tuple-element.299), channel_id=1, source_target_pairs={{0,8},{2,10},{4,12},{6,14},{8,0},{10,2},{12,4},{14,6},{16,24},{18,... | collective-permute-start | bytes 1880072 | tf_op jit(solution)/shard_map/ppermute | solution.py:1141
  497.2 19.4 %collective-permute-start.24 = (bf16[864,1152]{1,0:T(8,128)(2,1)}, bf16[864,1152]{1,0:T(8,128)(2,1)}, u32[]{:S(2)}, u32[]{:S(2)}) collective-permute-start(bf16[864,1152]{1,0:T(8,128)(2,1)} %get-tuple-element.310), channel_id=1, source_target_pairs={{0,2},{2,0},{4,6},{6,4},{8,10},{10,8},{12,14},{14,12},{16,18},{18,... | collective-permute-start | bytes 5971976 | tf_op jit(solution)/shard_map/ppermute | solution.py:1109
  497.2 24.0 %collective-permute-start.23 = (bf16[1088,1152]{1,0:T(8,128)(2,1)}, bf16[1088,1152]{1,0:T(8,128)(2,1)}, u32[]{:S(2)}, u32[]{:S(2)}) collective-permute-start(bf16[1088,1152]{1,0:T(8,128)(2,1)} %all-reduce.7.cloned.1.call-done.mine_ref), channel_id=1, source_target_pairs={{0,2},{2,0},{4,6},{6,4},{8,10},{10,8},{12,14},{14,12},{16,18},{18,... | collective-permute-start | bytes 7520264 | tf_op jit(solution)/shard_map/ppermute | solution.py:1109
  499.2 17.4 %copy-start.5 = (bf16[864,1152]{1,0:T(8,128)(2,1)S(1)}, bf16[864,1152]{1,0:T(8,128)(2,1)}, u32[]{:S(2)}) copy-start(bf16[864,1152]{1,0:T(8,128)(2,1)} %get-tuple-element.309) | copy-start | bytes 5971972
  499.2 17.2 %collective-permute-start.22 = (bf16[136,1152]{1,0:T(8,128)(2,1)S(1)}, bf16[136,1152]{1,0:T(8,128)(2,1)S(1)}, u32[]{:S(2)}, u32[]{:S(2)}) collective-permute-start(bf16[136,1152]{1,0:T(8,128)(2,1)S(1)} %get-tuple-element.304), channel_id=1, source_target_pairs={{0,16},{2,18},{4,20},{6,22},{8,24},{10,26},{12,28},{14,30},{16,0},... | collective-permute-start | bytes 940040 | tf_op jit(solution)/shard_map/ppermute | solution.py:1141
  521.2 17.7 %collective-permute-start.25 = (bf16[256,1152]{1,0:T(8,128)(2,1)S(1)}, bf16[256,1152]{1,0:T(8,128)(2,1)}, u32[]{:S(2)}, u32[]{:S(2)}) collective-permute-start(bf16[256,1152]{1,0:T(8,128)(2,1)S(1)} %get-tuple-element.312), channel_id=1, source_target_pairs={{0,1},{1,0},{2,3},{3,2},{4,5},{5,4},{6,7},{7,6},{8,9},{9,8},{10,11... | collective-permute-start | bytes 1769480 | tf_op jit(solution)/shard_map/ppermute | solution.py:1105
  522.6 16.3 %collective-permute-start.26 = (bf16[136,1152]{1,0:T(8,128)(2,1)S(1)}, bf16[136,1152]{1,0:T(8,128)(2,1)S(1)}, u32[]{:S(2)}, u32[]{:S(2)}) collective-permute-start(bf16[136,1152]{1,0:T(8,128)(2,1)S(1)} %add_convert_fusion.14), channel_id=1, source_target_pairs={{0,16},{2,18},{4,20},{6,22},{8,24},{10,26},{12,28},{14,30},{16,0},... | collective-permute-start | bytes 940040 | tf_op jit(solution)/shard_map/ppermute | solution.py:1141
  539.0 20.2 %collective-permute-start.28 = (bf16[272,1152]{1,0:T(8,128)(2,1)S(1)}, bf16[272,1152]{1,0:T(8,128)(2,1)S(1)}, u32[]{:S(2)}, u32[]{:S(2)}) collective-permute-start(bf16[272,1152]{1,0:T(8,128)(2,1)S(1)} %pad_maximum_fusion.3), channel_id=1, source_target_pairs={{0,8},{2,10},{4,12},{6,14},{8,0},{10,2},{12,4},{14,6},{16,24},{18,... | collective-permute-start | bytes 1880072 | tf_op jit(solution)/shard_map/ppermute | solution.py:1141
  540.5 18.7 %collective-permute-start.27 = (bf16[256,1152]{1,0:T(8,128)(2,1)}, bf16[256,1152]{1,0:T(8,128)(2,1)}, u32[]{:S(2)}, u32[]{:S(2)}) collective-permute-start(bf16[256,1152]{1,0:T(8,128)(2,1)} %get-tuple-element.319), channel_id=1, source_target_pairs={{0,1},{1,0},{2,3},{3,2},{4,5},{5,4},{6,7},{7,6},{8,9},{9,8},{10,11... | collective-permute-start | bytes 1769480 | tf_op jit(solution)/shard_map/ppermute | solution.py:1105
  559.5 23.2 %collective-permute-start.29 = (bf16[352,1152]{1,0:T(8,128)(2,1)}, bf16[352,1152]{1,0:T(8,128)(2,1)}, u32[]{:S(2)}, u32[]{:S(2)}) collective-permute-start(bf16[352,1152]{1,0:T(8,128)(2,1)} %add_convert_fusion.7), channel_id=1, source_target_pairs={{0,1},{1,0},{2,3},{3,2},{4,5},{5,4},{6,7},{7,6},{8,9},{9,8},{10,11... | collective-permute-start | bytes 2433032 | tf_op jit(solution)/shard_map/ppermute | solution.py:1105
  582.0 58.2 %collective-permute-start.32 = (bf16[544,1152]{1,0:T(8,128)(2,1)S(1)}, bf16[544,1152]{1,0:T(8,128)(2,1)S(1)}, u32[]{:S(2)}, u32[]{:S(2)}) collective-permute-start(bf16[544,1152]{1,0:T(8,128)(2,1)S(1)} %pad_maximum_fusion.2), channel_id=1, source_target_pairs={{0,4},{2,6},{4,0},{6,2},{8,12},{10,14},{12,8},{14,10},{16,20},{18,... | collective-permute-start | bytes 3760136 | tf_op jit(solution)/shard_map/ppermute | solution.py:1141
  582.6 19.5 %collective-permute-start.30 = (bf16[864,1152]{1,0:T(8,128)(2,1)}, bf16[864,1152]{1,0:T(8,128)(2,1)}, u32[]{:S(2)}, u32[]{:S(2)}) collective-permute-start(bf16[864,1152]{1,0:T(8,128)(2,1)} %get-tuple-element.340), channel_id=1, source_target_pairs={{0,2},{2,0},{4,6},{6,4},{8,10},{10,8},{12,14},{14,12},{16,18},{18,... | collective-permute-start | bytes 5971976 | tf_op jit(solution)/shard_map/ppermute | solution.py:1109
  582.6 19.5 %copy-start.6 = (bf16[864,1152]{1,0:T(8,128)(2,1)S(1)}, bf16[864,1152]{1,0:T(8,128)(2,1)}, u32[]{:S(2)}) copy-start(bf16[864,1152]{1,0:T(8,128)(2,1)} %get-tuple-element.339) | copy-start | bytes 5971972
  606.6 30.6 %copy-start.34 = (f32[1,1152]{1,0:T(1,128)S(1)}, f32[1,1152]{1,0:T(1,128)}, u32[]{:S(2)}) copy-start(f32[1,1152]{1,0:T(1,128)} %get-tuple-element.363) | copy-start | bytes 13828
  606.7 31.3 %copy-start.33 = (f32[1,1152]{1,0:T(1,128)S(1)}, f32[1,1152]{1,0:T(1,128)}, u32[]{:S(2)}) copy-start(f32[1,1152]{1,0:T(1,128)} %get-tuple-element.361) | copy-start | bytes 13828
  606.7 33.6 %collective-permute-start.31 = (bf16[1,576,729]{2,1,0:T(8,128)(2,1)}, bf16[1,576,729]{2,1,0:T(8,128)(2,1)S(1)}, u32[]{:S(2)}, u32[]{:S(2)}) collective-permute-start(bf16[1,576,729]{2,1,0:T(8,128)(2,1)} %get-tuple-element.351), channel_id=1, source_target_pairs={{0,1},{1,0},{2,3},{3,2},{4,5},{5,4},{6,7},{7,6},{8,9},{9,8},{10,11... | collective-permute-start | bytes 2519432 | tf_op jit(solution)/shard_map/ppermute | solution.py:1105
  638.7 39.5 %collective-permute-start.34 = (f32[13520]{0:T(1024)S(1)}, f32[13520]{0:T(1024)S(1)}, u32[]{:S(2)}, u32[]{:S(2)}) collective-permute-start(f32[13520]{0:T(1024)S(1)} %pad_maximum_fusion.4), channel_id=1, source_target_pairs={{0,1},{1,0},{2,3},{3,2},{4,5},{5,4},{6,7},{7,6},{8,9},{9,8},{10,11... | collective-permute-start | bytes 162248 | tf_op jit(solution)/shard_map/ppermute | solution.py:1105
  641.3 36.8 %copy-start = (bf16[1088,1152]{1,0:T(8,128)(2,1)}, bf16[1088,1152]{1,0:T(8,128)(2,1)S(1)}, u32[]{:S(2)}) copy-start(bf16[1088,1152]{1,0:T(8,128)(2,1)S(1)} %pad_maximum_fusion.1.mine_ref) | copy-start | bytes 7520260
  641.4 40.8 %collective-permute-start.33 = (bf16[2,576,729]{2,1,0:T(8,128)(2,1)}, bf16[2,576,729]{2,1,0:T(8,128)(2,1)}, u32[]{:S(2)}, u32[]{:S(2)}) collective-permute-start(bf16[2,576,729]{2,1,0:T(8,128)(2,1)} %get-tuple-element.354), channel_id=1, source_target_pairs={{0,1},{1,0},{2,3},{3,2},{4,5},{5,4},{6,7},{7,6},{8,9},{9,8},{10,11... | collective-permute-start | bytes 5038856 | tf_op jit(solution)/shard_map/ppermute | solution.py:1105
  642.0 40.2 %collective-permute-start.35 = (bf16[1088,1152]{1,0:T(8,128)(2,1)S(1)}, bf16[1088,1152]{1,0:T(8,128)(2,1)S(1)}, u32[]{:S(2)}, u32[]{:S(2)}) collective-permute-start(bf16[1088,1152]{1,0:T(8,128)(2,1)S(1)} %pad_maximum_fusion.1.mine_ref), channel_id=1, source_target_pairs={{0,2},{2,0},{4,6},{6,4},{8,10},{10,8},{12,14},{14,12},{16,18},{18,... | collective-permute-start | bytes 7520264 | tf_op jit(solution)/shard_map/ppermute | solution.py:1109
  682.2 9.8 %copy-start.3 = (bf16[1088,1152]{1,0:T(8,128)(2,1)}, bf16[1088,1152]{1,0:T(8,128)(2,1)S(1)}, u32[]{:S(2)}) copy-start(bf16[1088,1152]{1,0:T(8,128)(2,1)S(1)} %collective-permute-done.35.other_ref) | copy-start | bytes 7520260
  682.2 9.8 %copy-start.12 = (bf16[1,576,729]{2,1,0:T(8,128)(2,1)S(1)}, bf16[1,576,729]{2,1,0:T(8,128)(2,1)}, u32[]{:S(2)}) copy-start(bf16[1,576,729]{2,1,0:T(8,128)(2,1)} %copy-done.11) | copy-start | bytes 2519428
  682.2 43.9 %collective-permute-start.42 = (bf16[2,576,729]{2,1,0:T(8,128)(2,1)}, bf16[2,576,729]{2,1,0:T(8,128)(2,1)}, u32[]{:S(2)}, u32[]{:S(2)}) collective-permute-start(bf16[2,576,729]{2,1,0:T(8,128)(2,1)} %get-tuple-element.378), channel_id=1, source_target_pairs={{0,1},{1,0},{2,3},{3,2},{4,5},{5,4},{6,7},{7,6},{8,9},{9,8},{10,11... | collective-permute-start | bytes 5038856 | tf_op jit(solution)/shard_map/ppermute | solution.py:1105
  695.2 10.7 %collective-permute-start.38 = (f32[13520]{0:T(1024)S(1)}, f32[13520]{0:T(1024)S(1)}, u32[]{:S(2)}, u32[]{:S(2)}) collective-permute-start(f32[13520]{0:T(1024)S(1)} %fusion.4), channel_id=1, source_target_pairs={{0,6},{2,4},{4,2},{6,0},{8,14},{10,12},{12,10},{14,8},{16,22},{18,... | collective-permute-start | bytes 162248 | tf_op jit(solution)/shard_map/ppermute | solution.py:1116
  695.3 10.6 %collective-permute-start.37 = (f32[13520]{0:T(1024)S(1)}, f32[13520]{0:T(1024)S(1)}, u32[]{:S(2)}, u32[]{:S(2)}) collective-permute-start(f32[13520]{0:T(1024)S(1)} %fusion.4), channel_id=1, source_target_pairs={{0,4},{2,6},{4,0},{6,2},{8,12},{10,14},{12,8},{14,10},{16,20},{18,... | collective-permute-start | bytes 162248 | tf_op jit(solution)/shard_map/ppermute | solution.py:1116
  696.8 9.1 %collective-permute-start.36 = (f32[13520]{0:T(1024)S(1)}, f32[13520]{0:T(1024)S(1)}, u32[]{:S(2)}, u32[]{:S(2)}) collective-permute-start(f32[13520]{0:T(1024)S(1)} %fusion.4), channel_id=1, source_target_pairs={{0,2},{2,0},{4,6},{6,4},{8,10},{10,8},{12,14},{14,12},{16,18},{18,... | collective-permute-start | bytes 162248 | tf_op jit(solution)/shard_map/ppermute | solution.py:1116
  706.0 7.8 %collective-permute-start.41 = (f32[13520]{0:T(1024)S(1)}, f32[13520]{0:T(1024)S(1)}, u32[]{:S(2)}, u32[]{:S(2)}) collective-permute-start(f32[13520]{0:T(1024)S(1)} %add_add_fusion.1), channel_id=1, source_target_pairs={{0,24},{2,26},{4,28},{6,30},{8,16},{10,18},{12,20},{14,22},{16,8},... | collective-permute-start | bytes 162248 | tf_op jit(solution)/shard_map/ppermute | solution.py:1116
  707.5 12.8 %collective-permute-start.40 = (f32[13520]{0:T(1024)S(1)}, f32[13520]{0:T(1024)S(1)}, u32[]{:S(2)}, u32[]{:S(2)}) collective-permute-start(f32[13520]{0:T(1024)S(1)} %add_add_fusion.1), channel_id=1, source_target_pairs={{0,16},{2,18},{4,20},{6,22},{8,24},{10,26},{12,28},{14,30},{16,0},... | collective-permute-start | bytes 162248 | tf_op jit(solution)/shard_map/ppermute | solution.py:1116
  708.0 12.3 %collective-permute-start.39 = (f32[13520]{0:T(1024)S(1)}, f32[13520]{0:T(1024)S(1)}, u32[]{:S(2)}, u32[]{:S(2)}) collective-permute-start(f32[13520]{0:T(1024)S(1)} %add_add_fusion.1), channel_id=1, source_target_pairs={{0,8},{2,10},{4,12},{6,14},{8,0},{10,2},{12,4},{14,6},{16,24},{18,... | collective-permute-start | bytes 162248 | tf_op jit(solution)/shard_map/ppermute | solution.py:1116
  726.1 10.1 %collective-permute-start.43 = (bf16[1152,1152]{1,0:T(8,128)(2,1)}, bf16[1152,1152]{1,0:T(8,128)(2,1)S(1)}, u32[]{:S(2)}, u32[]{:S(2)}) collective-permute-start(bf16[1152,1152]{1,0:T(8,128)(2,1)} %all-reduce.9.cloned.1.call-done.mine_ref), channel_id=1, source_target_pairs={{0,2},{2,0},{4,6},{6,4},{8,10},{10,8},{12,14},{14,12},{16,18},{18,... | collective-permute-start | bytes 7962632 | tf_op jit(solution)/shard_map/ppermute | solution.py:1109
  726.1 22.7 %collective-permute-start.44 = (bf16[1,576,729]{2,1,0:T(8,128)(2,1)}, bf16[1,576,729]{2,1,0:T(8,128)(2,1)S(1)}, u32[]{:S(2)}, u32[]{:S(2)}) collective-permute-start(bf16[1,576,729]{2,1,0:T(8,128)(2,1)} %get-tuple-element.383), channel_id=1, source_target_pairs={{0,1},{1,0},{2,3},{3,2},{4,5},{5,4},{6,7},{7,6},{8,9},{9,8},{10,11... | collective-permute-start | bytes 2519432 | tf_op jit(solution)/shard_map/ppermute | solution.py:1105
  (21 other events, 53.4 us)
Sparse Core Ops, SparseCore 0:
  40.7 57.8 all-gather.2
  101.3 83.7 all-gather.4
  359.3 117.7 all-reduce.6
  606.8 119.3 all-reduce.8

commit v4 on v3

--- a/solution.py
+++ b/solution.py
@@ -543,7 +543,7 @@
         d_ref[0, heads + first + head] = (dot_nt(query, grad_scores) * scale).astype(BF16)
 
 
-def mix_back(qkv, out, log_total, grad, half, start, steps, earlier, per_step=2):
+def mix_back(qkv, out, log_total, grad, half, start, steps, earlier, per_step=4):
     count, groups, head_dim, seq = qkv.shape
     heads = groups // 3
     blocks = heads // per_step
@@ -1452,7 +1452,7 @@
         small_grads[6 * feat :].reshape(2, 2 * width + hidden), tensor, 0, keepdims=False
     )
 
-    g_q, g_k, g_v, g_o = widen(place, g_qkv, qkv_other_core, width // 2, width, 1, 4)
+    g_q, g_k, g_v, g_o = widen(place, g_qkv, qkv_other_core, width // 2, width, 2, 4)
     g_q, out_arrived[1] = lax.optimization_barrier((g_q, out_arrived[1]))
     layer_out = lax.dynamic_update_slice_in_dim(out_buffer, jnp.concatenate(out_arrived), far, 0)
     return (

time: 770 us -> 772 us (level)
  no operation moved by 1% of the time
where the time goes in v4:
time: 772 us; the launch traced here: 761 us
  Pallas kernels  576 us (75%)
  waiting for transfers between devices  51.1 us (7%)
  other arithmetic  47.1 us (6%)
  starting transfers between devices  40.8 us (5%)
  local copies, waits for them, and re-layouts  30.9 us (4%)
  between operations  14.7 us (2%)
    pallas_call x4, Pallas kernels, hidden_stage(): pl.pallas_call(functools.partial(hidden_kernel, which=which), out_shape=[...  145 us
    pallas_call x4, Pallas kernels, mix_back(): pl.pallas_call(functools.partial(mix_back_kernel, scale=1.0 / math.sqrt(h...  81.5 us
    pallas_call x4, Pallas kernels, mix(): pl.pallas_call(functools.partial(mix_kernel, scale=1.0 / math.sqrt(head_d...  58.2 us
    pallas_call x2, Pallas kernels, input_back(): pl.pallas_call(input_back_kernel, out_shape=[jax.ShapeDtypeStruct((2 * co...  49.6 us
    pallas_call x1, Pallas kernels, resid_back(): pl.pallas_call(resid_back_kernel, grid=(count,), out_shape=[jax.ShapeDtyp...  46.3 us
    pallas_call x2, Pallas kernels, project_back(): pl.pallas_call(project_back_kernel, out_shape=[part, part, jax.ShapeDtype...  38.3 us
    pallas_call x1, Pallas kernels, layer_result(): pl.pallas_call(layer_kernel, out_shape=[jax.ShapeDtypeStruct((2 * count,...  36.1 us
    ppermute x22, waiting for transfers between devices, swap_tensor(): return lax.ppermute(value, 'tensor', [(0, 1), (1, 0)])  34.5 us
  transfers between devices with their start and end apart: 49, of which 9 were waited for; matrix products, arithmetic and copies ran while one was open for 8% of the time, Pallas kernels for 71%

profile of v4, /device:TPU:0, one launch (start us, length us, event | category | flops | bytes accessed | tf_op | source)
XLA Modules:
  0.0 760.8 jit_solution(14567459663463327042)
XLA Ops:
  7.3 1.9 dynamic-slice_bitcast_fusion.3
  10.7 3.0 collective-permute-start
  13.8 26.8 %collective-permute-done.1 = bf16[144,1152]{1,0:T(8,128)(2,1)} collective-permute-done((bf16[144,1152]{1,0:T(8,128)(2,1)S(1)}, bf16[144,1152]{1,0:T(8,128)(2,1)}, u32[]{:S(2)}, u32[]{:S(2)}) %collective-permute-start.1) | collective-permute-done | bytes 331808 | tf_op jit(solution)/shard_map/ppermute | solution.py:1105
  40.7 3.5 concatenate.62
  44.2 1.8 collective-permute-start.3
  46.0 2.3 fusion
  52.6 10.2 %first_norm.3 = (bf16[3,1152,729]{2,1,0:T(8,128)(2,1)}, bf16[3,1152,729]{2,1,0:T(8,128)(2,1)}, bf16[3,24,72,729]{3,2,1,0:T(8,128)(2,1)}) custom-call(s32[8]{0:T(128)} %pad_add_fusion.place_ref, bf16[6,576,729]{2,1,0:T(8,128)(2,1)} %bitcast.42, bf16[1,576,729]{2,1,0:T(8,128)(2,1)} %copy-done.10, f32[1152,8]{1,0:T(8,128)} %convert_bitcast_fusion.feature_ref.gain_ref.b_ref, ...), custom_call_target="tpu_custom_call" | custom-call | flops 145118816 | bytes 629145 | tf_op jit(solution)/shard_map/first_norm/pallas_call | solution.py:419
  62.8 1.5 collective-permute-start.5
  64.3 10.3 %mix.4 = (bf16[3,16,72,729]{3,2,1,0:T(8,128)(2,1)}, f32[3,16,1,729]{3,2,1,0:T(1,128)}) custom-call(bf16[3,24,72,729]{3,2,1,0:T(8,128)(2,1)} %get-tuple-element.211.q_ref.k_ref.v_ref.rest_2_, bf16[3,24,72,729]{3,2,1,0:T(8,128)(2,1)} %get-tuple-element.211.q_ref.k_ref.v_ref.rest_2_, bf16[3,24,72,729]{3,2,1,0:T(8,128)(2,1)} %get-tuple-element.211.q_ref.k_ref.v_ref.rest_2_), custom_call_target="tpu_custom_call" | custom-call | flops 217678240 | bytes 167961 | tf_op jit(solution)/shard_map/mix/pallas_call | solution.py:504
  75.5 10.2 %first_norm.4 = (bf16[3,1152,729]{2,1,0:T(8,128)(2,1)}, bf16[3,1152,729]{2,1,0:T(8,128)(2,1)}, bf16[3,24,72,729]{3,2,1,0:T(8,128)(2,1)}) custom-call(s32[8]{0:T(128)} %pad_add_fusion.place_ref, bf16[6,576,729]{2,1,0:T(8,128)(2,1)} %bitcast.43, bf16[1,576,729]{2,1,0:T(8,128)(2,1)} %copy-done.9, ...), custom_call_target="tpu_custom_call", output_to_operand_aliasing={{0}: (8, {}), {1}: (9, {}), {2}: (10, {})} | custom-call | flops 145118816 | bytes 629145 | tf_op jit(solution)/shard_map/first_norm/pallas_call | solution.py:419
  87.5 2.8 dynamic-slice_bitcast_fusion
  91.0 2.1 copy.67
  93.1 10.2 %mix.5 = (bf16[3,16,72,729]{3,2,1,0:T(8,128)(2,1)}, f32[3,16,1,729]{3,2,1,0:T(1,128)}) custom-call(bf16[3,24,72,729]{3,2,1,0:T(8,128)(2,1)} %get-tuple-element.219.q_ref.k_ref.v_ref.rest_2_, bf16[3,24,72,729]{3,2,1,0:T(8,128)(2,1)} %get-tuple-element.219.q_ref.k_ref.v_ref.rest_2_, ...), custom_call_target="tpu_custom_call", output_to_operand_aliasing={{0}: (3, {}), {1}: (4, {})} | custom-call | flops 217678240 | bytes 167961 | tf_op jit(solution)/shard_map/mix/pallas_call | solution.py:504
  103.3 3.4 collective-permute-done.4.other_ref
  107.2 1.5 collective-permute-start.7
  109.3 10.1 %first_norm.5 = (bf16[3,1152,729]{2,1,0:T(8,128)(2,1)}, bf16[3,1152,729]{2,1,0:T(8,128)(2,1)}, bf16[3,24,72,729]{3,2,1,0:T(8,128)(2,1)}) custom-call(s32[8]{0:T(128)} %pad_add_fusion.place_ref, bf16[6,576,729]{2,1,0:T(8,128)(2,1)} %bitcast.44, bf16[1,576,729]{2,1,0:T(8,128)(2,1)} %copy-done.8, ...), custom_call_target="tpu_custom_call", output_to_operand_aliasing={{0}: (8, {}), {1}: (9, {}), {2}: (10, {})} | custom-call | flops 145118816 | bytes 629145 | tf_op jit(solution)/shard_map/first_norm/pallas_call | solution.py:419
  119.4 10.2 %mix.6 = (bf16[3,16,72,729]{3,2,1,0:T(8,128)(2,1)}, f32[3,16,1,729]{3,2,1,0:T(1,128)}) custom-call(bf16[3,24,72,729]{3,2,1,0:T(8,128)(2,1)} %get-tuple-element.227.q_ref.k_ref.v_ref, bf16[3,24,72,729]{3,2,1,0:T(8,128)(2,1)} %get-tuple-element.227.q_ref.k_ref.v_ref, ...), custom_call_target="tpu_custom_call", output_to_operand_aliasing={{0}: (3, {}), {1}: (4, {})} | custom-call | flops 217678240 | bytes 167961 | tf_op jit(solution)/shard_map/mix/pallas_call | solution.py:504
  129.5 15.1 %project.1.q_ref.k_ref.v_ref = bf16[3,24,72,729]{3,2,1,0:T(8,128)(2,1)} custom-call(bf16[3,1152,729]{2,1,0:T(8,128)(2,1)} %get-tuple-element.226.normed_ref, bf16[2304,1152]{1,0:T(8,128)(2,1)} %all-gather.3.cloned.1.call-done.q_ref.k_ref.v_ref.w_other_ref, bf16[2304,1152]{1,0:T(8,128)(2,1)} %all-gather.3.cloned.1.call-done.q_ref.k_ref.v_ref.w_other_ref, ...), custom_call_target="tpu_custom_call" | custom-call | flops 3482851840 | bytes 8388608 | tf_op jit(solution)/shard_map/project/pallas_call | solution.py:463
  144.6 27.5 %mix.7 = (bf16[3,16,72,729]{3,2,1,0:T(8,128)(2,1)}, f32[3,16,1,729]{3,2,1,0:T(1,128)}) custom-call(bf16[3,24,72,729]{3,2,1,0:T(8,128)(2,1)} %project.1.q_ref.k_ref.v_ref, bf16[3,24,72,729]{3,2,1,0:T(8,128)(2,1)} %project.1.q_ref.k_ref.v_ref, bf16[3,24,72,729]{3,2,1,0:T(8,128)(2,1)} %project.1.q_ref.k_ref.v_ref, ...), custom_call_target="tpu_custom_call", output_to_operand_aliasing={{0}: (3, {}), {1}: (4, {})} | custom-call | flops 5224277504 | bytes 4031078 | tf_op jit(solution)/shard_map/mix/pallas_call | solution.py:504
  173.0 22.4 %second_norm.1 = (bf16[3,1152,729]{2,1,0:T(8,128)(2,1)}, bf16[3,1152,729]{2,1,0:T(8,128)(2,1)}, bf16[3,1152,729]{2,1,0:T(8,128)(2,1)}, f32[1,1152]{1,0:T(1,128)}) custom-call(s32[8]{0:T(128)} %pad_add_fusion.place_ref, bf16[3,1152,729]{2,1,0:T(8,128)(2,1)} %bitcast.37, bf16[576,1152]{1,0:T(8,128)(2,1)} %w_own_ref.4, ...), custom_call_target="tpu_custom_call" | custom-call | flops 2321901056 | bytes 16777216 | tf_op jit(solution)/shard_map/second_norm/pallas_call | solution.py:625
  195.5 36.0 %hidden_stage.4 = (bf16[3,2152,729]{2,1,0:T(8,128)(2,1)}, bf16[3,2152,729]{2,1,0:T(8,128)(2,1)}, f32[2152,1]{1,0:T(8,128)}, bf16[1088,1152]{1,0:T(8,128)(2,1)}, bf16[1088,1152]{1,0:T(8,128)(2,1)}) custom-call(s32[8]{0:T(128)} %pad_add_fusion.place_ref, bf16[3,1152,729]{2,1,0:T(8,128)(2,1)} %get-tuple-element.243.low_ref, ...), custom_call_target="tpu_custom_call" | custom-call | flops 86748807168 | bytes 125829120 | tf_op jit(solution)/shard_map/hidden_stage/pallas_call | solution.py:695
  232.0 36.2 %hidden_stage.5 = (bf16[3,2152,729]{2,1,0:T(8,128)(2,1)}, bf16[3,2152,729]{2,1,0:T(8,128)(2,1)}, f32[2152,1]{1,0:T(8,128)}, bf16[1088,1152]{1,0:T(8,128)(2,1)}, bf16[1088,1152]{1,0:T(8,128)(2,1)}) custom-call(s32[8]{0:T(128)} %pad_add_fusion.place_ref, ...), custom_call_target="tpu_custom_call", output_to_operand_aliasing={{0}: (6, {}), {1}: (7, {}), {2}: (8, {})} | custom-call | flops 86748807168 | bytes 125829120 | tf_op jit(solution)/shard_map/hidden_stage/pallas_call | solution.py:695
  268.2 2.3 add_convert_fusion.8
  270.5 3.2 add_convert_fusion.3
  274.8 1.6 add_convert_fusion.4
  276.4 1.5 collective-permute-start.11
  278.0 36.3 %hidden_stage.6 = (bf16[3,2152,729]{2,1,0:T(8,128)(2,1)}, bf16[3,2152,729]{2,1,0:T(8,128)(2,1)}, f32[2152,1]{1,0:T(8,128)}, bf16[1088,1152]{1,0:T(8,128)(2,1)}, bf16[1088,1152]{1,0:T(8,128)(2,1)}) custom-call(s32[8]{0:T(128)} %pad_add_fusion.place_ref, bf16[3,1152,729]{2,1,0:T(8,128)(2,1)} %get-tuple-element.243.low_ref, ...), custom_call_target="tpu_custom_call" | custom-call | flops 86748807168 | bytes 125829120 | tf_op jit(solution)/shard_map/hidden_stage/pallas_call | solution.py:695
  314.9 1.5 collective-permute-start.14
  317.0 36.1 %hidden_stage.7 = (bf16[3,2152,729]{2,1,0:T(8,128)(2,1)}, bf16[3,2152,729]{2,1,0:T(8,128)(2,1)}, f32[2152,1]{1,0:T(8,128)}, bf16[1088,1152]{1,0:T(8,128)(2,1)}, bf16[1088,1152]{1,0:T(8,128)(2,1)}) custom-call(s32[8]{0:T(128)} %pad_add_fusion.place_ref, ...), custom_call_target="tpu_custom_call", output_to_operand_aliasing={{0}: (6, {}), {1}: (7, {}), {2}: (8, {})} | custom-call | flops 86748807168 | bytes 125829120 | tf_op jit(solution)/shard_map/hidden_stage/pallas_call | solution.py:695
  354.7 4.5 add_convert_fusion.1
  359.3 46.3 %resid_back.1 = (bf16[3,1152,729]{2,1,0:T(8,128)(2,1)}, f32[1,1152]{1,0:T(1,128)}, f32[1,1152]{1,0:T(1,128)}, f32[1,1152]{1,0:T(1,128)}) custom-call(bf16[3,2152,729]{2,1,0:T(8,128)(2,1)} %get-tuple-element.272.back_own_ref, bf16[3,2152,729]{2,1,0:T(8,128)(2,1)} %get-tuple-element.273.back_other_ref, bf16[2152,1152]{1,0:T(8,128)(2,1)} %bitcast.52, ...), custom_call_target="tpu_custom_call" | custom-call | flops 8674880512 | bytes 20971520 | tf_op jit(solution)/shard_map/resid_back/pallas_call | solution.py:841
  405.6 2.6 add_convert_fusion
  408.4 21.6 %context_back.1 = (bf16[3,1152,729]{2,1,0:T(8,128)(2,1)}, bf16[288,1152]{1,0:T(8,128)(2,1)}, bf16[288,1152]{1,0:T(8,128)(2,1)}, bf16[288,1152]{1,0:T(8,128)(2,1)}, bf16[288,1152]{1,0:T(8,128)(2,1)}) custom-call(s32[8]{0:T(128)} %pad_add_fusion.place_ref, bf16[3,1152,729]{2,1,0:T(8,128)(2,1)} %get-tuple-element.282.low_ref, bf16[3,1152,729]{2,1,0:T(8,128)(2,1)} %bitcast.38, ...), custom_call_target="tpu_custom_call" | custom-call | flops 4643802112 | bytes 10485760 | tf_op jit(solution)/shard_map/context_back/pallas_call | solution.py:907
  432.0 37.6 %mix_back.4 = bf16[3,24,72,729]{3,2,1,0:T(8,128)(2,1)} custom-call(bf16[3,24,72,729]{3,2,1,0:T(8,128)(2,1)} %project.1.q_ref.k_ref.v_ref, bf16[3,24,72,729]{3,2,1,0:T(8,128)(2,1)} %project.1.q_ref.k_ref.v_ref, bf16[3,24,72,729]{3,2,1,0:T(8,128)(2,1)} %project.1.q_ref.k_ref.v_ref, bf16[3,16,72,729]{3,2,1,0:T(8,128)(2,1)} %get-tuple-element.237.out_ref, ...), custom_call_target="tpu_custom_call" | custom-call | flops 13060694016 | bytes 8062156 | tf_op jit(solution)/shard_map/mix_back/pallas_call | solution.py:556
  475.8 1.6 collective-permute-start.21
  477.4 19.1 %project_back.2 = (bf16[864,1152]{1,0:T(8,128)(2,1)}, bf16[864,1152]{1,0:T(8,128)(2,1)}, f32[1728,1]{1,0:T(8,128)}) custom-call(s32[8]{0:T(128)} %pad_add_fusion.place_ref, bf16[3,1152,729]{2,1,0:T(8,128)(2,1)} %get-tuple-element.226.normed_ref, bf16[3,1728,729]{2,1,0:T(8,128)(2,1)} %bitcast.70), custom_call_target="tpu_custom_call" | custom-call | flops 3482851840 | bytes 8388608 | tf_op jit(solution)/shard_map/project_back/pallas_call | solution.py:960
  498.6 2.7 collective-permute-start.22
  501.3 14.8 %mix_back.5.rest_0_ = bf16[3,24,72,729]{3,2,1,0:T(8,128)(2,1)} custom-call(bf16[3,24,72,729]{3,2,1,0:T(8,128)(2,1)} %get-tuple-element.227.q_ref.k_ref.v_ref, bf16[3,24,72,729]{3,2,1,0:T(8,128)(2,1)} %get-tuple-element.227.q_ref.k_ref.v_ref, bf16[3,24,72,729]{3,2,1,0:T(8,128)(2,1)} %get-tuple-element.227.q_ref.k_ref.v_ref, ...), custom_call_target="tpu_custom_call" | custom-call | flops 544195584 | bytes 335923 | tf_op jit(solution)/shard_map/mix_back/pallas_call | solution.py:556
  516.2 2.3 add_convert_fusion.12
  518.6 2.3 add_convert_fusion.7
  522.7 14.4 %mix_back.6.rest_0_ = bf16[3,24,72,729]{3,2,1,0:T(8,128)(2,1)} custom-call(bf16[3,24,72,729]{3,2,1,0:T(8,128)(2,1)} %get-tuple-element.227.q_ref.k_ref.v_ref, bf16[3,24,72,729]{3,2,1,0:T(8,128)(2,1)} %get-tuple-element.227.q_ref.k_ref.v_ref, bf16[3,24,72,729]{3,2,1,0:T(8,128)(2,1)} %get-tuple-element.227.q_ref.k_ref.v_ref, ...), custom_call_target="tpu_custom_call", output_to_operand_aliasing={{}: (6, {})} | custom-call | flops 544195584 | bytes 335923 | tf_op jit(solution)/shard_map/mix_back/pallas_call | solution.py:556
  540.1 1.6 reduce.6
  543.6 14.6 %mix_back.7 = bf16[3,24,72,729]{3,2,1,0:T(8,128)(2,1)} custom-call(bf16[3,24,72,729]{3,2,1,0:T(8,128)(2,1)} %get-tuple-element.227.q_ref.k_ref.v_ref, bf16[3,24,72,729]{3,2,1,0:T(8,128)(2,1)} %get-tuple-element.227.q_ref.k_ref.v_ref, bf16[3,24,72,729]{3,2,1,0:T(8,128)(2,1)} %get-tuple-element.227.q_ref.k_ref.v_ref, ...), custom_call_target="tpu_custom_call", output_to_operand_aliasing={{}: (6, {})} | custom-call | flops 544195584 | bytes 335923 | tf_op jit(solution)/shard_map/mix_back/pallas_call | solution.py:556
  560.0 19.1 %project_back.3 = (bf16[864,1152]{1,0:T(8,128)(2,1)}, bf16[864,1152]{1,0:T(8,128)(2,1)}, f32[1728,1]{1,0:T(8,128)}) custom-call(s32[8]{0:T(128)} %pad_add_fusion.place_ref, bf16[3,1152,729]{2,1,0:T(8,128)(2,1)} %get-tuple-element.226.normed_ref, bf16[3,1728,729]{2,1,0:T(8,128)(2,1)} %bitcast.39), custom_call_target="tpu_custom_call" | custom-call | flops 3482851840 | bytes 8388608 | tf_op jit(solution)/shard_map/project_back/pallas_call | solution.py:960
  581.2 19.5 %input_back.2 = (bf16[6,576,729]{2,1,0:T(8,128)(2,1)}, bf16[1,576,729]{2,1,0:T(8,128)(2,1)}, f32[1,1152]{1,0:T(1,128)}, f32[1,1152]{1,0:T(1,128)}) custom-call(s32[8]{0:T(128)} %pad_add_fusion.place_ref, bf16[3,1728,729]{2,1,0:T(8,128)(2,1)} %bitcast.40, bf16[3,1728,729]{2,1,0:T(8,128)(2,1)} %bitcast.71, bf16[576,1152]{1,0:T(8,128)(2,1)} %bitcast.56, ...), custom_call_target="tpu_custom_call" | custom-call | flops 23219011584 | bytes 79691776 | tf_op jit(solution)/shard_map/input_back/pallas_call | solution.py:1024
  600.7 2.8 add_convert_fusion.2
  603.5 1.7 pad_maximum_fusion
  606.0 30.2 %input_back.3 = (bf16[6,576,729]{2,1,0:T(8,128)(2,1)}, bf16[2,576,729]{2,1,0:T(8,128)(2,1)}, f32[1,1152]{1,0:T(1,128)}, f32[1,1152]{1,0:T(1,128)}) custom-call(s32[8]{0:T(128)} %pad_add_fusion.place_ref, bf16[3,1728,729]{2,1,0:T(8,128)(2,1)} %bitcast.41, bf16[3,1728,729]{2,1,0:T(8,128)(2,1)} %bitcast.72, ...), custom_call_target="tpu_custom_call", output_to_operand_aliasing={{0}: (10, {})} | custom-call | flops 46438023168 | bytes 125829120 | tf_op jit(solution)/shard_map/input_back/pallas_call | solution.py:1024
  637.6 1.5 collective-permute-start.34
  640.9 36.1 %layer_result.1 = (bf16[6,576,729]{2,1,0:T(8,128)(2,1)}, bf16[2,576,729]{2,1,0:T(8,128)(2,1)}, bf16[1,576,729]{2,1,0:T(8,128)(2,1)}) custom-call(s32[8]{0:T(128)} %pad_add_fusion.place_ref, bf16[3,2152,729]{2,1,0:T(8,128)(2,1)} %get-tuple-element.357.act_own_ref, bf16[3,2152,729]{2,1,0:T(8,128)(2,1)} %get-tuple-element.358.act_other_ref, ...), custom_call_target="tpu_custom_call" | custom-call | flops 86748807168 | bytes 150994944 | tf_op jit(solution)/shard_map/layer_result/pallas_call | solution.py:767
  677.1 4.0 collective-permute-done.33
  681.7 9.1 %widen.4 = f32[2152,1152]{1,0:T(8,128)} custom-call(s32[8]{0:T(128)} %pad_add_fusion.place_ref, bf16[1088,1152]{1,0:T(8,128)(2,1)} %all-reduce.7.cloned.1.call-done.mine_ref, bf16[1088,1152]{1,0:T(8,128)(2,1)} %collective-permute-done.23.other_ref), custom_call_target="tpu_custom_call" | custom-call | bytes 991641 | tf_op jit(solution)/shard_map/widen/pallas_call | solution.py:1085
  690.9 3.2 maximum_dynamic-update-slice_fusion
  694.2 1.6 collective-permute-start.37
  696.1 8.8 %widen.3 = f32[2152,1152]{1,0:T(8,128)} custom-call(s32[8]{0:T(128)} %pad_add_fusion.place_ref, bf16[1088,1152]{1,0:T(8,128)(2,1)} %copy-done, bf16[1088,1152]{1,0:T(8,128)(2,1)} %copy-done.3), custom_call_target="tpu_custom_call" | custom-call | bytes 991641 | tf_op jit(solution)/shard_map/widen/pallas_call | solution.py:1085
  704.9 1.9 collective-permute-start.41
  707.6 1.7 collective-permute-start.39
  709.3 3.4 collective-permute-done.41
  712.7 7.2 collective-permute-done.40
  720.5 4.6 all-reduce.9.cloned.1.call-done.mine_ref
  725.1 1.5 collective-permute-start.44
  733.5 1.7 dynamic-slice_reduce_fusion.1
  736.7 14.1 %widen.5 = (f32[576,1152]{1,0:T(8,128)}, f32[576,1152]{1,0:T(8,128)}, f32[576,1152]{1,0:T(8,128)}, f32[576,1152]{1,0:T(8,128)}) custom-call(s32[8]{0:T(128)} %pad_add_fusion.place_ref, bf16[1152,1152]{1,0:T(8,128)(2,1)} %all-reduce.9.cloned.1.call-done.mine_ref, bf16[1152,1152]{1,0:T(8,128)(2,1)} %copy-done.1), custom_call_target="tpu_custom_call" | custom-call | bytes 1061683 | tf_op jit(solution)/shard_map/widen/pallas_call | solution.py:1085
  750.8 3.2 maximum_dynamic-update-slice_fusion.1
  (212 shorter events, 51.6 us)
Async XLA Ops:
  7.2 122.4 %all-gather.3.cloned.1.call-start = ((), (), s32[]{:S(2)}) async-start(), calls=%async_computation | async-start | bytes 5640192 | tf_op jit(solution)/shard_map/all_gather | solution.py:1227
  7.3 33.4 %copy-start.23 = (bf16[576]{0:T(1024)(128)(2,1)S(1)}, bf16[576]{0:T(1024)(128)(2,1)}, u32[]{:S(2)}) copy-start(bf16[576]{0:T(1024)(128)(2,1)} %param.21) | copy-start | bytes 3460
  7.3 33.4 %copy-start.24 = (bf16[576]{0:T(1024)(128)(2,1)S(1)}, bf16[576]{0:T(1024)(128)(2,1)}, u32[]{:S(2)}) copy-start(bf16[576]{0:T(1024)(128)(2,1)} %param.22) | copy-start | bytes 3460
  7.3 33.4 %copy-start.25 = (bf16[576]{0:T(1024)(128)(2,1)S(1)}, bf16[576]{0:T(1024)(128)(2,1)}, u32[]{:S(2)}) copy-start(bf16[576]{0:T(1024)(128)(2,1)} %param.29) | copy-start | bytes 3460
  7.3 33.4 %copy-start.26 = (bf16[576]{0:T(1024)(128)(2,1)S(1)}, bf16[576]{0:T(1024)(128)(2,1)}, u32[]{:S(2)}) copy-start(bf16[576]{0:T(1024)(128)(2,1)} %param.30) | copy-start | bytes 3460
  10.7 29.9 %collective-permute-start = (bf16[1,576,729]{2,1,0:T(8,128)(2,1)S(1)}, bf16[1,576,729]{2,1,0:T(8,128)(2,1)S(1)}, u32[]{:S(2)}, u32[]{:S(2)}) collective-permute-start(bf16[1,576,729]{2,1,0:T(8,128)(2,1)S(1)} %get-tuple-element.205), channel_id=1, source_target_pairs={{0,1},{1,0},{2,3},{3,2},{4,5},{5,4},{6,7},{7,6},{8,9},{9,8},{10,11... | collective-permute-start | bytes 2519432 | tf_op jit(solution)/shard_map/ppermute | solution.py:1105
  13.7 26.9 %collective-permute-start.1 = (bf16[144,1152]{1,0:T(8,128)(2,1)S(1)}, bf16[144,1152]{1,0:T(8,128)(2,1)}, u32[]{:S(2)}, u32[]{:S(2)}) collective-permute-start(bf16[144,1152]{1,0:T(8,128)(2,1)S(1)} %bitcast_select_fusion), channel_id=1, source_target_pairs={{0,1},{1,0},{2,3},{3,2},{4,5},{5,4},{6,7},{7,6},{8,9},{9,8},{10,11... | collective-permute-start | bytes 995336 | tf_op jit(solution)/shard_map/ppermute | solution.py:1105
  40.6 7.7 %copy-start.10 = (bf16[1,576,729]{2,1,0:T(8,128)(2,1)}, bf16[1,576,729]{2,1,0:T(8,128)(2,1)S(1)}, u32[]{:S(2)}) copy-start(bf16[1,576,729]{2,1,0:T(8,128)(2,1)S(1)} %collective-permute-done.other_ref) | copy-start | bytes 2519428
  40.6 154.9 %all-gather.5.cloned.1.call-start = ((), (), s32[]{:S(2)}) async-start(), calls=%async_computation.1 | async-start | bytes 10653696 | tf_op jit(solution)/shard_map/all_gather | solution.py:1264
  44.2 4.9 collective-permute-start.3
  51.1 23.4 %collective-permute-start.2 = (bf16[1,576,729]{2,1,0:T(8,128)(2,1)S(1)}, bf16[1,576,729]{2,1,0:T(8,128)(2,1)S(1)}, u32[]{:S(2)}, u32[]{:S(2)}) collective-permute-start(bf16[1,576,729]{2,1,0:T(8,128)(2,1)S(1)} %get-tuple-element.207), channel_id=1, source_target_pairs={{0,1},{1,0},{2,3},{3,2},{4,5},{5,4},{6,7},{7,6},{8,9},{9,8},{10,11... | collective-permute-start | bytes 2519432 | tf_op jit(solution)/shard_map/ppermute | solution.py:1105
  52.6 10.2 %copy-start.18 = (bf16[272,1152]{1,0:T(8,128)(2,1)S(1)}, bf16[272,1152]{1,0:T(8,128)(2,1)}, u32[]{:S(2)}) copy-start(bf16[272,1152]{1,0:T(8,128)(2,1)} %fusion) | copy-start | bytes 1880068
  62.8 22.9 %collective-permute-start.5 = (bf16[272,1152]{1,0:T(8,128)(2,1)S(1)}, bf16[272,1152]{1,0:T(8,128)(2,1)S(1)}, u32[]{:S(2)}, u32[]{:S(2)}) collective-permute-start(bf16[272,1152]{1,0:T(8,128)(2,1)S(1)} %copy-done.18), channel_id=1, source_target_pairs={{0,1},{1,0},{2,3},{3,2},{4,5},{5,4},{6,7},{7,6},{8,9},{9,8},{10,11... | collective-permute-start | bytes 1880072 | tf_op jit(solution)/shard_map/ppermute | solution.py:1105
  86.5 410.0 %all-reduce.7.cloned.1.call-start = ((), (), s32[]{:S(2)}) async-start(), calls=%async_computation.2 | async-start | bytes 5013504 | tf_op jit(solution)/shard_map/psum | solution.py:1322
  87.0 19.7 %collective-permute-start.4 = (bf16[1,576,729]{2,1,0:T(8,128)(2,1)S(1)}, bf16[1,576,729]{2,1,0:T(8,128)(2,1)S(1)}, u32[]{:S(2)}, u32[]{:S(2)}) collective-permute-start(bf16[1,576,729]{2,1,0:T(8,128)(2,1)S(1)} %get-tuple-element.213), channel_id=1, source_target_pairs={{0,1},{1,0},{2,3},{3,2},{4,5},{5,4},{6,7},{7,6},{8,9},{9,8},{10,11... | collective-permute-start | bytes 2519432 | tf_op jit(solution)/shard_map/ppermute | solution.py:1105
  106.7 65.4 %collective-permute-start.6 = (bf16[1,576,729]{2,1,0:T(8,128)(2,1)}, bf16[1,576,729]{2,1,0:T(8,128)(2,1)S(1)}, u32[]{:S(2)}, u32[]{:S(2)}) collective-permute-start(bf16[1,576,729]{2,1,0:T(8,128)(2,1)} %get-tuple-element.234), channel_id=1, source_target_pairs={{0,1},{1,0},{2,3},{3,2},{4,5},{5,4},{6,7},{7,6},{8,9},{9,8},{10,11... | collective-permute-start | bytes 2519432 | tf_op jit(solution)/shard_map/ppermute | solution.py:1105
  107.2 64.9 %collective-permute-start.7 = (bf16[1,576,729]{2,1,0:T(8,128)(2,1)S(1)}, bf16[1,576,729]{2,1,0:T(8,128)(2,1)}, u32[]{:S(2)}, u32[]{:S(2)}) collective-permute-start(bf16[1,576,729]{2,1,0:T(8,128)(2,1)S(1)} %get-tuple-element.235), channel_id=1, source_target_pairs={{0,1},{1,0},{2,3},{3,2},{4,5},{5,4},{6,7},{7,6},{8,9},{9,8},{10,11... | collective-permute-start | bytes 2519432 | tf_op jit(solution)/shard_map/ppermute | solution.py:1105
  108.8 63.4 %collective-permute-start.8 = (bf16[1,576,729]{2,1,0:T(8,128)(2,1)S(1)}, bf16[1,576,729]{2,1,0:T(8,128)(2,1)}, u32[]{:S(2)}, u32[]{:S(2)}) collective-permute-start(bf16[1,576,729]{2,1,0:T(8,128)(2,1)S(1)} %get-tuple-element.236), channel_id=1, source_target_pairs={{0,1},{1,0},{2,3},{3,2},{4,5},{5,4},{6,7},{7,6},{8,9},{9,8},{10,11... | collective-permute-start | bytes 2519432 | tf_op jit(solution)/shard_map/ppermute | solution.py:1105
  231.5 42.2 %collective-permute-start.9 = (bf16[1088,1152]{1,0:T(8,128)(2,1)}, bf16[1088,1152]{1,0:T(8,128)(2,1)S(1)}, u32[]{:S(2)}, u32[]{:S(2)}) collective-permute-start(bf16[1088,1152]{1,0:T(8,128)(2,1)} %get-tuple-element.250), channel_id=1, source_target_pairs={{0,2},{2,0},{4,6},{6,4},{8,10},{10,8},{12,14},{14,12},{16,18},{18,... | collective-permute-start | bytes 7520264 | tf_op jit(solution)/shard_map/ppermute | solution.py:1109
  231.5 36.7 %collective-permute-start.10 = (bf16[1088,1152]{1,0:T(8,128)(2,1)}, bf16[1088,1152]{1,0:T(8,128)(2,1)S(1)}, u32[]{:S(2)}, u32[]{:S(2)}) collective-permute-start(bf16[1088,1152]{1,0:T(8,128)(2,1)} %get-tuple-element.252), channel_id=1, source_target_pairs={{0,2},{2,0},{4,6},{6,4},{8,10},{10,8},{12,14},{14,12},{16,18},{18,... | collective-permute-start | bytes 7520264 | tf_op jit(solution)/shard_map/ppermute | solution.py:1109
  276.4 38.5 %collective-permute-start.11 = (bf16[720,1152]{1,0:T(8,128)(2,1)}, bf16[720,1152]{1,0:T(8,128)(2,1)}, u32[]{:S(2)}, u32[]{:S(2)}) collective-permute-start(bf16[720,1152]{1,0:T(8,128)(2,1)} %add_convert_fusion.4), channel_id=1, source_target_pairs={{0,1},{1,0},{2,3},{3,2},{4,5},{5,4},{6,7},{7,6},{8,9},{9,8},{10,11... | collective-permute-start | bytes 4976648 | tf_op jit(solution)/shard_map/ppermute | solution.py:1105
  314.3 40.3 %collective-permute-start.12 = (bf16[1088,1152]{1,0:T(8,128)(2,1)}, bf16[1088,1152]{1,0:T(8,128)(2,1)S(1)}, u32[]{:S(2)}, u32[]{:S(2)}) collective-permute-start(bf16[1088,1152]{1,0:T(8,128)(2,1)} %get-tuple-element.263), channel_id=1, source_target_pairs={{0,2},{2,0},{4,6},{6,4},{8,10},{10,8},{12,14},{14,12},{16,18},{18,... | collective-permute-start | bytes 7520264 | tf_op jit(solution)/shard_map/ppermute | solution.py:1109
  314.3 44.9 %collective-permute-start.15 = (bf16[1088,1152]{1,0:T(8,128)(2,1)}, bf16[1088,1152]{1,0:T(8,128)(2,1)S(1)}, u32[]{:S(2)}, u32[]{:S(2)}) collective-permute-start(bf16[1088,1152]{1,0:T(8,128)(2,1)} %get-tuple-element.270), channel_id=1, source_target_pairs={{0,2},{2,0},{4,6},{6,4},{8,10},{10,8},{12,14},{14,12},{16,18},{18,... | collective-permute-start | bytes 7520264 | tf_op jit(solution)/shard_map/ppermute | solution.py:1109
  314.9 38.2 %collective-permute-start.14 = (bf16[352,1152]{1,0:T(8,128)(2,1)}, bf16[352,1152]{1,0:T(8,128)(2,1)}, u32[]{:S(2)}, u32[]{:S(2)}) collective-permute-start(bf16[352,1152]{1,0:T(8,128)(2,1)} %add_convert_fusion.8), channel_id=1, source_target_pairs={{0,1},{1,0},{2,3},{3,2},{4,5},{5,4},{6,7},{7,6},{8,9},{9,8},{10,11... | collective-permute-start | bytes 2433032 | tf_op jit(solution)/shard_map/ppermute | solution.py:1105
  316.4 36.8 %collective-permute-start.13 = (bf16[368,1152]{1,0:T(8,128)(2,1)}, bf16[368,1152]{1,0:T(8,128)(2,1)S(1)}, u32[]{:S(2)}, u32[]{:S(2)}) collective-permute-start(bf16[368,1152]{1,0:T(8,128)(2,1)} %add_convert_fusion.6), channel_id=1, source_target_pairs={{0,1},{1,0},{2,3},{3,2},{4,5},{5,4},{6,7},{7,6},{8,9},{9,8},{10,11... | collective-permute-start | bytes 2543624 | tf_op jit(solution)/shard_map/ppermute | solution.py:1105
  353.3 52.4 %collective-permute-start.16 = (bf16[736,1152]{1,0:T(8,128)(2,1)}, bf16[736,1152]{1,0:T(8,128)(2,1)}, u32[]{:S(2)}, u32[]{:S(2)}) collective-permute-start(bf16[736,1152]{1,0:T(8,128)(2,1)} %add_convert_fusion.3), channel_id=1, source_target_pairs={{0,1},{1,0},{2,3},{3,2},{4,5},{5,4},{6,7},{7,6},{8,9},{9,8},{10,11... | collective-permute-start | bytes 5087240 | tf_op jit(solution)/shard_map/ppermute | solution.py:1105
  359.2 365.9 %all-reduce.9.cloned.1.call-start = ((), (), s32[]{:S(2)}) async-start(), calls=%async_computation.3 | async-start | bytes 5308416 | tf_op jit(solution)/shard_map/psum | solution.py:1413
  359.3 46.4 %copy-start.2 = (bf16[1088,1152]{1,0:T(8,128)(2,1)S(1)}, bf16[1088,1152]{1,0:T(8,128)(2,1)}, u32[]{:S(2)}) copy-start(bf16[1088,1152]{1,0:T(8,128)(2,1)} %get-tuple-element.278) | copy-start | bytes 7520260
  430.0 39.6 %collective-permute-start.18 = (bf16[288,1152]{1,0:T(8,128)(2,1)}, bf16[288,1152]{1,0:T(8,128)(2,1)S(1)}, u32[]{:S(2)}, u32[]{:S(2)}) collective-permute-start(bf16[288,1152]{1,0:T(8,128)(2,1)} %get-tuple-element.289), channel_id=1, source_target_pairs={{0,2},{2,0},{4,6},{6,4},{8,10},{10,8},{12,14},{14,12},{16,18},{18,... | collective-permute-start | bytes 1990664 | tf_op jit(solution)/shard_map/ppermute | solution.py:1109
  430.0 41.7 %collective-permute-start.19 = (bf16[288,1152]{1,0:T(8,128)(2,1)}, bf16[288,1152]{1,0:T(8,128)(2,1)S(1)}, u32[]{:S(2)}, u32[]{:S(2)}) collective-permute-start(bf16[288,1152]{1,0:T(8,128)(2,1)} %get-tuple-element.291), channel_id=1, source_target_pairs={{0,2},{2,0},{4,6},{6,4},{8,10},{10,8},{12,14},{14,12},{16,18},{18,... | collective-permute-start | bytes 1990664 | tf_op jit(solution)/shard_map/ppermute | solution.py:1109
  430.5 43.4 %collective-permute-start.17 = (bf16[544,1152]{1,0:T(8,128)(2,1)S(1)}, bf16[544,1152]{1,0:T(8,128)(2,1)S(1)}, u32[]{:S(2)}, u32[]{:S(2)}) collective-permute-start(bf16[544,1152]{1,0:T(8,128)(2,1)S(1)} %get-tuple-element.286), channel_id=1, source_target_pairs={{0,4},{2,6},{4,0},{6,2},{8,12},{10,14},{12,8},{14,10},{16,20},{18,... | collective-permute-start | bytes 3760136 | tf_op jit(solution)/shard_map/ppermute | solution.py:1141
  432.0 38.4 %copy-start.14 = (bf16[288,1152]{1,0:T(8,128)(2,1)S(1)}, bf16[288,1152]{1,0:T(8,128)(2,1)}, u32[]{:S(2)}) copy-start(bf16[288,1152]{1,0:T(8,128)(2,1)} %get-tuple-element.288) | copy-start | bytes 1990660
  475.2 21.3 %collective-permute-start.20 = (bf16[288,1152]{1,0:T(8,128)(2,1)S(1)}, bf16[288,1152]{1,0:T(8,128)(2,1)}, u32[]{:S(2)}, u32[]{:S(2)}) collective-permute-start(bf16[288,1152]{1,0:T(8,128)(2,1)S(1)} %add_convert_fusion.10), channel_id=1, source_target_pairs={{0,1},{1,0},{2,3},{3,2},{4,5},{5,4},{6,7},{7,6},{8,9},{9,8},{10,11... | collective-permute-start | bytes 1990664 | tf_op jit(solution)/shard_map/ppermute | solution.py:1105
  475.8 20.7 %collective-permute-start.21 = (bf16[272,1152]{1,0:T(8,128)(2,1)}, bf16[272,1152]{1,0:T(8,128)(2,1)S(1)}, u32[]{:S(2)}, u32[]{:S(2)}) collective-permute-start(bf16[272,1152]{1,0:T(8,128)(2,1)} %get-tuple-element.299), channel_id=1, source_target_pairs={{0,8},{2,10},{4,12},{6,14},{8,0},{10,2},{12,4},{14,6},{16,24},{18,... | collective-permute-start | bytes 1880072 | tf_op jit(solution)/shard_map/ppermute | solution.py:1141
  496.5 19.7 %collective-permute-start.24 = (bf16[864,1152]{1,0:T(8,128)(2,1)}, bf16[864,1152]{1,0:T(8,128)(2,1)}, u32[]{:S(2)}, u32[]{:S(2)}) collective-permute-start(bf16[864,1152]{1,0:T(8,128)(2,1)} %get-tuple-element.310), channel_id=1, source_target_pairs={{0,2},{2,0},{4,6},{6,4},{8,10},{10,8},{12,14},{14,12},{16,18},{18,... | collective-permute-start | bytes 5971976 | tf_op jit(solution)/shard_map/ppermute | solution.py:1109
  496.5 24.3 %collective-permute-start.23 = (bf16[1088,1152]{1,0:T(8,128)(2,1)}, bf16[1088,1152]{1,0:T(8,128)(2,1)}, u32[]{:S(2)}, u32[]{:S(2)}) collective-permute-start(bf16[1088,1152]{1,0:T(8,128)(2,1)} %all-reduce.7.cloned.1.call-done.mine_ref), channel_id=1, source_target_pairs={{0,2},{2,0},{4,6},{6,4},{8,10},{10,8},{12,14},{14,12},{16,18},{18,... | collective-permute-start | bytes 7520264 | tf_op jit(solution)/shard_map/ppermute | solution.py:1109
  498.5 17.7 %copy-start.5 = (bf16[864,1152]{1,0:T(8,128)(2,1)S(1)}, bf16[864,1152]{1,0:T(8,128)(2,1)}, u32[]{:S(2)}) copy-start(bf16[864,1152]{1,0:T(8,128)(2,1)} %get-tuple-element.309) | copy-start | bytes 5971972
  498.6 17.5 %collective-permute-start.22 = (bf16[136,1152]{1,0:T(8,128)(2,1)S(1)}, bf16[136,1152]{1,0:T(8,128)(2,1)S(1)}, u32[]{:S(2)}, u32[]{:S(2)}) collective-permute-start(bf16[136,1152]{1,0:T(8,128)(2,1)S(1)} %get-tuple-element.304), channel_id=1, source_target_pairs={{0,16},{2,18},{4,20},{6,22},{8,24},{10,26},{12,28},{14,30},{16,0},... | collective-permute-start | bytes 940040 | tf_op jit(solution)/shard_map/ppermute | solution.py:1141
  520.8 17.7 %collective-permute-start.25 = (bf16[256,1152]{1,0:T(8,128)(2,1)S(1)}, bf16[256,1152]{1,0:T(8,128)(2,1)}, u32[]{:S(2)}, u32[]{:S(2)}) collective-permute-start(bf16[256,1152]{1,0:T(8,128)(2,1)S(1)} %get-tuple-element.312), channel_id=1, source_target_pairs={{0,1},{1,0},{2,3},{3,2},{4,5},{5,4},{6,7},{7,6},{8,9},{9,8},{10,11... | collective-permute-start | bytes 1769480 | tf_op jit(solution)/shard_map/ppermute | solution.py:1105
  522.2 16.3 %collective-permute-start.26 = (bf16[136,1152]{1,0:T(8,128)(2,1)S(1)}, bf16[136,1152]{1,0:T(8,128)(2,1)S(1)}, u32[]{:S(2)}, u32[]{:S(2)}) collective-permute-start(bf16[136,1152]{1,0:T(8,128)(2,1)S(1)} %add_convert_fusion.14), channel_id=1, source_target_pairs={{0,16},{2,18},{4,20},{6,22},{8,24},{10,26},{12,28},{14,30},{16,0},... | collective-permute-start | bytes 940040 | tf_op jit(solution)/shard_map/ppermute | solution.py:1141
  538.6 19.6 %collective-permute-start.28 = (bf16[272,1152]{1,0:T(8,128)(2,1)S(1)}, bf16[272,1152]{1,0:T(8,128)(2,1)S(1)}, u32[]{:S(2)}, u32[]{:S(2)}) collective-permute-start(bf16[272,1152]{1,0:T(8,128)(2,1)S(1)} %pad_maximum_fusion.3), channel_id=1, source_target_pairs={{0,8},{2,10},{4,12},{6,14},{8,0},{10,2},{12,4},{14,6},{16,24},{18,... | collective-permute-start | bytes 1880072 | tf_op jit(solution)/shard_map/ppermute | solution.py:1141
  539.5 18.8 %collective-permute-start.27 = (bf16[256,1152]{1,0:T(8,128)(2,1)}, bf16[256,1152]{1,0:T(8,128)(2,1)}, u32[]{:S(2)}, u32[]{:S(2)}) collective-permute-start(bf16[256,1152]{1,0:T(8,128)(2,1)} %get-tuple-element.319), channel_id=1, source_target_pairs={{0,1},{1,0},{2,3},{3,2},{4,5},{5,4},{6,7},{7,6},{8,9},{9,8},{10,11... | collective-permute-start | bytes 1769480 | tf_op jit(solution)/shard_map/ppermute | solution.py:1105
  558.6 22.7 %collective-permute-start.29 = (bf16[352,1152]{1,0:T(8,128)(2,1)}, bf16[352,1152]{1,0:T(8,128)(2,1)}, u32[]{:S(2)}, u32[]{:S(2)}) collective-permute-start(bf16[352,1152]{1,0:T(8,128)(2,1)} %add_convert_fusion.7), channel_id=1, source_target_pairs={{0,1},{1,0},{2,3},{3,2},{4,5},{5,4},{6,7},{7,6},{8,9},{9,8},{10,11... | collective-permute-start | bytes 2433032 | tf_op jit(solution)/shard_map/ppermute | solution.py:1105
  580.7 58.4 %collective-permute-start.32 = (bf16[544,1152]{1,0:T(8,128)(2,1)S(1)}, bf16[544,1152]{1,0:T(8,128)(2,1)S(1)}, u32[]{:S(2)}, u32[]{:S(2)}) collective-permute-start(bf16[544,1152]{1,0:T(8,128)(2,1)S(1)} %pad_maximum_fusion.2), channel_id=1, source_target_pairs={{0,4},{2,6},{4,0},{6,2},{8,12},{10,14},{12,8},{14,10},{16,20},{18,... | collective-permute-start | bytes 3760136 | tf_op jit(solution)/shard_map/ppermute | solution.py:1141
  581.2 19.5 %collective-permute-start.30 = (bf16[864,1152]{1,0:T(8,128)(2,1)}, bf16[864,1152]{1,0:T(8,128)(2,1)}, u32[]{:S(2)}, u32[]{:S(2)}) collective-permute-start(bf16[864,1152]{1,0:T(8,128)(2,1)} %get-tuple-element.340), channel_id=1, source_target_pairs={{0,2},{2,0},{4,6},{6,4},{8,10},{10,8},{12,14},{14,12},{16,18},{18,... | collective-permute-start | bytes 5971976 | tf_op jit(solution)/shard_map/ppermute | solution.py:1109
  581.2 19.5 %copy-start.6 = (bf16[864,1152]{1,0:T(8,128)(2,1)S(1)}, bf16[864,1152]{1,0:T(8,128)(2,1)}, u32[]{:S(2)}) copy-start(bf16[864,1152]{1,0:T(8,128)(2,1)} %get-tuple-element.339) | copy-start | bytes 5971972
  605.3 30.9 %copy-start.34 = (f32[1,1152]{1,0:T(1,128)S(1)}, f32[1,1152]{1,0:T(1,128)}, u32[]{:S(2)}) copy-start(f32[1,1152]{1,0:T(1,128)} %get-tuple-element.363) | copy-start | bytes 13828
  605.3 31.6 %copy-start.33 = (f32[1,1152]{1,0:T(1,128)S(1)}, f32[1,1152]{1,0:T(1,128)}, u32[]{:S(2)}) copy-start(f32[1,1152]{1,0:T(1,128)} %get-tuple-element.361) | copy-start | bytes 13828
  605.3 33.8 %collective-permute-start.31 = (bf16[1,576,729]{2,1,0:T(8,128)(2,1)}, bf16[1,576,729]{2,1,0:T(8,128)(2,1)S(1)}, u32[]{:S(2)}, u32[]{:S(2)}) collective-permute-start(bf16[1,576,729]{2,1,0:T(8,128)(2,1)} %get-tuple-element.351), channel_id=1, source_target_pairs={{0,1},{1,0},{2,3},{3,2},{4,5},{5,4},{6,7},{7,6},{8,9},{9,8},{10,11... | collective-permute-start | bytes 2519432 | tf_op jit(solution)/shard_map/ppermute | solution.py:1105
  637.6 39.5 %collective-permute-start.34 = (f32[13520]{0:T(1024)S(1)}, f32[13520]{0:T(1024)S(1)}, u32[]{:S(2)}, u32[]{:S(2)}) collective-permute-start(f32[13520]{0:T(1024)S(1)} %pad_maximum_fusion.4), channel_id=1, source_target_pairs={{0,1},{1,0},{2,3},{3,2},{4,5},{5,4},{6,7},{7,6},{8,9},{9,8},{10,11... | collective-permute-start | bytes 162248 | tf_op jit(solution)/shard_map/ppermute | solution.py:1105
  640.2 36.8 %copy-start = (bf16[1088,1152]{1,0:T(8,128)(2,1)}, bf16[1088,1152]{1,0:T(8,128)(2,1)S(1)}, u32[]{:S(2)}) copy-start(bf16[1088,1152]{1,0:T(8,128)(2,1)S(1)} %pad_maximum_fusion.1.mine_ref) | copy-start | bytes 7520260
  640.2 40.8 %collective-permute-start.33 = (bf16[2,576,729]{2,1,0:T(8,128)(2,1)}, bf16[2,576,729]{2,1,0:T(8,128)(2,1)}, u32[]{:S(2)}, u32[]{:S(2)}) collective-permute-start(bf16[2,576,729]{2,1,0:T(8,128)(2,1)} %get-tuple-element.354), channel_id=1, source_target_pairs={{0,1},{1,0},{2,3},{3,2},{4,5},{5,4},{6,7},{7,6},{8,9},{9,8},{10,11... | collective-permute-start | bytes 5038856 | tf_op jit(solution)/shard_map/ppermute | solution.py:1105
  640.9 40.2 %collective-permute-start.35 = (bf16[1088,1152]{1,0:T(8,128)(2,1)S(1)}, bf16[1088,1152]{1,0:T(8,128)(2,1)S(1)}, u32[]{:S(2)}, u32[]{:S(2)}) collective-permute-start(bf16[1088,1152]{1,0:T(8,128)(2,1)S(1)} %pad_maximum_fusion.1.mine_ref), channel_id=1, source_target_pairs={{0,2},{2,0},{4,6},{6,4},{8,10},{10,8},{12,14},{14,12},{16,18},{18,... | collective-permute-start | bytes 7520264 | tf_op jit(solution)/shard_map/ppermute | solution.py:1109
  681.0 9.8 %copy-start.3 = (bf16[1088,1152]{1,0:T(8,128)(2,1)}, bf16[1088,1152]{1,0:T(8,128)(2,1)S(1)}, u32[]{:S(2)}) copy-start(bf16[1088,1152]{1,0:T(8,128)(2,1)S(1)} %collective-permute-done.35.other_ref) | copy-start | bytes 7520260
  681.0 9.8 %copy-start.12 = (bf16[1,576,729]{2,1,0:T(8,128)(2,1)S(1)}, bf16[1,576,729]{2,1,0:T(8,128)(2,1)}, u32[]{:S(2)}) copy-start(bf16[1,576,729]{2,1,0:T(8,128)(2,1)} %copy-done.11) | copy-start | bytes 2519428
  681.0 44.1 %collective-permute-start.42 = (bf16[2,576,729]{2,1,0:T(8,128)(2,1)}, bf16[2,576,729]{2,1,0:T(8,128)(2,1)}, u32[]{:S(2)}, u32[]{:S(2)}) collective-permute-start(bf16[2,576,729]{2,1,0:T(8,128)(2,1)} %get-tuple-element.378), channel_id=1, source_target_pairs={{0,1},{1,0},{2,3},{3,2},{4,5},{5,4},{6,7},{7,6},{8,9},{9,8},{10,11... | collective-permute-start | bytes 5038856 | tf_op jit(solution)/shard_map/ppermute | solution.py:1105
  694.1 10.7 %collective-permute-start.38 = (f32[13520]{0:T(1024)S(1)}, f32[13520]{0:T(1024)S(1)}, u32[]{:S(2)}, u32[]{:S(2)}) collective-permute-start(f32[13520]{0:T(1024)S(1)} %fusion.4), channel_id=1, source_target_pairs={{0,6},{2,4},{4,2},{6,0},{8,14},{10,12},{12,10},{14,8},{16,22},{18,... | collective-permute-start | bytes 162248 | tf_op jit(solution)/shard_map/ppermute | solution.py:1116
  694.2 10.6 %collective-permute-start.37 = (f32[13520]{0:T(1024)S(1)}, f32[13520]{0:T(1024)S(1)}, u32[]{:S(2)}, u32[]{:S(2)}) collective-permute-start(f32[13520]{0:T(1024)S(1)} %fusion.4), channel_id=1, source_target_pairs={{0,4},{2,6},{4,0},{6,2},{8,12},{10,14},{12,8},{14,10},{16,20},{18,... | collective-permute-start | bytes 162248 | tf_op jit(solution)/shard_map/ppermute | solution.py:1116
  695.8 9.1 %collective-permute-start.36 = (f32[13520]{0:T(1024)S(1)}, f32[13520]{0:T(1024)S(1)}, u32[]{:S(2)}, u32[]{:S(2)}) collective-permute-start(f32[13520]{0:T(1024)S(1)} %fusion.4), channel_id=1, source_target_pairs={{0,2},{2,0},{4,6},{6,4},{8,10},{10,8},{12,14},{14,12},{16,18},{18,... | collective-permute-start | bytes 162248 | tf_op jit(solution)/shard_map/ppermute | solution.py:1116
  704.9 7.8 %collective-permute-start.41 = (f32[13520]{0:T(1024)S(1)}, f32[13520]{0:T(1024)S(1)}, u32[]{:S(2)}, u32[]{:S(2)}) collective-permute-start(f32[13520]{0:T(1024)S(1)} %add_add_fusion.1), channel_id=1, source_target_pairs={{0,24},{2,26},{4,28},{6,30},{8,16},{10,18},{12,20},{14,22},{16,8},... | collective-permute-start | bytes 162248 | tf_op jit(solution)/shard_map/ppermute | solution.py:1116
  706.7 13.2 %collective-permute-start.40 = (f32[13520]{0:T(1024)S(1)}, f32[13520]{0:T(1024)S(1)}, u32[]{:S(2)}, u32[]{:S(2)}) collective-permute-start(f32[13520]{0:T(1024)S(1)} %add_add_fusion.1), channel_id=1, source_target_pairs={{0,16},{2,18},{4,20},{6,22},{8,24},{10,26},{12,28},{14,30},{16,0},... | collective-permute-start | bytes 162248 | tf_op jit(solution)/shard_map/ppermute | solution.py:1116
  707.6 12.3 %collective-permute-start.39 = (f32[13520]{0:T(1024)S(1)}, f32[13520]{0:T(1024)S(1)}, u32[]{:S(2)}, u32[]{:S(2)}) collective-permute-start(f32[13520]{0:T(1024)S(1)} %add_add_fusion.1), channel_id=1, source_target_pairs={{0,8},{2,10},{4,12},{6,14},{8,0},{10,2},{12,4},{14,6},{16,24},{18,... | collective-permute-start | bytes 162248 | tf_op jit(solution)/shard_map/ppermute | solution.py:1116
  725.1 10.1 %collective-permute-start.43 = (bf16[1152,1152]{1,0:T(8,128)(2,1)}, bf16[1152,1152]{1,0:T(8,128)(2,1)S(1)}, u32[]{:S(2)}, u32[]{:S(2)}) collective-permute-start(bf16[1152,1152]{1,0:T(8,128)(2,1)} %all-reduce.9.cloned.1.call-done.mine_ref), channel_id=1, source_target_pairs={{0,2},{2,0},{4,6},{6,4},{8,10},{10,8},{12,14},{14,12},{16,18},{18,... | collective-permute-start | bytes 7962632 | tf_op jit(solution)/shard_map/ppermute | solution.py:1109
  725.1 25.7 %collective-permute-start.44 = (bf16[1,576,729]{2,1,0:T(8,128)(2,1)}, bf16[1,576,729]{2,1,0:T(8,128)(2,1)S(1)}, u32[]{:S(2)}, u32[]{:S(2)}) collective-permute-start(bf16[1,576,729]{2,1,0:T(8,128)(2,1)} %get-tuple-element.383), channel_id=1, source_target_pairs={{0,1},{1,0},{2,3},{3,2},{4,5},{5,4},{6,7},{7,6},{8,9},{9,8},{10,11... | collective-permute-start | bytes 2519432 | tf_op jit(solution)/shard_map/ppermute | solution.py:1105
  (21 other events, 52.0 us)
Sparse Core Ops, SparseCore 0:
  40.7 57.8 all-gather.2
  101.3 83.7 all-gather.4
  359.3 117.9 all-reduce.6
  605.4 119.6 all-reduce.8
